TPU v7x, 128 devices: a whole 4x4x4 slice. The times are simulated.
128 devices in a mesh: dp: 8 (over y, core), row: 4 (over z), col: 4 (over x).
Axes of the slice: x: 4, y: 4, z: 4, core: 2. Of those that a mesh axis runs over, the one named last changes fastest.
Arguments:
- inputs: bfloat16 [8, 256, 128, 512], P('dp', None, 'row', 'col'), may hold values from -6 to 6
- reduce_weight: bfloat16 [64, 256], replicated, may hold values from -0.375 to 0.375
- spatial_weight: bfloat16 [3, 3, 64, 64], replicated, may hold values from -0.25 to 0.25
- expand_weight: bfloat16 [256, 64], replicated, may hold values from -0.75 to 0.75
- class_weight: bfloat16 [3, 3, 135, 256], replicated, may hold values from -0.125 to 0.125
- anchor_labels: int32 [8, 9, 128, 512], P('dp', None, 'row', 'col'), may hold values from 0 to 15, as said below
- anchor_mask: int32 [8, 9, 128, 512], P('dp', None, 'row', 'col'), may hold values from 0 to 1, as said below
Outputs:
- loss: float32 [], replicated
- grad_reduce: float32 [64, 256], replicated
- grad_spatial: float32 [3, 3, 64, 64], replicated
- grad_expand: float32 [256, 64], replicated
- grad_class: float32 [3, 3, 135, 256], replicated
Inputs may be any that keep to these rules, and one draw needn't show every extreme that they name: `anchor_labels`: labels are 0 to 15; anchor 0 at the first row and column of every tile is positive. `anchor_mask`: every anchor with a label above 0 has mask 1.
All inputs are finite; a program needn't handle non-finite values.
Results may differ from a plain program's by a relative error of at most 0.0034.
Values may be sent and summed in bfloat16 or wider, within the bound.
No kernel may reach another device: no remote copies, remote signals or barrier semaphores. Data moves between devices by JAX's collectives and lax.ppermute only.
A program may use at most 128 MiB of HBM per device.

v0:
```python
import jax
import jax.numpy as jnp
import numpy as np
from jax import lax
from jax.experimental import pallas as pl
from jax.experimental.pallas import tpu as pltpu
from jax.sharding import PartitionSpec as P

A = 9
K = 15
OUT = A * K
C = 256
MID = 64
HALO = 4
ROWS = 32
COLS = 128
FULL = ROWS + 2 * HALO
STRIDE = COLS + 2 * HALO
CHANNELS = 288
MARGIN = 256
WIDTH = 6400
CHUNK = 512
LABEL0 = C
MASK0 = C + A
ONE0 = C + 2 * A
TAIL = 8
STACK = 9 * 128 + 9 * TAIL + 8
ALL = ("dp", "row", "col")
TAPS = [(dy - 1) * STRIDE + (dx - 1) for dy in range(3) for dx in range(3)]
BF = jnp.bfloat16
F32 = jnp.float32


def row_of(top_ref, main_ref, bottom_ref, r):
    if r < HALO:
        return top_ref[r]
    if r < HALO + ROWS:
        return main_ref[r - HALO]
    return bottom_ref[r - HALO - ROWS]


def lanes_between(lo, hi):
    lane = lax.broadcasted_iota(jnp.int32, (CHANNELS, 128), 1)
    return (lane >= lo) & (lane < hi)


def put(ref, tile, value, lo, hi):
    where = slice(tile * 128, tile * 128 + 128)
    ref[:, where] = jnp.where(lanes_between(lo, hi), value, ref[:, where])


def pack_kernel(main_ref, top_ref, bottom_ref, left_ref, right_ref):
    left_ref[...] = jnp.zeros_like(left_ref)
    right_ref[...] = jnp.zeros_like(right_ref)
    for r in range(FULL):
        row = row_of(top_ref, main_ref, bottom_ref, r)
        at = (4 * r) % 128
        put(left_ref, 4 * r // 128, pltpu.roll(row, at, 1), at, at + 4)
        put(right_ref, 4 * r // 128, pltpu.roll(row, (at + 4) % 128, 1), at, at + 4)


def window(ref, rows, lane, shift):
    base = (shift // 128) * 128
    turn = shift - base
    if turn == 0:
        return ref[rows, pl.ds(pl.multiple_of(lane + base, 128), CHUNK)]
    wide = ref[rows, pl.ds(pl.multiple_of(lane + base, 128), CHUNK + 128)]
    return pltpu.roll(wide, CHUNK + 128 - turn, 1)[:, :CHUNK]


def interior(lane, shift):
    p = lane - MARGIN + shift + lax.broadcasted_iota(jnp.int32, (1, CHUNK), 1)
    r = (p * 30841) >> 22
    c = p - r * STRIDE
    return (r >= HALO) & (r < HALO + ROWS) & (c >= HALO) & (c < HALO + COLS)


def dot(a, b):
    return jnp.dot(a, b, preferred_element_type=F32)


def dot_nt(a, b):
    return lax.dot_general(a, b, (((1,), (1,)), ((), ())), preferred_element_type=F32)


def chunks(start, count, body):
    def step(j, carry):
        body(pl.multiple_of(MARGIN + start + j * CHUNK, 128))
        return carry

    lax.fori_loop(0, count, step, 0)


def main_kernel(
    main_ref, top_ref, bottom_ref, left_ref, right_ref,
    wr_ref, w2_ref, w2t_ref, we_ref, wet_ref, w3_ref, w3t_ref, e_ref,
    gclass_ref, gred_ref, gspat_ref, gexp_ref, stat_ref,
    x_ref, first_ref, second_ref, block_ref, d_ref, dt_ref, ds_ref, facc_ref, cacc_ref,
):
    for ref in (x_ref, first_ref, second_ref, block_ref, d_ref, dt_ref, ds_ref):
        ref[...] = jnp.zeros_like(ref)
    for ref in (gclass_ref, gred_ref, gspat_ref, gexp_ref, facc_ref, cacc_ref):
        ref[...] = jnp.zeros_like(ref)
    for r in range(FULL):
        row = row_of(top_ref, main_ref, bottom_ref, r)
        at = MARGIN + r * STRIDE + HALO
        turn, tile = (at % 128, at // 128)
        turned = pltpu.roll(row, turn, 1)
        put(x_ref, tile, turned, turn, 128)
        put(x_ref, tile + 1, turned, 0, turn)
        source = slice(4 * r // 128 * 128, 4 * r // 128 * 128 + 128)
        at = MARGIN + r * STRIDE
        put(x_ref, at // 128, pltpu.roll(left_ref[:, source], (4 * r) % 128, 1), at % 128, at % 128 + 4)
        at = at + HALO + COLS
        put(x_ref, at // 128, pltpu.roll(right_ref[:, source], (4 * r + 4) % 128, 1), at % 128, at % 128 + 4)

    def first_step(lane):
        x = x_ref[:C, pl.ds(lane, CHUNK)]
        first_ref[:, pl.ds(lane, CHUNK)] = jnp.maximum(dot(wr_ref[...], x), 0.0).astype(BF)

    chunks(0, 11, first_step)

    def block_step(lane):
        here = pl.ds(lane, CHUNK)
        stack = jnp.concatenate([window(first_ref, slice(None), lane, s) for s in TAPS], axis=0)
        second = jnp.maximum(dot(w2_ref[...], stack), 0.0)
        inside = x_ref[ONE0 - 2 : ONE0 + 14, here].astype(F32)[2:3]
        second = jnp.where(inside > 0.5, second, 0.0).astype(BF)
        second_ref[:, here] = second
        total = x_ref[:C, here].astype(F32) + dot(we_ref[...], second)
        block_ref[:, here] = jnp.maximum(total, 0.0).astype(BF)

    chunks(128, 11, block_step)

    channel = lax.broadcasted_iota(jnp.int32, (136, 1), 0)
    wanted = (channel - 15 * ((channel * 4370) >> 16) + 17).astype(F32)

    def logit_step(lane):
        here = pl.ds(lane, CHUNK)
        stack = jnp.concatenate([window(block_ref, slice(None), lane, s) for s in TAPS], axis=0)
        z = dot(w3_ref[...], stack)
        tags = x_ref[C:CHANNELS, here]
        code = dot(e_ref[...], tags)
        target = code == wanted
        counted = code > 15.5
        u = jnp.where(target, z, -z)
        alpha = jnp.where(target, 0.25, 0.75)
        e = jnp.exp(-jnp.abs(u))
        d = 1.0 / (1.0 + e)
        ed = e * d
        positive = u >= 0
        p = jnp.where(positive, ed, d)
        q = jnp.where(positive, d, ed)
        ls = jnp.minimum(u, 0.0) - jnp.log1p(e)
        ap2 = jnp.where(counted, alpha, 0.0) * p * p
        grad = ap2 * (2.0 * q * ls - p)
        grad = jnp.where(target, grad, -grad)
        d_ref[:, here] = grad[:128].astype(BF)
        dt_ref[:, here] = grad[128:].astype(BF).astype(F32)
        inner = interior(lane, 0)
        focal = jnp.where(inner, ap2 * ls, 0.0)
        facc_ref[...] -= jnp.sum(focal.reshape(17, 8, CHUNK), axis=0)
        labels = tags[:16].astype(F32)
        tag = lax.broadcasted_iota(jnp.int32, (16, CHUNK), 0)
        positives = jnp.where((labels > 0.5) & (tag < A) & inner, 1.0, 0.0)
        cacc_ref[...] += positives[:8] + positives[8:]

    chunks(256, 10, logit_step)

    def class_step(lane):
        here = pl.ds(lane, CHUNK)
        mains = [window(d_ref, slice(None), lane, -s) for s in TAPS]
        tails = [window(dt_ref, slice(None), lane, -s) for s in TAPS]
        inner = [interior(lane, -s) for s in TAPS]
        spare = jnp.zeros((8, CHUNK), F32)
        block = block_ref[:, here]
        stack = jnp.concatenate(
            mains + [jnp.concatenate(tails + [spare], axis=0).astype(BF)], axis=0
        )
        dblock = dot(w3t_ref[...], stack)
        dsum = jnp.where(block.astype(F32) > 0, dblock, 0.0).astype(BF)
        second = second_ref[:, here]
        within = interior(lane, 0)
        second32 = second.astype(F32)
        gexp_ref[...] += dot_nt(dsum, jnp.where(within, second32, 0.0).astype(BF))
        ds_ref[:, here] = jnp.where(second32 > 0, dot(wet_ref[...], dsum), 0.0).astype(BF)
        own = jnp.concatenate(
            [m * jnp.where(i, 1.0, 0.0).astype(BF) for m, i in zip(mains, inner)]
            + [
                jnp.concatenate(
                    [jnp.where(i, t, 0.0) for t, i in zip(tails, inner)] + [spare], axis=0
                ).astype(BF)
            ],
            axis=0,
        )
        gclass_ref[...] += dot_nt(own, block)

    chunks(384, 10, class_step)

    def first_back(lane):
        here = pl.ds(lane, CHUNK)
        parts = [window(ds_ref, slice(None), lane, -s) for s in TAPS]
        inner = [interior(lane, -s) for s in TAPS]
        first = first_ref[:, here]
        own = jnp.concatenate(
            [m * jnp.where(i, 1.0, 0.0).astype(BF) for m, i in zip(parts, inner)], axis=0
        )
        gspat_ref[...] += dot_nt(own, first)
        dfirst = dot(w2t_ref[...], jnp.concatenate(parts, axis=0))
        keep = (first.astype(F32) > 0) & interior(lane, 0)
        dfirst = jnp.where(keep, dfirst, 0.0).astype(BF)
        gred_ref[...] += dot_nt(dfirst, x_ref[:C, here])

    chunks(384, 10, first_back)

    focal = jnp.sum(facc_ref[...])
    count = jnp.sum(cacc_ref[...])
    lane = lax.broadcasted_iota(jnp.int32, (8, 128), 1)
    stat_ref[...] = jnp.where(lane == 0, focal, jnp.where(lane == 1, count, 0.0))


def split3(x):
    hi = lax.reduce_precision(x, 8, 7)
    mid = lax.reduce_precision(x - hi, 8, 7)
    return [hi, mid, x - hi - mid]


def per_device(
    inputs, reduce_weight, spatial_weight, expand_weight, class_weight, anchor_labels, anchor_mask
):
    one = jnp.ones((1, ROWS, COLS), BF)
    none = jnp.zeros((CHANNELS - C - 2 * A - 1, ROWS, COLS), BF)
    fields = jnp.concatenate(
        [inputs[0], anchor_labels[0].astype(BF), anchor_mask[0].astype(BF), one, none], axis=0
    )
    fields = jnp.transpose(fields, (1, 0, 2))
    ahead = [(i, i + 1) for i in range(3)]
    back = [(i + 1, i) for i in range(3)]
    top = lax.ppermute(fields[ROWS - HALO :], "row", ahead)
    bottom = lax.ppermute(fields[:HALO], "row", back)
    pack = jax.ShapeDtypeStruct((CHANNELS, 256), BF)
    left_edge, right_edge = pl.pallas_call(
        pack_kernel,
        out_shape=(pack, pack),
        compiler_params=pltpu.CompilerParams(vmem_limit_bytes=56 << 20),
    )(fields, top, bottom)
    left = lax.ppermute(right_edge, "col", ahead)
    right = lax.ppermute(left_edge, "col", back)

    w2 = jnp.transpose(spatial_weight, (2, 0, 1, 3)).reshape(MID, 9 * MID)
    w2t = jnp.transpose(spatial_weight, (3, 0, 1, 2)).reshape(MID, 9 * MID)
    w3 = jnp.transpose(class_weight, (2, 0, 1, 3)).reshape(OUT, 9 * C)
    w3 = jnp.pad(w3, ((0, 136 - OUT), (0, 0)))
    w9 = class_weight.reshape(9, OUT, C)
    w3t = jnp.concatenate(
        [
            w9[:, :128].reshape(9 * 128, C),
            jnp.pad(w9[:, 128:], ((0, 0), (0, TAIL - 7), (0, 0))).reshape(9 * TAIL, C),
            jnp.zeros((8, C), BF),
        ],
        axis=0,
    ).T
    spread = np.zeros((136, CHANNELS - C), np.float32)
    for o in range(OUT):
        spread[o, o // K] = 1.0
        spread[o, A + o // K] = 16.0
    spread = jnp.asarray(spread, BF)

    shape = jax.ShapeDtypeStruct
    gclass, gred, gspat, gexp, stat = pl.pallas_call(
        main_kernel,
        out_shape=(
            shape((STACK, C), F32),
            shape((MID, C), F32),
            shape((9 * MID, MID), F32),
            shape((C, MID), F32),
            shape((8, 128), F32),
        ),
        scratch_shapes=[
            pltpu.VMEM((CHANNELS, WIDTH), BF),
            pltpu.VMEM((MID, WIDTH), BF),
            pltpu.VMEM((MID, WIDTH), BF),
            pltpu.VMEM((C, WIDTH), BF),
            pltpu.VMEM((128, WIDTH), BF),
            pltpu.VMEM((TAIL, WIDTH), F32),
            pltpu.VMEM((MID, WIDTH), BF),
            pltpu.VMEM((8, CHUNK), F32),
            pltpu.VMEM((8, CHUNK), F32),
        ],
        compiler_params=pltpu.CompilerParams(vmem_limit_bytes=56 << 20),
    )(
        fields, top, bottom, left, right,
        reduce_weight, w2, w2t, expand_weight, expand_weight.T, w3, w3t, spread,
    )

    focal, count = (stat[0, 0], stat[0, 1])
    flat = jnp.concatenate([gclass.reshape(-1), gred.reshape(-1), gspat.reshape(-1), gexp.reshape(-1)])
    size = flat.size
    share = -(-size // (128 * 128))
    flat = jnp.pad(flat, (0, share * 128 * 128 - size)).reshape(128, share, 128)
    stats = jnp.stack(split3(focal) + split3(count))
    stats = jnp.broadcast_to(jnp.pad(stats, (0, 122))[None, None], (128, 1, 128))
    sent = jnp.concatenate([flat, stats], axis=1).astype(BF)
    came = lax.all_to_all(sent, ALL, 0, 0, tiled=True)
    summed = jnp.sum(came.astype(F32), axis=0)
    focal = jnp.sum(summed[share, 0:3])
    count = jnp.sum(summed[share, 3:6])
    mine = (summed[:share] / count).astype(BF)
    copies = jnp.broadcast_to(mine[None], (128, share, 128))
    flat = lax.all_to_all(copies, ALL, 0, 0, tiled=True).astype(F32).reshape(-1)
    at = STACK * C
    rows = flat[:at].reshape(STACK, C)
    gclass = jnp.concatenate(
        [rows[: 9 * 128].reshape(9, 128, C), rows[9 * 128 : 9 * 136].reshape(9, TAIL, C)[:, :7]], axis=1
    ).reshape(3, 3, OUT, C)
    gred = flat[at : at + MID * C].reshape(MID, C)
    at = at + MID * C
    gspat = flat[at : at + 9 * MID * MID].reshape(3, 3, MID, MID)
    at = at + 9 * MID * MID
    gexp = flat[at : at + C * MID].reshape(C, MID)
    return (focal / count, gred, gspat, gexp, gclass)


def solution(mesh):
    maps = P("dp", None, "row", "col")
    return jax.shard_map(
        per_device,
        mesh=mesh,
        in_specs=(maps, P(), P(), P(), P(), maps, maps),
        out_specs=(P(), P(), P(), P(), P()),
        check_vma=False,
    )
```

profile of v0, /device:TPU:1, one launch (start us, length us, event | category | flops | bytes accessed | tf_op | source)
XLA Modules:
  0.0 168.3 jit_solution(289639422719704055)
XLA Ops:
  0.7 3.8 %copy.90 = bf16[1,256,32,128]{3,1,2,0:T(8,128)(2,1)} copy(bf16[1,256,32,128]{3,2,1,0:T(8,128)(2,1)} %param.8) | data formatting | bytes 4194304 | tf_op args[0]
  4.7 8.5 %concatenate.22 = bf16[288,32,128]{2,0,1:T(8,128)(2,1)S(1)} concatenate(bf16[256,32,128]{2,0,1:T(8,128)(2,1)} %bitcast.39, bf16[9,32,128]{2,0,1:T(8,128)(2,1)S(1)} %get-tuple-element.50, bf16[9,32,128]{2,0,1:T(8,128)(2,1)S(1)} %get-tuple-element.51, bf16[1,32,128]{2,0,1:T(2,128)(2,1)S(1)} %broadcast_in_dim.10, bf16[13,32,128]{2,0,1:T(8,128)(2,1)S(1)} %broadcast_in_dim.22), dimensions={0} | concatenate | bytes 4718592 | tf_op jit(solution)/shard_map/concatenate | solution.py:233
  13.2 1.4 collective-permute-start.1
  14.7 5.1 %collective-permute-start = (bf16[4,288,128]{2,1,0:T(8,128)(2,1)S(1)}, bf16[4,288,128]{2,1,0:T(8,128)(2,1)S(1)}, u32[]{:S(2)}, u32[]{:S(2)}) collective-permute-start(bf16[4,288,128]{2,1,0:T(8,128)(2,1)S(1)} %get-tuple-element.47), channel_id=1, source_target_pairs={{0,4},{4,8},{8,12},{1,5},{5,9},{9,13},{2,6},{6,10},{10,14},{3,7},{... | collective-permute-start | bytes 884744 | tf_op jit(solution)/shard_map/ppermute | solution.py:239
  19.9 4.6 %collective-permute-done.1.bottom_ref = bf16[4,288,128]{2,1,0:T(8,128)(2,1)S(1)} collective-permute-done((bf16[4,288,128]{2,1,0:T(8,128)(2,1)S(1)}, bf16[4,288,128]{2,1,0:T(8,128)(2,1)S(1)}, u32[]{:S(2)}, u32[]{:S(2)}) %collective-permute-start.1) | collective-permute-done | bytes 294944 | tf_op jit(solution)/shard_map/ppermute | solution.py:240
  24.5 1.0 collective-permute-done.top_ref
  26.2 4.0 %shard_map.119 = (bf16[288,256]{1,0:T(8,128)(2,1)}, bf16[288,256]{1,0:T(8,128)(2,1)}) custom-call(bf16[32,288,128]{2,1,0:T(8,128)(2,1)} %bitcast.37, bf16[4,288,128]{2,1,0:T(8,128)(2,1)} %copy-done.3, bf16[4,288,128]{2,1,0:T(8,128)(2,1)} %copy-done.2), custom_call_target="tpu_custom_call" | custom-call | tf_op jit(solution)/shard_map/pallas_call | solution.py:242
  30.2 3.0 %collective-permute-start.2 = (bf16[288,256]{1,0:T(8,128)(2,1)}, bf16[288,256]{1,0:T(8,128)(2,1)S(1)}, u32[]{:S(2)}, u32[]{:S(2)}) collective-permute-start(bf16[288,256]{1,0:T(8,128)(2,1)} %get-tuple-element.12), channel_id=1, source_target_pairs={{0,1},{1,2},{2,3},{4,5},{5,6},{6,7},{8,9},{9,10},{10,11},{12,13},{... | collective-permute-start | bytes 442376 | tf_op jit(solution)/shard_map/ppermute | solution.py:247
  33.3 1.5 collective-permute-start.3
  36.6 0.8 copy.75.w2_ref
  38.8 0.9 pad.17.w3_ref
  39.6 1.0 concatenate.23
  41.3 47.5 %shard_map.120 = (f32[1232,256]{1,0:T(8,128)}, f32[64,256]{1,0:T(8,128)}, f32[576,64]{1,0:T(8,128)}, f32[256,64]{1,0:T(8,128)}, f32[8,128]{1,0:T(8,128)}) custom-call(bf16[32,288,128]{2,1,0:T(8,128)(2,1)} %bitcast.38, bf16[4,288,128]{2,1,0:T(8,128)(2,1)} %copy-done.3, bf16[4,288,128]{2,1,0:T(8,128)(2,1)} %copy-done.2, bf16[288,256]{1,0:T(8,128)(2,1)} %copy-done.7, ...), custom_call_target="tpu_custom_call" | custom-call | tf_op jit(solution)/shard_map/pallas_call | solution.py:270
  88.8 1.4 convert_bitcast_fusion
  90.9 1.3 fusion.11
  99.5 2.7 %stack.27 = bf16[6]{0:T(256)(128)(2,1)S(1)} concatenate(f32[1]{0:T(128)} %bitcast.16, f32[1]{0:T(128)} %bitcast.17, bf16[1]{0:T(256)(128)(2,1)} %bitcast.18, f32[1]{0:T(128)} %bitcast.20, f32[1]{0:T(128)} %bitcast.21, bf16[1]{0:T(256)(128)(2,1)} %bitcast.22), dimensions={0} | concatenate | bytes 32 | tf_op jit(solution)/shard_map/stack | solution.py:301
  102.8 33.0 %all_to_all.10 = bf16[128,25,128]{2,1,0:T(8,128)(2,1)S(1)} all-to-all(bf16[128,25,128]{2,1,0:T(8,128)(2,1)S(1)} %pad_maximum_fusion.1), channel_id=1, replica_groups=mesh['dp'=8,'row'=4,'col'=4] {'dp','row','col'}, dimensions={0} | all-to-all | bytes 1638400 | tf_op jit(solution)/shard_map/all_to_all | solution.py:304
  137.4 1.0 broadcast_in_dim.25
  138.4 4.2 %all-to-all-start.1 = ((bf16[128,24,128]{2,1,0:T(8,128)(2,1)}), bf16[128,24,128]{2,1,0:T(8,128)(2,1)S(1)}, u32[]{:S(2)}, u32[]{:S(2)}) async-start(bf16[128,24,128]{2,1,0:T(8,128)(2,1)} %broadcast_in_dim.25), calls=%async_computation.1 | async-start | bytes 1572864 | tf_op jit(solution)/shard_map/all_to_all | solution.py:310
  144.0 15.6 %all-to-all-done.1 = bf16[128,24,128]{2,1,0:T(8,128)(2,1)S(1)} async-done(((bf16[128,24,128]{2,1,0:T(8,128)(2,1)}), bf16[128,24,128]{2,1,0:T(8,128)(2,1)S(1)}, u32[]{:S(2)}, u32[]{:S(2)}) %all-to-all-start.1) | async-done | bytes 786464 | tf_op jit(solution)/shard_map/all_to_all | solution.py:310
  159.6 0.8 reshape.93
  162.5 1.9 %slice.73 = f32[6144,64]{1,0:T(8,128)} reshape(bf16[128,24,128]{2,1,0:T(8,128)(2,1)S(1)} %all-to-all-done.1) | data formatting | bytes 2359296 | tf_op jit(solution)/shard_map/slice | solution.py:320
  164.4 0.9 slice.87
  166.1 1.2 pad_maximum_fusion
  (65 shorter events, 10.4 us)
Async XLA Ops:
  0.6 3.8 %copy-start.9 = (s32[1,9,32,128]{3,2,1,0:T(8,128)S(1)}, s32[1,9,32,128]{3,2,1,0:T(8,128)}, u32[]{:S(2)}) copy-start(s32[1,9,32,128]{3,2,1,0:T(8,128)} %param.14) | copy-start | bytes 442372
  0.6 3.8 %copy-start.8 = (s32[1,9,32,128]{3,2,1,0:T(8,128)S(1)}, s32[1,9,32,128]{3,2,1,0:T(8,128)}, u32[]{:S(2)}) copy-start(s32[1,9,32,128]{3,2,1,0:T(8,128)} %param.13) | copy-start | bytes 442372
  13.2 12.3 %copy-start = (bf16[288,32,128]{2,0,1:T(8,128)(2,1)}, bf16[288,32,128]{2,0,1:T(8,128)(2,1)S(1)}, u32[]{:S(2)}) copy-start(bf16[288,32,128]{2,0,1:T(8,128)(2,1)S(1)} %concatenate.22) | copy-start | bytes 7077892
  13.2 21.5 %copy-start.1 = (bf16[3,3,135,256]{3,2,1,0:T(8,128)(2,1)S(1)}, bf16[3,3,135,256]{3,2,1,0:T(8,128)(2,1)}, u32[]{:S(2)}) copy-start(bf16[3,3,135,256]{3,2,1,0:T(8,128)(2,1)} %param.12) | copy-start | bytes 1866244
  13.2 11.2 %collective-permute-start.1 = (bf16[4,288,128]{2,1,0:T(8,128)(2,1)S(1)}, bf16[4,288,128]{2,1,0:T(8,128)(2,1)S(1)}, u32[]{:S(2)}, u32[]{:S(2)}) collective-permute-start(bf16[4,288,128]{2,1,0:T(8,128)(2,1)S(1)} %get-tuple-element.46), channel_id=1, source_target_pairs={{4,0},{8,4},{12,8},{5,1},{9,5},{13,9},{6,2},{10,6},{14,10},{7,3},{... | collective-permute-start | bytes 884744 | tf_op jit(solution)/shard_map/ppermute | solution.py:240
  14.7 20.3 %copy-start.10 = (bf16[256,64]{0,1:T(8,128)(2,1)S(1)}, bf16[256,64]{0,1:T(8,128)(2,1)}, u32[]{:S(2)}) copy-start(bf16[256,64]{0,1:T(8,128)(2,1)} %param.11) | copy-start | bytes 98308
  14.7 21.0 %copy-start.4 = (bf16[3,3,64,64]{3,2,1,0:T(8,128)(2,1)S(1)}, bf16[3,3,64,64]{3,2,1,0:T(8,128)(2,1)}, u32[]{:S(2)}) copy-start(bf16[3,3,64,64]{3,2,1,0:T(8,128)(2,1)} %param.10) | copy-start | bytes 221188
  14.7 10.8 %collective-permute-start = (bf16[4,288,128]{2,1,0:T(8,128)(2,1)S(1)}, bf16[4,288,128]{2,1,0:T(8,128)(2,1)S(1)}, u32[]{:S(2)}, u32[]{:S(2)}) collective-permute-start(bf16[4,288,128]{2,1,0:T(8,128)(2,1)S(1)} %get-tuple-element.47), channel_id=1, source_target_pairs={{0,4},{4,8},{8,12},{1,5},{5,9},{9,13},{2,6},{6,10},{10,14},{3,7},{... | collective-permute-start | bytes 884744 | tf_op jit(solution)/shard_map/ppermute | solution.py:239
  24.5 1.0 copy-start.2
  25.5 0.7 copy-start.3
  30.2 10.4 %collective-permute-start.2 = (bf16[288,256]{1,0:T(8,128)(2,1)}, bf16[288,256]{1,0:T(8,128)(2,1)S(1)}, u32[]{:S(2)}, u32[]{:S(2)}) collective-permute-start(bf16[288,256]{1,0:T(8,128)(2,1)} %get-tuple-element.12), channel_id=1, source_target_pairs={{0,1},{1,2},{2,3},{4,5},{5,6},{6,7},{8,9},{9,10},{10,11},{12,13},{... | collective-permute-start | bytes 442376 | tf_op jit(solution)/shard_map/ppermute | solution.py:247
  33.3 7.4 %collective-permute-start.3 = (bf16[288,256]{1,0:T(8,128)(2,1)}, bf16[288,256]{1,0:T(8,128)(2,1)}, u32[]{:S(2)}, u32[]{:S(2)}) collective-permute-start(bf16[288,256]{1,0:T(8,128)(2,1)} %get-tuple-element.13), channel_id=1, source_target_pairs={{1,0},{2,1},{3,2},{5,4},{6,5},{7,6},{9,8},{10,9},{11,10},{13,12},{... | collective-permute-start | bytes 442376 | tf_op jit(solution)/shard_map/ppermute | solution.py:248
  40.6 0.7 copy-start.7
  88.8 13.4 %copy-start.12 = (f32[64,256]{1,0:T(8,128)S(1)}, f32[64,256]{1,0:T(8,128)}, u32[]{:S(2)}) copy-start(f32[64,256]{1,0:T(8,128)} %get-tuple-element.15) | copy-start | bytes 196612
  88.8 13.4 %copy-start.11 = (f32[256,64]{1,0:T(8,128)S(1)}, f32[256,64]{1,0:T(8,128)}, u32[]{:S(2)}) copy-start(f32[256,64]{1,0:T(8,128)} %get-tuple-element.17) | copy-start | bytes 196612
  88.8 13.5 %copy-start.6 = (f32[576,64]{1,0:T(8,128)S(1)}, f32[576,64]{1,0:T(8,128)}, u32[]{:S(2)}) copy-start(f32[576,64]{1,0:T(8,128)} %get-tuple-element.16) | copy-start | bytes 442372
  138.4 21.2 %all-to-all-start.1 = ((bf16[128,24,128]{2,1,0:T(8,128)(2,1)}), bf16[128,24,128]{2,1,0:T(8,128)(2,1)S(1)}, u32[]{:S(2)}, u32[]{:S(2)}) async-start(bf16[128,24,128]{2,1,0:T(8,128)(2,1)} %broadcast_in_dim.25), calls=%async_computation.1 | async-start | bytes 1572864 | tf_op jit(solution)/shard_map/all_to_all | solution.py:310
  162.5 3.6 %copy-start.5 = (f32[9,7,256]{2,1,0:T(8,128)S(1)}, f32[9,7,256]{2,1,0:T(8,128)}, u32[]{:S(2)}) copy-start(f32[9,7,256]{2,1,0:T(8,128)} %slice.89) | copy-start | bytes 193540
where the time goes:
time: 169 us; the launch traced here: 168 us
  Pallas kernels  51.5 us (30%)
  blocking collectives  33 us (20%)
  local copies, waits for them, and re-layouts  31.9 us (19%)
  waiting for transfers between devices  21.2 us (13%)
  starting transfers between devices  15.3 us (9%)
  between operations  10.7 us (6%)
  other arithmetic  4.6 us (3%)
    pallas_call x1, Pallas kernels, per_device(): pl.pallas_call(main_kernel, out_shape=(shape((STACK, C), F32), shape((MID...  47.5 us
    all_to_all x1, blocking collectives, per_device(): came = lax.all_to_all(sent, ALL, 0, 0, tiled=True)  33 us
    all_to_all x1, waiting for transfers between devices, per_device(): flat = lax.all_to_all(copies, ALL, 0, 0, tiled=True).astype(F32).reshape(-1)  15.6 us
    concatenate x1, local copies, waits for them, and re-layouts, per_device(): jnp.concatenate([inputs[0], anchor_labels[0].astype(BF), anchor_mask[0].a...  8.49 us
    unnamed x31, local copies, waits for them, and re-layouts  7.26 us
    ppermute x1, starting transfers between devices, per_device(): top = lax.ppermute(fields[ROWS - HALO:], 'row', ahead)  5.15 us
    ppermute x1, waiting for transfers between devices, per_device(): bottom = lax.ppermute(fields[:HALO], 'row', back)  4.6 us
    all_to_all x1, starting transfers between devices, per_device(): flat = lax.all_to_all(copies, ALL, 0, 0, tiled=True).astype(F32).reshape(-1)  4.24 us
  transfers between devices with their start and end apart: 5, of which 3 were waited for; matrix products, arithmetic and copies ran while one was open for 3% of the time, Pallas kernels for 0%

commit v1 on v0

--- a/solution.py
+++ b/solution.py
@@ -23,40 +23,51 @@
 LABEL0 = C
 MASK0 = C + A
 ONE0 = C + 2 * A
+TAGS = CHANNELS - C
 TAIL = 8
 STACK = 9 * 128 + 9 * TAIL + 8
 ALL = ("dp", "row", "col")
+DEVICES = 128
+SHARE = 24
+RED0 = 2 * STACK
+SPAT0 = RED0 + 2 * MID
+EXP0 = SPAT0 + 9 * MID // 2
+STAT0 = EXP0 + C // 2
 TAPS = [(dy - 1) * STRIDE + (dx - 1) for dy in range(3) for dx in range(3)]
 BF = jnp.bfloat16
 F32 = jnp.float32
 
 
-def row_of(top_ref, main_ref, bottom_ref, r):
-    if r < HALO:
-        return top_ref[r]
-    if r < HALO + ROWS:
-        return main_ref[r - HALO]
-    return bottom_ref[r - HALO - ROWS]
-
-
-def lanes_between(lo, hi):
-    lane = lax.broadcasted_iota(jnp.int32, (CHANNELS, 128), 1)
-    return (lane >= lo) & (lane < hi)
-
-
-def put(ref, tile, value, lo, hi):
+def put(ref, rows, tile, value, lo, hi):
+    lane = lax.broadcasted_iota(jnp.int32, value.shape, 1)
     where = slice(tile * 128, tile * 128 + 128)
-    ref[:, where] = jnp.where(lanes_between(lo, hi), value, ref[:, where])
-
-
-def pack_kernel(main_ref, top_ref, bottom_ref, left_ref, right_ref):
+    ref[rows, where] = jnp.where((lane >= lo) & (lane < hi), value, ref[rows, where])
+
+
+BODY = slice(0, C)
+REST = slice(C, CHANNELS)
+BOTH = slice(0, CHANNELS)
+
+
+def edges_kernel(maps_ref, tags_ref, left_ref, right_ref):
     left_ref[...] = jnp.zeros_like(left_ref)
     right_ref[...] = jnp.zeros_like(right_ref)
-    for r in range(FULL):
-        row = row_of(top_ref, main_ref, bottom_ref, r)
-        at = (4 * r) % 128
-        put(left_ref, 4 * r // 128, pltpu.roll(row, at, 1), at, at + 4)
-        put(right_ref, 4 * r // 128, pltpu.roll(row, (at + 4) % 128, 1), at, at + 4)
+    for r in range(ROWS):
+        at = HALO * r
+        for rows, source in ((BODY, maps_ref[r]), (REST, tags_ref[r])):
+            put(left_ref, rows, 0, pltpu.roll(source, at, 1), at, at + HALO)
+            put(right_ref, rows, 0, pltpu.roll(source, (at + HALO) % 128, 1), at, at + HALO)
+
+
+def corners_kernel(left_ref, right_ref, top_ref, bottom_ref, wide_left_ref, wide_right_ref):
+    for edge_ref, wide_ref in ((left_ref, wide_left_ref), (right_ref, wide_right_ref)):
+        wide_ref[:, :128] = edge_ref[...]
+        wide_ref[:, 128:] = jnp.zeros_like(edge_ref)
+    for h in range(2 * HALO):
+        source = top_ref[h] if h < HALO else bottom_ref[h - HALO]
+        at = HALO * h
+        put(wide_left_ref, BOTH, 1, pltpu.roll(source, at, 1), at, at + HALO)
+        put(wide_right_ref, BOTH, 1, pltpu.roll(source, at + HALO, 1), at, at + HALO)
 
 
 def window(ref, rows, lane, shift):
@@ -92,27 +103,37 @@
 
 
 def main_kernel(
-    main_ref, top_ref, bottom_ref, left_ref, right_ref,
+    maps_ref, tags_ref, top_ref, bottom_ref, left_ref, right_ref,
     wr_ref, w2_ref, w2t_ref, we_ref, wet_ref, w3_ref, w3t_ref, e_ref,
-    gclass_ref, gred_ref, gspat_ref, gexp_ref, stat_ref,
+    out_ref,
     x_ref, first_ref, second_ref, block_ref, d_ref, dt_ref, ds_ref, facc_ref, cacc_ref,
+    gclass_ref, gred_ref, gspat_ref, gexp_ref,
 ):
     for ref in (x_ref, first_ref, second_ref, block_ref, d_ref, dt_ref, ds_ref):
         ref[...] = jnp.zeros_like(ref)
     for ref in (gclass_ref, gred_ref, gspat_ref, gexp_ref, facc_ref, cacc_ref):
         ref[...] = jnp.zeros_like(ref)
     for r in range(FULL):
-        row = row_of(top_ref, main_ref, bottom_ref, r)
+        if r < HALO:
+            sources = ((BOTH, top_ref[r]),)
+        elif r < HALO + ROWS:
+            sources = ((BODY, maps_ref[r - HALO]), (REST, tags_ref[r - HALO]))
+        else:
+            sources = ((BOTH, bottom_ref[r - HALO - ROWS]),)
         at = MARGIN + r * STRIDE + HALO
         turn, tile = (at % 128, at // 128)
-        turned = pltpu.roll(row, turn, 1)
-        put(x_ref, tile, turned, turn, 128)
-        put(x_ref, tile + 1, turned, 0, turn)
-        source = slice(4 * r // 128 * 128, 4 * r // 128 * 128 + 128)
-        at = MARGIN + r * STRIDE
-        put(x_ref, at // 128, pltpu.roll(left_ref[:, source], (4 * r) % 128, 1), at % 128, at % 128 + 4)
-        at = at + HALO + COLS
-        put(x_ref, at // 128, pltpu.roll(right_ref[:, source], (4 * r + 4) % 128, 1), at % 128, at % 128 + 4)
+        for rows, source in sources:
+            turned = pltpu.roll(source, turn, 1)
+            put(x_ref, rows, tile, turned, turn, 128)
+            put(x_ref, rows, tile + 1, turned, 0, turn)
+        if HALO <= r < HALO + ROWS:
+            spot = HALO * (r - HALO)
+        else:
+            spot = 128 + HALO * (r if r < HALO else r - ROWS)
+        source = slice(spot // 128 * 128, spot // 128 * 128 + 128)
+        for edge_ref, at in ((left_ref, MARGIN + r * STRIDE), (right_ref, MARGIN + r * STRIDE + HALO + COLS)):
+            turned = pltpu.roll(edge_ref[:, source], (at - spot) % 128, 1)
+            put(x_ref, BOTH, at // 128, turned, at % 128, at % 128 + HALO)
 
     def first_step(lane):
         x = x_ref[:C, pl.ds(lane, CHUNK)]
@@ -213,37 +234,108 @@
 
     chunks(384, 10, first_back)
 
-    focal = jnp.sum(facc_ref[...])
-    count = jnp.sum(cacc_ref[...])
-    lane = lax.broadcasted_iota(jnp.int32, (8, 128), 1)
-    stat_ref[...] = jnp.where(lane == 0, focal, jnp.where(lane == 1, count, 0.0))
-
-
-def split3(x):
-    hi = lax.reduce_precision(x, 8, 7)
-    mid = lax.reduce_precision(x - hi, 8, 7)
-    return [hi, mid, x - hi - mid]
+    out_ref[:STACK] = gclass_ref[:, :128].astype(BF)
+    out_ref[STACK:RED0] = gclass_ref[:, 128:].astype(BF)
+    out_ref[RED0 : RED0 + MID] = gred_ref[:, :128].astype(BF)
+    out_ref[RED0 + MID : SPAT0] = gred_ref[:, 128:].astype(BF)
+    half = 9 * MID // 2
+    out_ref[SPAT0:EXP0] = jnp.concatenate([gspat_ref[:half], gspat_ref[half:]], axis=1).astype(BF)
+    half = C // 2
+    out_ref[EXP0:STAT0] = jnp.concatenate([gexp_ref[:half], gexp_ref[half:]], axis=1).astype(BF)
+    out_ref[STAT0:] = jnp.zeros((DEVICES * SHARE - STAT0, 128), BF)
+    focal = jnp.sum(facc_ref[...], keepdims=True)
+    count = jnp.sum(cacc_ref[...], keepdims=True)
+    out_ref[STAT0 : STAT0 + 16] = stat_rows(focal, count, 16).astype(BF)
+
+
+def rounded(x):
+    return x.astype(BF).astype(F32)
+
+
+def stat_rows(focal, count, rows):
+    lane = lax.broadcasted_iota(jnp.int32, (rows, 128), 1)
+    out = jnp.zeros((rows, 128), F32)
+    for at, value in ((0, focal), (3, count)):
+        value = jnp.broadcast_to(value, (rows, 128))
+        for k in range(3):
+            piece = rounded(value)
+            out = jnp.where(lane == at + k, piece, out)
+            value = value - piece
+    return out
+
+
+def stat_values(row):
+    lane = lax.broadcasted_iota(jnp.int32, row.shape, 1)
+    focal = jnp.sum(jnp.where(lane < 3, row, 0.0), axis=1, keepdims=True)
+    count = jnp.sum(jnp.where((lane >= 3) & (lane < 6), row, 0.0), axis=1, keepdims=True)
+    return focal, count
+
+
+def sum_kernel(index_ref, came_ref, copies_ref):
+    total = came_ref[0].astype(F32)
+    for k in range(1, DEVICES):
+        total = total + came_ref[k].astype(F32)
+    row = STAT0 % SHARE
+    at = lax.broadcasted_iota(jnp.int32, (SHARE, 128), 0)
+    focal, count = stat_values(total[row : row + 1])
+    stats = stat_rows(focal, count, SHARE)
+    total = jnp.where((at == row) & (index_ref[0] == STAT0 // SHARE), stats, total)
+    total = total.astype(BF)
+    for k in range(DEVICES):
+        copies_ref[k] = total
+
+
+def final_kernel(flat_ref, loss_ref, gred_ref, gspat_ref, gexp_ref, gclass_ref):
+    focal, count = stat_values(flat_ref[STAT0 : STAT0 + 16].astype(F32)[:1])
+    scale = 1.0 / count
+    loss_ref[...] = focal * scale
+
+    def rows(lo, n):
+        return flat_ref[lo : lo + n].astype(F32) * scale
+
+    for half in range(2):
+        lanes = slice(half * 128, half * 128 + 128)
+        tails = rows(half * STACK + 9 * 128, STACK - 9 * 128)
+        for t in range(9):
+            gclass_ref[t, :128, lanes] = rows(half * STACK + t * 128, 128)
+            gclass_ref[t, 128:, lanes] = tails[t * TAIL : t * TAIL + 7]
+        gred_ref[:, lanes] = rows(RED0 + half * MID, MID)
+    spat = rows(SPAT0, 9 * MID // 2)
+    gspat_ref[: 9 * MID // 2] = spat[:, :MID]
+    gspat_ref[9 * MID // 2 :] = spat[:, MID:]
+    expand = rows(EXP0, C // 2)
+    gexp_ref[: C // 2] = expand[:, :MID]
+    gexp_ref[C // 2 :] = expand[:, MID:]
 
 
 def per_device(
     inputs, reduce_weight, spatial_weight, expand_weight, class_weight, anchor_labels, anchor_mask
 ):
     one = jnp.ones((1, ROWS, COLS), BF)
-    none = jnp.zeros((CHANNELS - C - 2 * A - 1, ROWS, COLS), BF)
-    fields = jnp.concatenate(
-        [inputs[0], anchor_labels[0].astype(BF), anchor_mask[0].astype(BF), one, none], axis=0
+    none = jnp.zeros((TAGS - 2 * A - 1, ROWS, COLS), BF)
+    tags = jnp.concatenate(
+        [anchor_labels[0].astype(BF), anchor_mask[0].astype(BF), one, none], axis=0
     )
-    fields = jnp.transpose(fields, (1, 0, 2))
+
+    def edge_rows(at):
+        fields = jnp.concatenate([inputs[0, :, at : at + HALO], tags[:, at : at + HALO]], axis=0)
+        return jnp.transpose(fields, (1, 0, 2))
+
     ahead = [(i, i + 1) for i in range(3)]
     back = [(i + 1, i) for i in range(3)]
-    top = lax.ppermute(fields[ROWS - HALO :], "row", ahead)
-    bottom = lax.ppermute(fields[:HALO], "row", back)
+    top = lax.ppermute(edge_rows(ROWS - HALO), "row", ahead)
+    bottom = lax.ppermute(edge_rows(0), "row", back)
+    maps = jnp.transpose(inputs[0], (1, 0, 2))
+    tags = jnp.transpose(tags, (1, 0, 2))
+    params = pltpu.CompilerParams(vmem_limit_bytes=56 << 20)
+    pack = jax.ShapeDtypeStruct((CHANNELS, 128), BF)
+    left_edge, right_edge = pl.pallas_call(
+        edges_kernel, out_shape=(pack, pack), compiler_params=params
+    )(maps, tags)
     pack = jax.ShapeDtypeStruct((CHANNELS, 256), BF)
     left_edge, right_edge = pl.pallas_call(
-        pack_kernel,
-        out_shape=(pack, pack),
-        compiler_params=pltpu.CompilerParams(vmem_limit_bytes=56 << 20),
-    )(fields, top, bottom)
+        corners_kernel, out_shape=(pack, pack), compiler_params=params
+    )(left_edge, right_edge, top, bottom)
     left = lax.ppermute(right_edge, "col", ahead)
     right = lax.ppermute(left_edge, "col", back)
 
@@ -267,15 +359,9 @@
     spread = jnp.asarray(spread, BF)
 
     shape = jax.ShapeDtypeStruct
-    gclass, gred, gspat, gexp, stat = pl.pallas_call(
+    out = pl.pallas_call(
         main_kernel,
-        out_shape=(
-            shape((STACK, C), F32),
-            shape((MID, C), F32),
-            shape((9 * MID, MID), F32),
-            shape((C, MID), F32),
-            shape((8, 128), F32),
-        ),
+        out_shape=shape((DEVICES * SHARE, 128), BF),
         scratch_shapes=[
             pltpu.VMEM((CHANNELS, WIDTH), BF),
             pltpu.VMEM((MID, WIDTH), BF),
@@ -286,39 +372,48 @@
             pltpu.VMEM((MID, WIDTH), BF),
             pltpu.VMEM((8, CHUNK), F32),
             pltpu.VMEM((8, CHUNK), F32),
+            pltpu.VMEM((STACK, C), F32),
+            pltpu.VMEM((MID, C), F32),
+            pltpu.VMEM((9 * MID, MID), F32),
+            pltpu.VMEM((C, MID), F32),
         ],
-        compiler_params=pltpu.CompilerParams(vmem_limit_bytes=56 << 20),
+        compiler_params=params,
     )(
-        fields, top, bottom, left, right,
+        maps, tags, top, bottom, left, right,
         reduce_weight, w2, w2t, expand_weight, expand_weight.T, w3, w3t, spread,
     )
 
-    focal, count = (stat[0, 0], stat[0, 1])
-    flat = jnp.concatenate([gclass.reshape(-1), gred.reshape(-1), gspat.reshape(-1), gexp.reshape(-1)])
-    size = flat.size
-    share = -(-size // (128 * 128))
-    flat = jnp.pad(flat, (0, share * 128 * 128 - size)).reshape(128, share, 128)
-    stats = jnp.stack(split3(focal) + split3(count))
-    stats = jnp.broadcast_to(jnp.pad(stats, (0, 122))[None, None], (128, 1, 128))
-    sent = jnp.concatenate([flat, stats], axis=1).astype(BF)
+    sent = out.reshape(DEVICES, SHARE, 128)
     came = lax.all_to_all(sent, ALL, 0, 0, tiled=True)
-    summed = jnp.sum(came.astype(F32), axis=0)
-    focal = jnp.sum(summed[share, 0:3])
-    count = jnp.sum(summed[share, 3:6])
-    mine = (summed[:share] / count).astype(BF)
-    copies = jnp.broadcast_to(mine[None], (128, share, 128))
-    flat = lax.all_to_all(copies, ALL, 0, 0, tiled=True).astype(F32).reshape(-1)
-    at = STACK * C
-    rows = flat[:at].reshape(STACK, C)
-    gclass = jnp.concatenate(
-        [rows[: 9 * 128].reshape(9, 128, C), rows[9 * 128 : 9 * 136].reshape(9, TAIL, C)[:, :7]], axis=1
-    ).reshape(3, 3, OUT, C)
-    gred = flat[at : at + MID * C].reshape(MID, C)
-    at = at + MID * C
-    gspat = flat[at : at + 9 * MID * MID].reshape(3, 3, MID, MID)
-    at = at + 9 * MID * MID
-    gexp = flat[at : at + C * MID].reshape(C, MID)
-    return (focal / count, gred, gspat, gexp, gclass)
+    index = lax.axis_index(ALL).astype(jnp.int32).reshape(1)
+    copies = pl.pallas_call(
+        sum_kernel,
+        out_shape=shape((DEVICES, SHARE, 128), BF),
+        in_specs=[
+            pl.BlockSpec(memory_space=pltpu.SMEM),
+            pl.BlockSpec(memory_space=pltpu.VMEM),
+        ],
+        compiler_params=params,
+    )(index, came)
+    flat = lax.all_to_all(copies, ALL, 0, 0, tiled=True).reshape(DEVICES * SHARE, 128)
+    loss, gred, gspat, gexp, gclass = pl.pallas_call(
+        final_kernel,
+        out_shape=(
+            shape((1, 1), F32),
+            shape((MID, C), F32),
+            shape((9 * MID, MID), F32),
+            shape((C, MID), F32),
+            shape((9, OUT, C), F32),
+        ),
+        compiler_params=params,
+    )(flat)
+    return (
+        loss.reshape(()),
+        gred,
+        gspat.reshape(3, 3, MID, MID),
+        gexp,
+        gclass.reshape(3, 3, OUT, C),
+    )
 
 
 def solution(mesh):

time: 169 us -> 140 us (0.83)
  local copies, waits for them, and re-layouts: 31.9 us -> 12.3 us
  blocking collectives: 33 us -> 21.9 us
  between operations: 10.7 us -> 0.84 us
  starting transfers between devices: 15.3 us -> 22.8 us
  Pallas kernels: 51.5 us -> 58.1 us
  other arithmetic: 4.6 us -> 2.17 us
    all_to_all x1, blocking collectives: 33 us -> 21.9 us  [per_device(): lax.all_to_all(copies, ALL, 0, 0, tiled=True).reshape(DEVICES * SHARE, 128)]
    concatenate x2, local copies, waits for them, and re-layouts: 8.83 us -> 0.15 us  [per_device(): jnp.concatenate([anchor_labels[0].astype(BF), anchor_mask[0].astype(BF),...]
    all_to_all x1, starting transfers between devices: 4.24 us -> 12.4 us  [per_device(): came = lax.all_to_all(sent, ALL, 0, 0, tiled=True)]
    pallas_call x2 -> x5, Pallas kernels: 51.5 us -> 58.1 us  [the longest x1 47.6 us: per_device(): pl.pallas_call(main_kernel, out_shape=shape((DEVICES * SHARE, 128), BF),...]
    slice x10 -> x1, local copies, waits for them, and re-layouts: 5.98 us -> 0.01 us  [edge_rows(): tags[:, at:at + HALO]]
    another operation x2 -> x0, local copies, waits for them, and re-layouts: 2.68 us -> none  [the longest x1 2.67 us: per_device(): stats = jnp.stack(split3(focal) + split3(count))]
    unnamed x31 -> x21, local copies, waits for them, and re-layouts: 7.26 us -> 7.05 us
  transfers between devices with their start and end apart: 5 -> 5, of which waited for: 3 -> 2; matrix products, arithmetic and copies ran while one was open for 3% -> 5% of each run, Pallas kernels for 0% -> 3%
where the time goes in v1:
time: 140 us; the launch traced here: 139 us
  Pallas kernels  58.1 us (42%)
  starting transfers between devices  22.8 us (16%)
  blocking collectives  21.9 us (16%)
  waiting for transfers between devices  20.9 us (15%)
  local copies, waits for them, and re-layouts  12.3 us (9%)
  other arithmetic  2.17 us (2%)
    pallas_call x1, Pallas kernels, per_device(): pl.pallas_call(main_kernel, out_shape=shape((DEVICES * SHARE, 128), BF),...  47.6 us
    all_to_all x1, blocking collectives, per_device(): lax.all_to_all(copies, ALL, 0, 0, tiled=True).reshape(DEVICES * SHARE, 128)  21.9 us
    all_to_all x1, waiting for transfers between devices, per_device(): came = lax.all_to_all(sent, ALL, 0, 0, tiled=True)  16.8 us
    all_to_all x1, starting transfers between devices, per_device(): came = lax.all_to_all(sent, ALL, 0, 0, tiled=True)  12.4 us
    unnamed x21, local copies, waits for them, and re-layouts  7.05 us
    ppermute x1, starting transfers between devices, per_device(): top = lax.ppermute(edge_rows(ROWS - HALO), 'row', ahead)  4.39 us
    ppermute x1, waiting for transfers between devices, per_device(): bottom = lax.ppermute(edge_rows(0), 'row', back)  4.16 us
    pallas_call x1, Pallas kernels, per_device(): pl.pallas_call(edges_kernel, out_shape=(pack, pack), compiler_params=params)  3.52 us
  transfers between devices with their start and end apart: 5, of which 2 were waited for; matrix products, arithmetic and copies ran while one was open for 5% of the time, Pallas kernels for 3%

profile of v1, /device:TPU:1, one launch (start us, length us, event | category | flops | bytes accessed | tf_op | source)
XLA Modules:
  0.0 139.2 jit_solution(8714113088130935856)
XLA Ops:
  0.8 1.2 fusion
  2.1 2.4 %copy.46 = bf16[1,256,32,128]{3,1,2,0:T(8,128)(2,1)S(1)} copy(bf16[1,256,32,128]{3,2,1,0:T(8,128)(2,1)} %param.8) | data formatting | bytes 4194304 | tf_op args[0]
  4.6 4.4 %collective-permute-start = (bf16[4,288,128]{2,1,0:T(8,128)(2,1)S(1)}, bf16[4,288,128]{2,1,0:T(8,128)(2,1)S(1)}, u32[]{:S(2)}, u32[]{:S(2)}) collective-permute-start(bf16[4,288,128]{2,1,0:T(8,128)(2,1)S(1)} %maximum_bitcast_fusion), channel_id=1, source_target_pairs={{0,4},{4,8},{8,12},{1,5},{5,9},{9,13},{2,6},{6,10},{10,14},{3,7},{... | collective-permute-start | bytes 884744 | tf_op jit(solution)/shard_map/ppermute | solution.py:326
  9.0 1.4 %collective-permute-start.1 = (bf16[4,288,128]{2,1,0:T(8,128)(2,1)S(1)}, bf16[4,288,128]{2,1,0:T(8,128)(2,1)S(1)}, u32[]{:S(2)}, u32[]{:S(2)}) collective-permute-start(bf16[4,288,128]{2,1,0:T(8,128)(2,1)S(1)} %maximum_bitcast_fusion.1), channel_id=1, source_target_pairs={{4,0},{8,4},{12,8},{5,1},{9,5},{13,9},{6,2},{10,6},{14,10},{7,3},{... | collective-permute-start | bytes 884744 | tf_op jit(solution)/shard_map/ppermute | solution.py:327
  10.5 0.8 fusion.4.tags_ref
  11.3 3.5 %shard_map.119 = (bf16[288,128]{1,0:T(8,128)(2,1)}, bf16[288,128]{1,0:T(8,128)(2,1)}) custom-call(bf16[32,256,128]{2,1,0:T(8,128)(2,1)} %bitcast.37, bf16[32,32,128]{2,1,0:T(8,128)(2,1)} %fusion.4.tags_ref), custom_call_target="tpu_custom_call" | custom-call | tf_op jit(solution)/shard_map/pallas_call | solution.py:332
  14.8 4.2 %collective-permute-done.1.bottom_ref = bf16[4,288,128]{2,1,0:T(8,128)(2,1)S(1)} collective-permute-done((bf16[4,288,128]{2,1,0:T(8,128)(2,1)S(1)}, bf16[4,288,128]{2,1,0:T(8,128)(2,1)S(1)}, u32[]{:S(2)}, u32[]{:S(2)}) %collective-permute-start.1) | collective-permute-done | bytes 294944 | tf_op jit(solution)/shard_map/ppermute | solution.py:327
  19.7 2.2 %shard_map.120 = (bf16[288,256]{1,0:T(8,128)(2,1)}, bf16[288,256]{1,0:T(8,128)(2,1)}) custom-call(bf16[288,128]{1,0:T(8,128)(2,1)} %get-tuple-element.14.left_ref, bf16[288,128]{1,0:T(8,128)(2,1)} %get-tuple-element.15.right_ref, bf16[4,288,128]{2,1,0:T(8,128)(2,1)} %copy-done.3, bf16[4,288,128]{2,1,0:T(8,128)(2,1)} %copy-done.4), custom_call_target="tpu_custom_call" | custom-call | tf_op jit(solution)/shard_map/pallas_call | solution.py:336
  21.9 3.1 %collective-permute-start.2 = (bf16[288,256]{1,0:T(8,128)(2,1)}, bf16[288,256]{1,0:T(8,128)(2,1)S(1)}, u32[]{:S(2)}, u32[]{:S(2)}) collective-permute-start(bf16[288,256]{1,0:T(8,128)(2,1)} %get-tuple-element.16), channel_id=1, source_target_pairs={{0,1},{1,2},{2,3},{4,5},{5,6},{6,7},{8,9},{9,10},{10,11},{12,13},{... | collective-permute-start | bytes 442376 | tf_op jit(solution)/shard_map/ppermute | solution.py:339
  25.0 1.5 %collective-permute-start.3 = (bf16[288,256]{1,0:T(8,128)(2,1)}, bf16[288,256]{1,0:T(8,128)(2,1)S(1)}, u32[]{:S(2)}, u32[]{:S(2)}) collective-permute-start(bf16[288,256]{1,0:T(8,128)(2,1)} %get-tuple-element.17), channel_id=1, source_target_pairs={{1,0},{2,1},{3,2},{5,4},{6,5},{7,6},{9,8},{10,9},{11,10},{13,12},{... | collective-permute-start | bytes 442376 | tf_op jit(solution)/shard_map/ppermute | solution.py:340
  27.3 0.7 reshape.51
  28.0 0.9 pad.8.w3_ref
  29.1 0.8 copy.34.w2_ref
  29.8 0.8 copy.35.w2t_ref
  30.6 0.7 copy.36.we_ref
  31.4 1.0 concatenate.15
  33.1 47.6 %shard_map.121 = bf16[3072,128]{1,0:T(8,128)(2,1)} custom-call(bf16[32,256,128]{2,1,0:T(8,128)(2,1)} %bitcast.38, bf16[32,32,128]{2,1,0:T(8,128)(2,1)} %fusion.4.tags_ref, bf16[4,288,128]{2,1,0:T(8,128)(2,1)} %copy-done.3, bf16[4,288,128]{2,1,0:T(8,128)(2,1)} %copy-done.4, bf16[288,256]{1,0:T(8,128)(2,1)} %copy-done.6, bf16[288,256]{1,0:T(8,128)(2,1)} %copy-done.7, ...), custom_call_target="tpu_custom_call" | custom-call | tf_op jit(solution)/shard_map/pallas_call | solution.py:362
  80.7 12.4 %all-to-all-start = ((bf16[128,24,128]{2,1,0:T(8,128)(2,1)}), bf16[128,24,128]{2,1,0:T(8,128)(2,1)S(1)}, u32[]{:S(2)}, u32[]{:S(2)}) async-start(bf16[128,24,128]{2,1,0:T(8,128)(2,1)} %bitcast.40), calls=%async_computation | async-start | bytes 1572864 | tf_op jit(solution)/shard_map/all_to_all | solution.py:387
  93.2 16.8 %all-to-all-done.came_ref = bf16[128,24,128]{2,1,0:T(8,128)(2,1)S(1)} async-done(((bf16[128,24,128]{2,1,0:T(8,128)(2,1)}), bf16[128,24,128]{2,1,0:T(8,128)(2,1)S(1)}, u32[]{:S(2)}, u32[]{:S(2)}) %all-to-all-start) | async-done | bytes 786464 | tf_op jit(solution)/shard_map/all_to_all | solution.py:387
  109.9 0.9 copy-done.1
  110.8 2.3 %shard_map.122 = bf16[128,24,128]{2,1,0:T(8,128)(2,1)} custom-call(s32[1]{0:T(128)} %bitcast.index_ref, bf16[128,24,128]{2,1,0:T(8,128)(2,1)} %copy-done.1), custom_call_target="tpu_custom_call" | custom-call | tf_op jit(solution)/shard_map/pallas_call | solution.py:389
  113.1 21.9 %all_to_all.10 = bf16[128,24,128]{2,1,0:T(8,128)(2,1)} all-to-all(bf16[128,24,128]{2,1,0:T(8,128)(2,1)} %shard_map.122), channel_id=1, replica_groups=mesh['dp'=8,'row'=4,'col'=4] {'dp','row','col'}, dimensions={0} | all-to-all | bytes 1572864 | tf_op jit(solution)/shard_map/all_to_all | solution.py:398
  135.0 2.5 %shard_map.123 = (f32[1,1]{1,0:T(1,128)}, f32[64,256]{1,0:T(8,128)}, f32[576,64]{1,0:T(8,128)}, f32[256,64]{1,0:T(8,128)}, f32[9,135,256]{2,1,0:T(8,128)}) custom-call(bf16[3072,128]{1,0:T(8,128)(2,1)} %bitcast.39), custom_call_target="tpu_custom_call" | custom-call | tf_op jit(solution)/shard_map/pallas_call | solution.py:399
  137.6 1.6 %copy.37 = f32[256,64]{0,1:T(8,128)} copy(f32[256,64]{1,0:T(8,128)} %get-tuple-element.31) | data formatting | bytes 131072
  (36 shorter events, 2.7 us)
Async XLA Ops:
  4.5 6.8 %copy-start = (bf16[1,256,32,128]{3,1,2,0:T(8,128)(2,1)}, bf16[1,256,32,128]{3,1,2,0:T(8,128)(2,1)S(1)}, u32[]{:S(2)}) copy-start(bf16[1,256,32,128]{3,1,2,0:T(8,128)(2,1)S(1)} %copy.46) | copy-start | bytes 6291460
  4.6 10.2 %collective-permute-start = (bf16[4,288,128]{2,1,0:T(8,128)(2,1)S(1)}, bf16[4,288,128]{2,1,0:T(8,128)(2,1)S(1)}, u32[]{:S(2)}, u32[]{:S(2)}) collective-permute-start(bf16[4,288,128]{2,1,0:T(8,128)(2,1)S(1)} %maximum_bitcast_fusion), channel_id=1, source_target_pairs={{0,4},{4,8},{8,12},{1,5},{5,9},{9,13},{2,6},{6,10},{10,14},{3,7},{... | collective-permute-start | bytes 884744 | tf_op jit(solution)/shard_map/ppermute | solution.py:326
  9.0 17.5 %copy-start.2 = (bf16[3,3,135,256]{3,2,1,0:T(8,128)(2,1)S(1)}, bf16[3,3,135,256]{3,2,1,0:T(8,128)(2,1)}, u32[]{:S(2)}) copy-start(bf16[3,3,135,256]{3,2,1,0:T(8,128)(2,1)} %param.12) | copy-start | bytes 1866244
  9.0 9.9 %collective-permute-start.1 = (bf16[4,288,128]{2,1,0:T(8,128)(2,1)S(1)}, bf16[4,288,128]{2,1,0:T(8,128)(2,1)S(1)}, u32[]{:S(2)}, u32[]{:S(2)}) collective-permute-start(bf16[4,288,128]{2,1,0:T(8,128)(2,1)S(1)} %maximum_bitcast_fusion.1), channel_id=1, source_target_pairs={{4,0},{8,4},{12,8},{5,1},{9,5},{13,9},{6,2},{10,6},{14,10},{7,3},{... | collective-permute-start | bytes 884744 | tf_op jit(solution)/shard_map/ppermute | solution.py:327
  14.8 4.2 %copy-start.3 = (bf16[4,288,128]{2,1,0:T(8,128)(2,1)}, bf16[4,288,128]{2,1,0:T(8,128)(2,1)S(1)}, u32[]{:S(2)}) copy-start(bf16[4,288,128]{2,1,0:T(8,128)(2,1)S(1)} %collective-permute-done.top_ref) | copy-start | bytes 884740
  19.0 0.7 copy-start.4
  21.9 10.5 %collective-permute-start.2 = (bf16[288,256]{1,0:T(8,128)(2,1)}, bf16[288,256]{1,0:T(8,128)(2,1)S(1)}, u32[]{:S(2)}, u32[]{:S(2)}) collective-permute-start(bf16[288,256]{1,0:T(8,128)(2,1)} %get-tuple-element.16), channel_id=1, source_target_pairs={{0,1},{1,2},{2,3},{4,5},{5,6},{6,7},{8,9},{9,10},{10,11},{12,13},{... | collective-permute-start | bytes 442376 | tf_op jit(solution)/shard_map/ppermute | solution.py:339
  25.0 7.4 %collective-permute-start.3 = (bf16[288,256]{1,0:T(8,128)(2,1)}, bf16[288,256]{1,0:T(8,128)(2,1)S(1)}, u32[]{:S(2)}, u32[]{:S(2)}) collective-permute-start(bf16[288,256]{1,0:T(8,128)(2,1)} %get-tuple-element.17), channel_id=1, source_target_pairs={{1,0},{2,1},{3,2},{5,4},{6,5},{7,6},{9,8},{10,9},{11,10},{13,12},{... | collective-permute-start | bytes 442376 | tf_op jit(solution)/shard_map/ppermute | solution.py:340
  27.0 2.0 %copy-start.5 = (bf16[3,3,64,64]{3,2,1,0:T(8,128)(2,1)S(1)}, bf16[3,3,64,64]{3,2,1,0:T(8,128)(2,1)}, u32[]{:S(2)}) copy-start(bf16[3,3,64,64]{3,2,1,0:T(8,128)(2,1)} %param.10) | copy-start | bytes 221188
  27.3 3.3 %copy-start.8 = (bf16[256,64]{0,1:T(8,128)(2,1)S(1)}, bf16[256,64]{0,1:T(8,128)(2,1)}, u32[]{:S(2)}) copy-start(bf16[256,64]{0,1:T(8,128)(2,1)} %param.11) | copy-start | bytes 98308
  32.4 0.6 copy-start.6
  32.4 0.7 copy-start.7
  80.7 29.2 %all-to-all-start = ((bf16[128,24,128]{2,1,0:T(8,128)(2,1)}), bf16[128,24,128]{2,1,0:T(8,128)(2,1)S(1)}, u32[]{:S(2)}, u32[]{:S(2)}) async-start(bf16[128,24,128]{2,1,0:T(8,128)(2,1)} %bitcast.40), calls=%async_computation | async-start | bytes 1572864 | tf_op jit(solution)/shard_map/all_to_all | solution.py:387
  109.9 0.9 copy-start.1

commit v2 on v1

--- a/solution.py
+++ b/solution.py
@@ -19,7 +19,17 @@
 CHANNELS = 288
 MARGIN = 256
 WIDTH = 6400
-CHUNK = 512
+RIGHT = MARGIN + 5120
+SPLIT = (
+    (0, 2816, 2),
+    (0, 2816, 2),
+    (128, 2688, 2),
+    (0, 2816, 2),
+    (256, 1024, 5),
+    (384, 2432, 2),
+    (384, 2432, 2),
+    (512, 2304, 2),
+)
 LABEL0 = C
 MASK0 = C + A
 ONE0 = C + 2 * A
@@ -70,22 +80,26 @@
         put(wide_right_ref, BOTH, 1, pltpu.roll(source, at + HALO, 1), at, at + HALO)
 
 
-def window(ref, rows, lane, shift):
+def window(ref, rows, lane, shift, n):
     base = (shift // 128) * 128
     turn = shift - base
     if turn == 0:
-        return ref[rows, pl.ds(pl.multiple_of(lane + base, 128), CHUNK)]
-    wide = ref[rows, pl.ds(pl.multiple_of(lane + base, 128), CHUNK + 128)]
-    return pltpu.roll(wide, CHUNK + 128 - turn, 1)[:, :CHUNK]
-
-
-def interior(lane, shift):
-    p = lane - MARGIN + shift + lax.broadcasted_iota(jnp.int32, (1, CHUNK), 1)
+        return ref[rows, pl.ds(pl.multiple_of(lane + base, 128), n)]
+    wide = ref[rows, pl.ds(pl.multiple_of(lane + base, 128), n + 128)]
+    return pltpu.roll(wide, n + 128 - turn, 1)[:, :n]
+
+
+def interior(lane, shift, n):
+    p = lane - MARGIN + shift + lax.broadcasted_iota(jnp.int32, (1, n), 1)
     r = (p * 30841) >> 22
     c = p - r * STRIDE
     return (r >= HALO) & (r < HALO + ROWS) & (c >= HALO) & (c < HALO + COLS)
 
 
+def masked(value, mask):
+    return value * jnp.where(mask, 1.0, 0.0).astype(BF)
+
+
 def dot(a, b):
     return jnp.dot(a, b, preferred_element_type=F32)
 
@@ -94,23 +108,36 @@
     return lax.dot_general(a, b, (((1,), (1,)), ((), ())), preferred_element_type=F32)
 
 
-def chunks(start, count, body):
+def chunks(start, n, count, body):
     def step(j, carry):
-        body(pl.multiple_of(MARGIN + start + j * CHUNK, 128))
+        body(pl.multiple_of(MARGIN + start + j * n, 128), n)
         return carry
 
     lax.fori_loop(0, count, step, 0)
+
+
+def across(ref, lane, sign, n):
+    return jnp.concatenate([window(ref, slice(None), lane, sign * k, n) for k in (-1, 0, 1)], axis=0)
+
+
+def down(ref, lane, sign, size, n):
+    parts = [
+        window(ref, slice(k * size, k * size + size), lane, sign * (k - 1) * STRIDE, n)
+        for k in range(3)
+    ]
+    return parts[0] + parts[1] + parts[2]
 
 
 def main_kernel(
     maps_ref, tags_ref, top_ref, bottom_ref, left_ref, right_ref,
     wr_ref, w2_ref, w2t_ref, we_ref, wet_ref, w3_ref, w3t_ref, e_ref,
     out_ref,
-    x_ref, first_ref, second_ref, block_ref, d_ref, dt_ref, ds_ref, facc_ref, cacc_ref,
+    x_ref, first_ref, second_ref, block_ref, d_ref, dt_ref, ds_ref, p_ref, facc_ref, cacc_ref,
     gclass_ref, gred_ref, gspat_ref, gexp_ref,
 ):
-    for ref in (x_ref, first_ref, second_ref, block_ref, d_ref, dt_ref, ds_ref):
-        ref[...] = jnp.zeros_like(ref)
+    for ref in (x_ref, first_ref, second_ref, block_ref, d_ref, dt_ref, ds_ref, p_ref):
+        ref[:, : 2 * MARGIN] = jnp.zeros((ref.shape[0], 2 * MARGIN), ref.dtype)
+        ref[:, RIGHT:] = jnp.zeros((ref.shape[0], WIDTH - RIGHT), ref.dtype)
     for ref in (gclass_ref, gred_ref, gspat_ref, gexp_ref, facc_ref, cacc_ref):
         ref[...] = jnp.zeros_like(ref)
     for r in range(FULL):
@@ -135,31 +162,39 @@
             turned = pltpu.roll(edge_ref[:, source], (at - spot) % 128, 1)
             put(x_ref, BOTH, at // 128, turned, at % 128, at % 128 + HALO)
 
-    def first_step(lane):
-        x = x_ref[:C, pl.ds(lane, CHUNK)]
-        first_ref[:, pl.ds(lane, CHUNK)] = jnp.maximum(dot(wr_ref[...], x), 0.0).astype(BF)
-
-    chunks(0, 11, first_step)
-
-    def block_step(lane):
-        here = pl.ds(lane, CHUNK)
-        stack = jnp.concatenate([window(first_ref, slice(None), lane, s) for s in TAPS], axis=0)
-        second = jnp.maximum(dot(w2_ref[...], stack), 0.0)
+    def first_step(lane, n):
+        x = x_ref[:C, pl.ds(lane, n)]
+        first_ref[:, pl.ds(lane, n)] = jnp.maximum(dot(wr_ref[...], x), 0.0).astype(BF)
+
+    chunks(*SPLIT[0], first_step)
+
+    def spatial_step(lane, n):
+        p_ref[: 3 * MID, pl.ds(lane, n)] = dot(w2_ref[...], across(first_ref, lane, 1, n))
+
+    chunks(*SPLIT[1], spatial_step)
+
+    def block_step(lane, n):
+        here = pl.ds(lane, n)
+        second = jnp.maximum(down(p_ref, lane, 1, MID, n), 0.0)
         inside = x_ref[ONE0 - 2 : ONE0 + 14, here].astype(F32)[2:3]
         second = jnp.where(inside > 0.5, second, 0.0).astype(BF)
         second_ref[:, here] = second
         total = x_ref[:C, here].astype(F32) + dot(we_ref[...], second)
         block_ref[:, here] = jnp.maximum(total, 0.0).astype(BF)
 
-    chunks(128, 11, block_step)
+    chunks(*SPLIT[2], block_step)
+
+    def class_step(lane, n):
+        p_ref[:, pl.ds(lane, n)] = dot(w3_ref[...], across(block_ref, lane, 1, n))
+
+    chunks(*SPLIT[3], class_step)
 
     channel = lax.broadcasted_iota(jnp.int32, (136, 1), 0)
     wanted = (channel - 15 * ((channel * 4370) >> 16) + 17).astype(F32)
 
-    def logit_step(lane):
-        here = pl.ds(lane, CHUNK)
-        stack = jnp.concatenate([window(block_ref, slice(None), lane, s) for s in TAPS], axis=0)
-        z = dot(w3_ref[...], stack)
+    def focal_step(lane, n):
+        here = pl.ds(lane, n)
+        z = down(p_ref, lane, 1, 136, n)
         tags = x_ref[C:CHANNELS, here]
         code = dot(e_ref[...], tags)
         target = code == wanted
@@ -178,22 +213,22 @@
         grad = jnp.where(target, grad, -grad)
         d_ref[:, here] = grad[:128].astype(BF)
         dt_ref[:, here] = grad[128:].astype(BF).astype(F32)
-        inner = interior(lane, 0)
+        inner = interior(lane, 0, n)
         focal = jnp.where(inner, ap2 * ls, 0.0)
-        facc_ref[...] -= jnp.sum(focal.reshape(17, 8, CHUNK), axis=0)
+        facc_ref[...] -= jnp.sum(focal.reshape(17, 8, n), axis=0)
         labels = tags[:16].astype(F32)
-        tag = lax.broadcasted_iota(jnp.int32, (16, CHUNK), 0)
+        tag = lax.broadcasted_iota(jnp.int32, (16, n), 0)
         positives = jnp.where((labels > 0.5) & (tag < A) & inner, 1.0, 0.0)
         cacc_ref[...] += positives[:8] + positives[8:]
 
-    chunks(256, 10, logit_step)
-
-    def class_step(lane):
-        here = pl.ds(lane, CHUNK)
-        mains = [window(d_ref, slice(None), lane, -s) for s in TAPS]
-        tails = [window(dt_ref, slice(None), lane, -s) for s in TAPS]
-        inner = [interior(lane, -s) for s in TAPS]
-        spare = jnp.zeros((8, CHUNK), F32)
+    chunks(*SPLIT[4], focal_step)
+
+    def class_back(lane, n):
+        here = pl.ds(lane, n)
+        mains = [window(d_ref, slice(None), lane, -s, n) for s in TAPS]
+        tails = [window(dt_ref, slice(None), lane, -s, n) for s in TAPS]
+        inner = [interior(lane, -s, n) for s in TAPS]
+        spare = jnp.zeros((8, n), F32)
         block = block_ref[:, here]
         stack = jnp.concatenate(
             mains + [jnp.concatenate(tails + [spare], axis=0).astype(BF)], axis=0
@@ -201,12 +236,12 @@
         dblock = dot(w3t_ref[...], stack)
         dsum = jnp.where(block.astype(F32) > 0, dblock, 0.0).astype(BF)
         second = second_ref[:, here]
-        within = interior(lane, 0)
-        second32 = second.astype(F32)
-        gexp_ref[...] += dot_nt(dsum, jnp.where(within, second32, 0.0).astype(BF))
-        ds_ref[:, here] = jnp.where(second32 > 0, dot(wet_ref[...], dsum), 0.0).astype(BF)
+        within = interior(lane, 0, n)
+        gexp_ref[...] += dot_nt(masked(second, within), dsum)
+        dsecond = jnp.where(second.astype(F32) > 0, dot(wet_ref[...], dsum), 0.0)
+        ds_ref[:, here] = dsecond.astype(BF)
         own = jnp.concatenate(
-            [m * jnp.where(i, 1.0, 0.0).astype(BF) for m, i in zip(mains, inner)]
+            [masked(m, i) for m, i in zip(mains, inner)]
             + [
                 jnp.concatenate(
                     [jnp.where(i, t, 0.0) for t, i in zip(tails, inner)] + [spare], axis=0
@@ -216,32 +251,45 @@
         )
         gclass_ref[...] += dot_nt(own, block)
 
-    chunks(384, 10, class_step)
-
-    def first_back(lane):
-        here = pl.ds(lane, CHUNK)
-        parts = [window(ds_ref, slice(None), lane, -s) for s in TAPS]
-        inner = [interior(lane, -s) for s in TAPS]
-        first = first_ref[:, here]
+    chunks(*SPLIT[5], class_back)
+
+    def spatial_back(lane, n):
+        stack = across(ds_ref, lane, -1, n)
+        p_ref[: 3 * MID, pl.ds(lane, n)] = dot(w2t_ref[...], stack)
         own = jnp.concatenate(
-            [m * jnp.where(i, 1.0, 0.0).astype(BF) for m, i in zip(parts, inner)], axis=0
+            [
+                masked(stack[k * MID : k * MID + MID], interior(lane, 1 - k, n))
+                for k in range(3)
+            ],
+            axis=0,
+        )
+        first = jnp.concatenate(
+            [window(first_ref, slice(None), lane, k * STRIDE, n) for k in (-1, 0, 1)], axis=0
         )
         gspat_ref[...] += dot_nt(own, first)
-        dfirst = dot(w2t_ref[...], jnp.concatenate(parts, axis=0))
-        keep = (first.astype(F32) > 0) & interior(lane, 0)
+
+    chunks(*SPLIT[6], spatial_back)
+
+    def first_back(lane, n):
+        here = pl.ds(lane, n)
+        dfirst = down(p_ref, lane, -1, MID, n)
+        keep = (first_ref[:, here].astype(F32) > 0) & interior(lane, 0, n)
         dfirst = jnp.where(keep, dfirst, 0.0).astype(BF)
         gred_ref[...] += dot_nt(dfirst, x_ref[:C, here])
 
-    chunks(384, 10, first_back)
+    chunks(*SPLIT[7], first_back)
 
     out_ref[:STACK] = gclass_ref[:, :128].astype(BF)
     out_ref[STACK:RED0] = gclass_ref[:, 128:].astype(BF)
     out_ref[RED0 : RED0 + MID] = gred_ref[:, :128].astype(BF)
     out_ref[RED0 + MID : SPAT0] = gred_ref[:, 128:].astype(BF)
-    half = 9 * MID // 2
-    out_ref[SPAT0:EXP0] = jnp.concatenate([gspat_ref[:half], gspat_ref[half:]], axis=1).astype(BF)
-    half = C // 2
-    out_ref[EXP0:STAT0] = jnp.concatenate([gexp_ref[:half], gexp_ref[half:]], axis=1).astype(BF)
+    out_ref[SPAT0 : SPAT0 + 3 * MID] = gspat_ref[:, : 2 * MID].astype(BF)
+    half = 3 * MID // 2
+    out_ref[SPAT0 + 3 * MID : EXP0] = jnp.concatenate(
+        [gspat_ref[:half, 2 * MID :], gspat_ref[half:, 2 * MID :]], axis=1
+    ).astype(BF)
+    out_ref[EXP0 : EXP0 + MID] = gexp_ref[:, :128].astype(BF)
+    out_ref[EXP0 + MID : STAT0] = gexp_ref[:, 128:].astype(BF)
     out_ref[STAT0:] = jnp.zeros((DEVICES * SHARE - STAT0, 128), BF)
     focal = jnp.sum(facc_ref[...], keepdims=True)
     count = jnp.sum(cacc_ref[...], keepdims=True)
@@ -300,12 +348,17 @@
             gclass_ref[t, :128, lanes] = rows(half * STACK + t * 128, 128)
             gclass_ref[t, 128:, lanes] = tails[t * TAIL : t * TAIL + 7]
         gred_ref[:, lanes] = rows(RED0 + half * MID, MID)
-    spat = rows(SPAT0, 9 * MID // 2)
-    gspat_ref[: 9 * MID // 2] = spat[:, :MID]
-    gspat_ref[9 * MID // 2 :] = spat[:, MID:]
-    expand = rows(EXP0, C // 2)
-    gexp_ref[: C // 2] = expand[:, :MID]
-    gexp_ref[C // 2 :] = expand[:, MID:]
+        gexp_ref[:, lanes] = rows(EXP0 + half * MID, MID)
+    spat = rows(SPAT0, 3 * MID)
+    last = rows(SPAT0 + 3 * MID, 3 * MID // 2)
+    half = 3 * MID // 2
+    for dx in range(3):
+        for dy in range(2):
+            gspat_ref[3 * dy + dx] = spat[dx * MID : dx * MID + MID, dy * MID : dy * MID + MID]
+    gspat_ref[6] = last[:MID, :MID]
+    gspat_ref[7, : half - MID] = last[MID:, :MID]
+    gspat_ref[7, half - MID :] = last[: 2 * MID - half, MID:]
+    gspat_ref[8] = last[2 * MID - half :, MID:]
 
 
 def per_device(
@@ -339,10 +392,10 @@
     left = lax.ppermute(right_edge, "col", ahead)
     right = lax.ppermute(left_edge, "col", back)
 
-    w2 = jnp.transpose(spatial_weight, (2, 0, 1, 3)).reshape(MID, 9 * MID)
-    w2t = jnp.transpose(spatial_weight, (3, 0, 1, 2)).reshape(MID, 9 * MID)
-    w3 = jnp.transpose(class_weight, (2, 0, 1, 3)).reshape(OUT, 9 * C)
-    w3 = jnp.pad(w3, ((0, 136 - OUT), (0, 0)))
+    w2 = jnp.transpose(spatial_weight, (0, 2, 1, 3)).reshape(3 * MID, 3 * MID)
+    w2t = jnp.transpose(spatial_weight, (0, 3, 1, 2)).reshape(3 * MID, 3 * MID)
+    w3 = jnp.pad(class_weight, ((0, 0), (0, 0), (0, 136 - OUT), (0, 0)))
+    w3 = jnp.transpose(w3, (0, 2, 1, 3)).reshape(3 * 136, 3 * C)
     w9 = class_weight.reshape(9, OUT, C)
     w3t = jnp.concatenate(
         [
@@ -370,12 +423,13 @@
             pltpu.VMEM((128, WIDTH), BF),
             pltpu.VMEM((TAIL, WIDTH), F32),
             pltpu.VMEM((MID, WIDTH), BF),
-            pltpu.VMEM((8, CHUNK), F32),
-            pltpu.VMEM((8, CHUNK), F32),
+            pltpu.VMEM((3 * 136, WIDTH), F32),
+            pltpu.VMEM((8, SPLIT[4][1]), F32),
+            pltpu.VMEM((8, SPLIT[4][1]), F32),
             pltpu.VMEM((STACK, C), F32),
             pltpu.VMEM((MID, C), F32),
-            pltpu.VMEM((9 * MID, MID), F32),
-            pltpu.VMEM((C, MID), F32),
+            pltpu.VMEM((3 * MID, 3 * MID), F32),
+            pltpu.VMEM((MID, C), F32),
         ],
         compiler_params=params,
     )(
@@ -401,8 +455,8 @@
         out_shape=(
             shape((1, 1), F32),
             shape((MID, C), F32),
-            shape((9 * MID, MID), F32),
-            shape((C, MID), F32),
+            shape((9, MID, MID), F32),
+            shape((MID, C), F32),
             shape((9, OUT, C), F32),
         ),
         compiler_params=params,
@@ -411,7 +465,7 @@
         loss.reshape(()),
         gred,
         gspat.reshape(3, 3, MID, MID),
-        gexp,
+        gexp.T,
         gclass.reshape(3, 3, OUT, C),
     )
 

time: 140 us -> 120 us (0.86)
  Pallas kernels: 58.1 us -> 40.8 us
  local copies, waits for them, and re-layouts: 12.3 us -> 10.5 us
    pallas_call x1, Pallas kernels: 47.6 us -> 30.3 us  [per_device(): pl.pallas_call(main_kernel, out_shape=shape((DEVICES * SHARE, 128), BF),...]
where the time goes in v2:
time: 120 us
  Pallas kernels  40.8 us (34%)
  starting transfers between devices  22.7 us (19%)
  blocking collectives  21.9 us (18%)
  waiting for transfers between devices  20.9 us (17%)
  local copies, waits for them, and re-layouts  10.5 us (9%)
  other arithmetic  2.17 us (2%)
    pallas_call x1, Pallas kernels, per_device(): pl.pallas_call(main_kernel, out_shape=shape((DEVICES * SHARE, 128), BF),...  30.3 us
    all_to_all x1, blocking collectives, per_device(): lax.all_to_all(copies, ALL, 0, 0, tiled=True).reshape(DEVICES * SHARE, 128)  21.9 us
    all_to_all x1, waiting for transfers between devices, per_device(): came = lax.all_to_all(sent, ALL, 0, 0, tiled=True)  16.8 us
    all_to_all x1, starting transfers between devices, per_device(): came = lax.all_to_all(sent, ALL, 0, 0, tiled=True)  12.5 us
    unnamed x21, local copies, waits for them, and re-layouts  6.4 us
    ppermute x1, starting transfers between devices, per_device(): top = lax.ppermute(edge_rows(ROWS - HALO), 'row', ahead)  4.52 us
    ppermute x1, waiting for transfers between devices, per_device(): bottom = lax.ppermute(edge_rows(0), 'row', back)  4.14 us
    pallas_call x1, Pallas kernels, per_device(): pl.pallas_call(edges_kernel, out_shape=(pack, pack), compiler_params=params)  3.52 us
  transfers between devices with their start and end apart: 5, of which 2 were waited for; matrix products, arithmetic and copies ran while one was open for 5% of the time, Pallas kernels for 3%

profile of v2, /device:TPU:1, one launch (start us, length us, event | category | flops | bytes accessed | tf_op | source)
XLA Modules:
  0.0 119.8 jit_solution(13182567565119053115)
XLA Ops:
  0.8 1.2 fusion
  2.1 2.4 %copy.44 = bf16[1,256,32,128]{3,1,2,0:T(8,128)(2,1)S(1)} copy(bf16[1,256,32,128]{3,2,1,0:T(8,128)(2,1)} %param.8) | data formatting | bytes 4194304 | tf_op args[0]
  4.6 4.5 %collective-permute-start = (bf16[4,288,128]{2,1,0:T(8,128)(2,1)S(1)}, bf16[4,288,128]{2,1,0:T(8,128)(2,1)S(1)}, u32[]{:S(2)}, u32[]{:S(2)}) collective-permute-start(bf16[4,288,128]{2,1,0:T(8,128)(2,1)S(1)} %maximum_bitcast_fusion), channel_id=1, source_target_pairs={{0,4},{4,8},{8,12},{1,5},{5,9},{9,13},{2,6},{6,10},{10,14},{3,7},{... | collective-permute-start | bytes 884744 | tf_op jit(solution)/shard_map/ppermute | solution.py:379
  9.2 1.3 %collective-permute-start.1 = (bf16[4,288,128]{2,1,0:T(8,128)(2,1)S(1)}, bf16[4,288,128]{2,1,0:T(8,128)(2,1)S(1)}, u32[]{:S(2)}, u32[]{:S(2)}) collective-permute-start(bf16[4,288,128]{2,1,0:T(8,128)(2,1)S(1)} %maximum_bitcast_fusion.1), channel_id=1, source_target_pairs={{4,0},{8,4},{12,8},{5,1},{9,5},{13,9},{6,2},{10,6},{14,10},{7,3},{... | collective-permute-start | bytes 884744 | tf_op jit(solution)/shard_map/ppermute | solution.py:380
  10.5 0.8 fusion.4.tags_ref
  11.3 3.5 %shard_map.119 = (bf16[288,128]{1,0:T(8,128)(2,1)}, bf16[288,128]{1,0:T(8,128)(2,1)}) custom-call(bf16[32,256,128]{2,1,0:T(8,128)(2,1)} %bitcast.39, bf16[32,32,128]{2,1,0:T(8,128)(2,1)} %fusion.4.tags_ref), custom_call_target="tpu_custom_call" | custom-call | tf_op jit(solution)/shard_map/pallas_call | solution.py:385
  14.9 4.1 %collective-permute-done.1.bottom_ref = bf16[4,288,128]{2,1,0:T(8,128)(2,1)S(1)} collective-permute-done((bf16[4,288,128]{2,1,0:T(8,128)(2,1)S(1)}, bf16[4,288,128]{2,1,0:T(8,128)(2,1)S(1)}, u32[]{:S(2)}, u32[]{:S(2)}) %collective-permute-start.1) | collective-permute-done | bytes 294944 | tf_op jit(solution)/shard_map/ppermute | solution.py:380
  19.0 0.7 copy-done.4
  19.7 2.2 %shard_map.120 = (bf16[288,256]{1,0:T(8,128)(2,1)}, bf16[288,256]{1,0:T(8,128)(2,1)}) custom-call(bf16[288,128]{1,0:T(8,128)(2,1)} %get-tuple-element.14.left_ref, bf16[288,128]{1,0:T(8,128)(2,1)} %get-tuple-element.15.right_ref, bf16[4,288,128]{2,1,0:T(8,128)(2,1)} %copy-done.3, bf16[4,288,128]{2,1,0:T(8,128)(2,1)} %copy-done.4), custom_call_target="tpu_custom_call" | custom-call | tf_op jit(solution)/shard_map/pallas_call | solution.py:389
  21.9 3.1 %collective-permute-start.2 = (bf16[288,256]{1,0:T(8,128)(2,1)}, bf16[288,256]{1,0:T(8,128)(2,1)S(1)}, u32[]{:S(2)}, u32[]{:S(2)}) collective-permute-start(bf16[288,256]{1,0:T(8,128)(2,1)} %get-tuple-element.16), channel_id=1, source_target_pairs={{0,1},{1,2},{2,3},{4,5},{5,6},{6,7},{8,9},{9,10},{10,11},{12,13},{... | collective-permute-start | bytes 442376 | tf_op jit(solution)/shard_map/ppermute | solution.py:392
  25.0 1.3 %collective-permute-start.3 = (bf16[288,256]{1,0:T(8,128)(2,1)}, bf16[288,256]{1,0:T(8,128)(2,1)S(1)}, u32[]{:S(2)}, u32[]{:S(2)}) collective-permute-start(bf16[288,256]{1,0:T(8,128)(2,1)} %get-tuple-element.17), channel_id=1, source_target_pairs={{1,0},{2,1},{3,2},{5,4},{6,5},{7,6},{9,8},{10,9},{11,10},{13,12},{... | collective-permute-start | bytes 442376 | tf_op jit(solution)/shard_map/ppermute | solution.py:393
  27.2 1.0 copy.35
  28.3 0.8 reshape.49.w2_ref
  29.2 0.8 reshape.50.w2t_ref
  30.1 0.7 copy.34.we_ref
  30.8 1.2 concatenate.15
  32.0 0.6 copy-done.6
  32.7 30.3 %shard_map.121 = bf16[3072,128]{1,0:T(8,128)(2,1)} custom-call(bf16[32,256,128]{2,1,0:T(8,128)(2,1)} %bitcast.40, bf16[32,32,128]{2,1,0:T(8,128)(2,1)} %fusion.4.tags_ref, bf16[4,288,128]{2,1,0:T(8,128)(2,1)} %copy-done.3, bf16[4,288,128]{2,1,0:T(8,128)(2,1)} %copy-done.4, bf16[288,256]{1,0:T(8,128)(2,1)} %copy-done.6, bf16[288,256]{1,0:T(8,128)(2,1)} %copy-done.7, ...), custom_call_target="tpu_custom_call" | custom-call | tf_op jit(solution)/shard_map/pallas_call | solution.py:415
  63.1 12.5 %all-to-all-start = ((bf16[128,24,128]{2,1,0:T(8,128)(2,1)}), bf16[128,24,128]{2,1,0:T(8,128)(2,1)S(1)}, u32[]{:S(2)}, u32[]{:S(2)}) async-start(bf16[128,24,128]{2,1,0:T(8,128)(2,1)} %bitcast.43), calls=%async_computation | async-start | bytes 1572864 | tf_op jit(solution)/shard_map/all_to_all | solution.py:441
  75.5 16.8 %all-to-all-done.came_ref = bf16[128,24,128]{2,1,0:T(8,128)(2,1)S(1)} async-done(((bf16[128,24,128]{2,1,0:T(8,128)(2,1)}), bf16[128,24,128]{2,1,0:T(8,128)(2,1)S(1)}, u32[]{:S(2)}, u32[]{:S(2)}) %all-to-all-start) | async-done | bytes 786464 | tf_op jit(solution)/shard_map/all_to_all | solution.py:441
  92.3 0.9 copy-done.1
  93.2 2.3 %shard_map.122 = bf16[128,24,128]{2,1,0:T(8,128)(2,1)} custom-call(s32[1]{0:T(128)} %bitcast.index_ref, bf16[128,24,128]{2,1,0:T(8,128)(2,1)} %copy-done.1), custom_call_target="tpu_custom_call" | custom-call | tf_op jit(solution)/shard_map/pallas_call | solution.py:443
  95.5 21.9 %all_to_all.10 = bf16[128,24,128]{2,1,0:T(8,128)(2,1)} all-to-all(bf16[128,24,128]{2,1,0:T(8,128)(2,1)} %shard_map.122), channel_id=1, replica_groups=mesh['dp'=8,'row'=4,'col'=4] {'dp','row','col'}, dimensions={0} | all-to-all | bytes 1572864 | tf_op jit(solution)/shard_map/all_to_all | solution.py:452
  117.4 2.5 %shard_map.123 = (f32[1,1]{1,0:T(1,128)}, f32[64,256]{1,0:T(8,128)}, f32[9,64,64]{2,1,0:T(8,128)}, f32[64,256]{1,0:T(8,128)}, f32[9,135,256]{2,1,0:T(8,128)}) custom-call(bf16[3072,128]{1,0:T(8,128)(2,1)} %bitcast.42), custom_call_target="tpu_custom_call" | custom-call | tf_op jit(solution)/shard_map/pallas_call | solution.py:453
  (36 shorter events, 1.6 us)
Async XLA Ops:
  4.5 6.8 %copy-start = (bf16[1,256,32,128]{3,1,2,0:T(8,128)(2,1)}, bf16[1,256,32,128]{3,1,2,0:T(8,128)(2,1)S(1)}, u32[]{:S(2)}) copy-start(bf16[1,256,32,128]{3,1,2,0:T(8,128)(2,1)S(1)} %copy.44) | copy-start | bytes 6291460
  4.5 5.9 %copy-start.2 = (bf16[3,3,135,256]{3,2,1,0:T(8,128)(2,1)S(1)}, bf16[3,3,135,256]{3,2,1,0:T(8,128)(2,1)}, u32[]{:S(2)}) copy-start(bf16[3,3,135,256]{3,2,1,0:T(8,128)(2,1)} %param.12) | copy-start | bytes 1866244
  4.6 10.2 %collective-permute-start = (bf16[4,288,128]{2,1,0:T(8,128)(2,1)S(1)}, bf16[4,288,128]{2,1,0:T(8,128)(2,1)S(1)}, u32[]{:S(2)}, u32[]{:S(2)}) collective-permute-start(bf16[4,288,128]{2,1,0:T(8,128)(2,1)S(1)} %maximum_bitcast_fusion), channel_id=1, source_target_pairs={{0,4},{4,8},{8,12},{1,5},{5,9},{9,13},{2,6},{6,10},{10,14},{3,7},{... | collective-permute-start | bytes 884744 | tf_op jit(solution)/shard_map/ppermute | solution.py:379
  9.2 9.8 %collective-permute-start.1 = (bf16[4,288,128]{2,1,0:T(8,128)(2,1)S(1)}, bf16[4,288,128]{2,1,0:T(8,128)(2,1)S(1)}, u32[]{:S(2)}, u32[]{:S(2)}) collective-permute-start(bf16[4,288,128]{2,1,0:T(8,128)(2,1)S(1)} %maximum_bitcast_fusion.1), channel_id=1, source_target_pairs={{4,0},{8,4},{12,8},{5,1},{9,5},{13,9},{6,2},{10,6},{14,10},{7,3},{... | collective-permute-start | bytes 884744 | tf_op jit(solution)/shard_map/ppermute | solution.py:380
  14.8 4.1 %copy-start.3 = (bf16[4,288,128]{2,1,0:T(8,128)(2,1)}, bf16[4,288,128]{2,1,0:T(8,128)(2,1)S(1)}, u32[]{:S(2)}) copy-start(bf16[4,288,128]{2,1,0:T(8,128)(2,1)S(1)} %collective-permute-done.top_ref) | copy-start | bytes 884740
  19.0 0.7 copy-start.4
  21.9 10.1 %collective-permute-start.2 = (bf16[288,256]{1,0:T(8,128)(2,1)}, bf16[288,256]{1,0:T(8,128)(2,1)S(1)}, u32[]{:S(2)}, u32[]{:S(2)}) collective-permute-start(bf16[288,256]{1,0:T(8,128)(2,1)} %get-tuple-element.16), channel_id=1, source_target_pairs={{0,1},{1,2},{2,3},{4,5},{5,6},{6,7},{8,9},{9,10},{10,11},{12,13},{... | collective-permute-start | bytes 442376 | tf_op jit(solution)/shard_map/ppermute | solution.py:392
  25.0 7.0 %collective-permute-start.3 = (bf16[288,256]{1,0:T(8,128)(2,1)}, bf16[288,256]{1,0:T(8,128)(2,1)S(1)}, u32[]{:S(2)}, u32[]{:S(2)}) collective-permute-start(bf16[288,256]{1,0:T(8,128)(2,1)} %get-tuple-element.17), channel_id=1, source_target_pairs={{1,0},{2,1},{3,2},{5,4},{6,5},{7,6},{9,8},{10,9},{11,10},{13,12},{... | collective-permute-start | bytes 442376 | tf_op jit(solution)/shard_map/ppermute | solution.py:393
  26.8 1.4 %copy-start.5 = (bf16[3,3,64,64]{3,2,1,0:T(8,128)(2,1)S(1)}, bf16[3,3,64,64]{3,2,1,0:T(8,128)(2,1)}, u32[]{:S(2)}) copy-start(bf16[3,3,64,64]{3,2,1,0:T(8,128)(2,1)} %param.10) | copy-start | bytes 221188
  26.8 3.2 %copy-start.8 = (bf16[256,64]{0,1:T(8,128)(2,1)S(1)}, bf16[256,64]{0,1:T(8,128)(2,1)}, u32[]{:S(2)}) copy-start(bf16[256,64]{0,1:T(8,128)(2,1)} %param.11) | copy-start | bytes 98308
  32.0 0.6 copy-start.6
  32.0 0.7 copy-start.7
  63.1 29.2 %all-to-all-start = ((bf16[128,24,128]{2,1,0:T(8,128)(2,1)}), bf16[128,24,128]{2,1,0:T(8,128)(2,1)S(1)}, u32[]{:S(2)}, u32[]{:S(2)}) async-start(bf16[128,24,128]{2,1,0:T(8,128)(2,1)} %bitcast.43), calls=%async_computation | async-start | bytes 1572864 | tf_op jit(solution)/shard_map/all_to_all | solution.py:441
  92.3 0.9 copy-start.1

commit v3 on v2

--- a/solution.py
+++ b/solution.py
@@ -18,14 +18,15 @@
 STRIDE = COLS + 2 * HALO
 CHANNELS = 288
 MARGIN = 256
-WIDTH = 6400
+WIDTH = 6656
 RIGHT = MARGIN + 5120
+PIPE = 640
 SPLIT = (
     (0, 2816, 2),
     (0, 2816, 2),
     (128, 2688, 2),
-    (0, 2816, 2),
-    (256, 1024, 5),
+    (0, PIPE, 9),
+    (256, PIPE, 8),
     (384, 2432, 2),
     (384, 2432, 2),
     (512, 2304, 2),
@@ -59,7 +60,16 @@
 BOTH = slice(0, CHANNELS)
 
 
-def edges_kernel(maps_ref, tags_ref, left_ref, right_ref):
+def place(ref, rows, source, r):
+    at = MARGIN + r * STRIDE + HALO
+    turn, tile = (at % 128, at // 128)
+    turned = pltpu.roll(source, turn, 1)
+    put(ref, rows, tile, turned, turn, 128)
+    put(ref, rows, tile + 1, turned, 0, turn)
+
+
+def edges_kernel(maps_ref, tags_ref, left_ref, right_ref, x_ref):
+    x_ref[...] = jnp.zeros_like(x_ref)
     left_ref[...] = jnp.zeros_like(left_ref)
     right_ref[...] = jnp.zeros_like(right_ref)
     for r in range(ROWS):
@@ -67,6 +77,7 @@
         for rows, source in ((BODY, maps_ref[r]), (REST, tags_ref[r])):
             put(left_ref, rows, 0, pltpu.roll(source, at, 1), at, at + HALO)
             put(right_ref, rows, 0, pltpu.roll(source, (at + HALO) % 128, 1), at, at + HALO)
+            place(x_ref, rows, source, r + HALO)
 
 
 def corners_kernel(left_ref, right_ref, top_ref, bottom_ref, wide_left_ref, wide_right_ref):
@@ -80,12 +91,16 @@
         put(wide_right_ref, BOTH, 1, pltpu.roll(source, at + HALO, 1), at, at + HALO)
 
 
+def aligned(lane):
+    return lane if isinstance(lane, int) else pl.multiple_of(lane, 128)
+
+
 def window(ref, rows, lane, shift, n):
     base = (shift // 128) * 128
     turn = shift - base
     if turn == 0:
-        return ref[rows, pl.ds(pl.multiple_of(lane + base, 128), n)]
-    wide = ref[rows, pl.ds(pl.multiple_of(lane + base, 128), n + 128)]
+        return ref[rows, pl.ds(aligned(lane + base), n)]
+    wide = ref[rows, pl.ds(aligned(lane + base), n + 128)]
     return pltpu.roll(wide, n + 128 - turn, 1)[:, :n]
 
 
@@ -129,30 +144,25 @@
 
 
 def main_kernel(
-    maps_ref, tags_ref, top_ref, bottom_ref, left_ref, right_ref,
+    x0_ref, top_ref, bottom_ref, left_ref, right_ref,
     wr_ref, w2_ref, w2t_ref, we_ref, wet_ref, w3_ref, w3t_ref, e_ref,
     out_ref,
     x_ref, first_ref, second_ref, block_ref, d_ref, dt_ref, ds_ref, p_ref, facc_ref, cacc_ref,
-    gclass_ref, gred_ref, gspat_ref, gexp_ref,
+    gclass_ref, gred_ref, gspat_ref, gexp_ref, sem,
 ):
-    for ref in (x_ref, first_ref, second_ref, block_ref, d_ref, dt_ref, ds_ref, p_ref):
+    copy = pltpu.make_async_copy(x0_ref, x_ref, sem)
+    copy.start()
+    for ref in (first_ref, second_ref, block_ref, d_ref, dt_ref, ds_ref, p_ref):
         ref[:, : 2 * MARGIN] = jnp.zeros((ref.shape[0], 2 * MARGIN), ref.dtype)
         ref[:, RIGHT:] = jnp.zeros((ref.shape[0], WIDTH - RIGHT), ref.dtype)
     for ref in (gclass_ref, gred_ref, gspat_ref, gexp_ref, facc_ref, cacc_ref):
         ref[...] = jnp.zeros_like(ref)
+    copy.wait()
     for r in range(FULL):
         if r < HALO:
-            sources = ((BOTH, top_ref[r]),)
-        elif r < HALO + ROWS:
-            sources = ((BODY, maps_ref[r - HALO]), (REST, tags_ref[r - HALO]))
-        else:
-            sources = ((BOTH, bottom_ref[r - HALO - ROWS]),)
-        at = MARGIN + r * STRIDE + HALO
-        turn, tile = (at % 128, at // 128)
-        for rows, source in sources:
-            turned = pltpu.roll(source, turn, 1)
-            put(x_ref, rows, tile, turned, turn, 128)
-            put(x_ref, rows, tile + 1, turned, 0, turn)
+            place(x_ref, BOTH, top_ref[r], r)
+        elif r >= HALO + ROWS:
+            place(x_ref, BOTH, bottom_ref[r - HALO - ROWS], r)
         if HALO <= r < HALO + ROWS:
             spot = HALO * (r - HALO)
         else:
@@ -186,8 +196,6 @@
 
     def class_step(lane, n):
         p_ref[:, pl.ds(lane, n)] = dot(w3_ref[...], across(block_ref, lane, 1, n))
-
-    chunks(*SPLIT[3], class_step)
 
     channel = lax.broadcasted_iota(jnp.int32, (136, 1), 0)
     wanted = (channel - 15 * ((channel * 4370) >> 16) + 17).astype(F32)
@@ -221,7 +229,13 @@
         positives = jnp.where((labels > 0.5) & (tag < A) & inner, 1.0, 0.0)
         cacc_ref[...] += positives[:8] + positives[8:]
 
-    chunks(*SPLIT[4], focal_step)
+    begin, n, count = SPLIT[3]
+    for j in range(count + 2):
+        if j >= 2 and j - 2 < SPLIT[4][2]:
+            for k in range(0, n, 128):
+                focal_step(MARGIN + SPLIT[4][0] + (j - 2) * n + k, 128)
+        if j < count:
+            class_step(MARGIN + begin + j * n, n)
 
     def class_back(lane, n):
         here = pl.ds(lane, n)
@@ -382,8 +396,9 @@
     tags = jnp.transpose(tags, (1, 0, 2))
     params = pltpu.CompilerParams(vmem_limit_bytes=56 << 20)
     pack = jax.ShapeDtypeStruct((CHANNELS, 128), BF)
-    left_edge, right_edge = pl.pallas_call(
-        edges_kernel, out_shape=(pack, pack), compiler_params=params
+    start = jax.ShapeDtypeStruct((CHANNELS, WIDTH), BF)
+    left_edge, right_edge, start = pl.pallas_call(
+        edges_kernel, out_shape=(pack, pack, start), compiler_params=params
     )(maps, tags)
     pack = jax.ShapeDtypeStruct((CHANNELS, 256), BF)
     left_edge, right_edge = pl.pallas_call(
@@ -415,6 +430,7 @@
     out = pl.pallas_call(
         main_kernel,
         out_shape=shape((DEVICES * SHARE, 128), BF),
+        in_specs=[pl.BlockSpec(memory_space=pl.ANY)] + [pl.BlockSpec(memory_space=pltpu.VMEM)] * 12,
         scratch_shapes=[
             pltpu.VMEM((CHANNELS, WIDTH), BF),
             pltpu.VMEM((MID, WIDTH), BF),
@@ -424,16 +440,17 @@
             pltpu.VMEM((TAIL, WIDTH), F32),
             pltpu.VMEM((MID, WIDTH), BF),
             pltpu.VMEM((3 * 136, WIDTH), F32),
-            pltpu.VMEM((8, SPLIT[4][1]), F32),
-            pltpu.VMEM((8, SPLIT[4][1]), F32),
+            pltpu.VMEM((8, 128), F32),
+            pltpu.VMEM((8, 128), F32),
             pltpu.VMEM((STACK, C), F32),
             pltpu.VMEM((MID, C), F32),
             pltpu.VMEM((3 * MID, 3 * MID), F32),
             pltpu.VMEM((MID, C), F32),
+            pltpu.SemaphoreType.DMA(()),
         ],
         compiler_params=params,
     )(
-        maps, tags, top, bottom, left, right,
+        start, top, bottom, left, right,
         reduce_weight, w2, w2t, expand_weight, expand_weight.T, w3, w3t, spread,
     )
 

time: 120 us -> 119 us (level)
  waiting for transfers between devices: 20.9 us -> 18.9 us
    ppermute x1, waiting for transfers between devices: 4.14 us -> 2.08 us  [per_device(): bottom = lax.ppermute(edge_rows(0), 'row', back)]
    pallas_call x1, Pallas kernels: 3.52 us -> 5.56 us  [per_device(): pl.pallas_call(edges_kernel, out_shape=(pack, pack, start), compiler_para...]
    pallas_call x1, Pallas kernels: 30.3 us -> 29 us  [per_device(): pl.pallas_call(main_kernel, out_shape=shape((DEVICES * SHARE, 128), BF),...]
  transfers between devices with their start and end apart: 5 -> 5, of which waited for: 2 -> 2; matrix products, arithmetic and copies ran while one was open for 5% -> 5% of each run, Pallas kernels for 3% -> 5%
where the time goes in v3:
time: 119 us
  Pallas kernels  41.5 us (35%)
  starting transfers between devices  22.7 us (19%)
  blocking collectives  21.9 us (18%)
  waiting for transfers between devices  18.9 us (16%)
  local copies, waits for them, and re-layouts  10.6 us (9%)
  other arithmetic  2.18 us (2%)
    pallas_call x1, Pallas kernels, per_device(): pl.pallas_call(main_kernel, out_shape=shape((DEVICES * SHARE, 128), BF),...  29 us
    all_to_all x1, blocking collectives, per_device(): lax.all_to_all(copies, ALL, 0, 0, tiled=True).reshape(DEVICES * SHARE, 128)  21.9 us
    all_to_all x1, waiting for transfers between devices, per_device(): came = lax.all_to_all(sent, ALL, 0, 0, tiled=True)  16.8 us
    all_to_all x1, starting transfers between devices, per_device(): came = lax.all_to_all(sent, ALL, 0, 0, tiled=True)  12.5 us
    unnamed x21, local copies, waits for them, and re-layouts  6.44 us
    pallas_call x1, Pallas kernels, per_device(): pl.pallas_call(edges_kernel, out_shape=(pack, pack, start), compiler_para...  5.56 us
    ppermute x1, starting transfers between devices, per_device(): top = lax.ppermute(edge_rows(ROWS - HALO), 'row', ahead)  4.52 us
    ppermute x1, starting transfers between devices, per_device(): left = lax.ppermute(right_edge, 'col', ahead)  3.11 us
  transfers between devices with their start and end apart: 5, of which 2 were waited for; matrix products, arithmetic and copies ran while one was open for 5% of the time, Pallas kernels for 5%

profile of v3, /device:TPU:1, one launch (start us, length us, event | category | flops | bytes accessed | tf_op | source)
XLA Modules:
  0.0 118.6 jit_solution(16465976577113522388)
XLA Ops:
  0.8 1.2 fusion
  2.1 2.4 %copy.44 = bf16[1,256,32,128]{3,1,2,0:T(8,128)(2,1)S(1)} copy(bf16[1,256,32,128]{3,2,1,0:T(8,128)(2,1)} %param.8) | data formatting | bytes 4194304 | tf_op args[0]
  4.6 4.5 %collective-permute-start = (bf16[4,288,128]{2,1,0:T(8,128)(2,1)S(1)}, bf16[4,288,128]{2,1,0:T(8,128)(2,1)S(1)}, u32[]{:S(2)}, u32[]{:S(2)}) collective-permute-start(bf16[4,288,128]{2,1,0:T(8,128)(2,1)S(1)} %maximum_bitcast_fusion), channel_id=1, source_target_pairs={{0,4},{4,8},{8,12},{1,5},{5,9},{9,13},{2,6},{6,10},{10,14},{3,7},{... | collective-permute-start | bytes 884744 | tf_op jit(solution)/shard_map/ppermute | solution.py:393
  9.2 1.3 %collective-permute-start.1 = (bf16[4,288,128]{2,1,0:T(8,128)(2,1)S(1)}, bf16[4,288,128]{2,1,0:T(8,128)(2,1)S(1)}, u32[]{:S(2)}, u32[]{:S(2)}) collective-permute-start(bf16[4,288,128]{2,1,0:T(8,128)(2,1)S(1)} %maximum_bitcast_fusion.1), channel_id=1, source_target_pairs={{4,0},{8,4},{12,8},{5,1},{9,5},{13,9},{6,2},{10,6},{14,10},{7,3},{... | collective-permute-start | bytes 884744 | tf_op jit(solution)/shard_map/ppermute | solution.py:394
  10.5 0.8 fusion.4.tags_ref
  11.3 5.6 %shard_map.119 = (bf16[288,128]{1,0:T(8,128)(2,1)}, bf16[288,128]{1,0:T(8,128)(2,1)}, bf16[288,6656]{1,0:T(8,128)(2,1)}) custom-call(bf16[32,256,128]{2,1,0:T(8,128)(2,1)} %bitcast.39, bf16[32,32,128]{2,1,0:T(8,128)(2,1)} %fusion.4.tags_ref), custom_call_target="tpu_custom_call" | custom-call | tf_op jit(solution)/shard_map/pallas_call | solution.py:400
  16.9 2.1 %collective-permute-done.1.bottom_ref = bf16[4,288,128]{2,1,0:T(8,128)(2,1)S(1)} collective-permute-done((bf16[4,288,128]{2,1,0:T(8,128)(2,1)S(1)}, bf16[4,288,128]{2,1,0:T(8,128)(2,1)S(1)}, u32[]{:S(2)}, u32[]{:S(2)}) %collective-permute-start.1) | collective-permute-done | bytes 294944 | tf_op jit(solution)/shard_map/ppermute | solution.py:394
  19.0 0.7 copy-done.4
  19.7 2.2 %shard_map.120 = (bf16[288,256]{1,0:T(8,128)(2,1)}, bf16[288,256]{1,0:T(8,128)(2,1)}) custom-call(bf16[288,128]{1,0:T(8,128)(2,1)} %get-tuple-element.16.left_ref, bf16[288,128]{1,0:T(8,128)(2,1)} %get-tuple-element.17.right_ref, bf16[4,288,128]{2,1,0:T(8,128)(2,1)} %copy-done.3, bf16[4,288,128]{2,1,0:T(8,128)(2,1)} %copy-done.4), custom_call_target="tpu_custom_call" | custom-call | tf_op jit(solution)/shard_map/pallas_call | solution.py:404
  21.9 3.1 %collective-permute-start.2 = (bf16[288,256]{1,0:T(8,128)(2,1)}, bf16[288,256]{1,0:T(8,128)(2,1)S(1)}, u32[]{:S(2)}, u32[]{:S(2)}) collective-permute-start(bf16[288,256]{1,0:T(8,128)(2,1)} %get-tuple-element.18), channel_id=1, source_target_pairs={{0,1},{1,2},{2,3},{4,5},{5,6},{6,7},{8,9},{9,10},{10,11},{12,13},{... | collective-permute-start | bytes 442376 | tf_op jit(solution)/shard_map/ppermute | solution.py:407
  25.0 1.3 %collective-permute-start.3 = (bf16[288,256]{1,0:T(8,128)(2,1)}, bf16[288,256]{1,0:T(8,128)(2,1)S(1)}, u32[]{:S(2)}, u32[]{:S(2)}) collective-permute-start(bf16[288,256]{1,0:T(8,128)(2,1)} %get-tuple-element.19), channel_id=1, source_target_pairs={{1,0},{2,1},{3,2},{5,4},{6,5},{7,6},{9,8},{10,9},{11,10},{13,12},{... | collective-permute-start | bytes 442376 | tf_op jit(solution)/shard_map/ppermute | solution.py:408
  27.2 1.0 copy.35
  28.3 0.8 reshape.49.w2_ref
  29.3 0.8 reshape.50.w2t_ref
  30.1 0.7 copy.34.we_ref
  30.9 1.2 %concatenate.15 = bf16[1232,256]{0,1:T(8,128)(2,1)} concatenate(bf16[1152,256]{0,1:T(8,128)(2,1)S(1)} %copy.32, bf16[72,256]{0,1:T(8,128)(2,1)S(1)} %copy.33, bf16[8,256]{0,1:T(8,128)(2,1)S(1)} %broadcast_in_dim.11), dimensions={0} | concatenate | bytes 1261568 | tf_op jit(solution)/shard_map/concatenate | solution.py:415
  32.1 0.6 copy-done.6
  32.8 29.0 %shard_map.121 = bf16[3072,128]{1,0:T(8,128)(2,1)} custom-call(bf16[288,6656]{1,0:T(8,128)(2,1)} %get-tuple-element.15.x0_ref, bf16[4,288,128]{2,1,0:T(8,128)(2,1)} %copy-done.3, bf16[4,288,128]{2,1,0:T(8,128)(2,1)} %copy-done.4, bf16[288,256]{1,0:T(8,128)(2,1)} %copy-done.6, bf16[288,256]{1,0:T(8,128)(2,1)} %copy-done.7, bf16[64,256]{1,0:T(8,128)(2,1)} %wr_ref.1, ...), custom_call_target="tpu_custom_call" | custom-call | tf_op jit(solution)/shard_map/pallas_call | solution.py:430
  61.8 12.5 %all-to-all-start = ((bf16[128,24,128]{2,1,0:T(8,128)(2,1)}), bf16[128,24,128]{2,1,0:T(8,128)(2,1)S(1)}, u32[]{:S(2)}, u32[]{:S(2)}) async-start(bf16[128,24,128]{2,1,0:T(8,128)(2,1)} %bitcast.41), calls=%async_computation | async-start | bytes 1572864 | tf_op jit(solution)/shard_map/all_to_all | solution.py:458
  74.3 16.8 %all-to-all-done.came_ref = bf16[128,24,128]{2,1,0:T(8,128)(2,1)S(1)} async-done(((bf16[128,24,128]{2,1,0:T(8,128)(2,1)}), bf16[128,24,128]{2,1,0:T(8,128)(2,1)S(1)}, u32[]{:S(2)}, u32[]{:S(2)}) %all-to-all-start) | async-done | bytes 786464 | tf_op jit(solution)/shard_map/all_to_all | solution.py:458
  91.1 0.9 copy-done.1
  91.9 2.3 %shard_map.122 = bf16[128,24,128]{2,1,0:T(8,128)(2,1)} custom-call(s32[1]{0:T(128)} %bitcast.index_ref, bf16[128,24,128]{2,1,0:T(8,128)(2,1)} %copy-done.1), custom_call_target="tpu_custom_call" | custom-call | tf_op jit(solution)/shard_map/pallas_call | solution.py:460
  94.2 21.9 %all_to_all.10 = bf16[128,24,128]{2,1,0:T(8,128)(2,1)} all-to-all(bf16[128,24,128]{2,1,0:T(8,128)(2,1)} %shard_map.122), channel_id=1, replica_groups=mesh['dp'=8,'row'=4,'col'=4] {'dp','row','col'}, dimensions={0} | all-to-all | bytes 1572864 | tf_op jit(solution)/shard_map/all_to_all | solution.py:469
  116.1 2.5 %shard_map.123 = (f32[1,1]{1,0:T(1,128)}, f32[64,256]{1,0:T(8,128)}, f32[9,64,64]{2,1,0:T(8,128)}, f32[64,256]{1,0:T(8,128)}, f32[9,135,256]{2,1,0:T(8,128)}) custom-call(bf16[3072,128]{1,0:T(8,128)(2,1)} %bitcast.42), custom_call_target="tpu_custom_call" | custom-call | tf_op jit(solution)/shard_map/pallas_call | solution.py:470
  (36 shorter events, 1.6 us)
Async XLA Ops:
  4.5 6.8 %copy-start = (bf16[1,256,32,128]{3,1,2,0:T(8,128)(2,1)}, bf16[1,256,32,128]{3,1,2,0:T(8,128)(2,1)S(1)}, u32[]{:S(2)}) copy-start(bf16[1,256,32,128]{3,1,2,0:T(8,128)(2,1)S(1)} %copy.44) | copy-start | bytes 6291460
  4.5 5.9 %copy-start.2 = (bf16[3,3,135,256]{3,2,1,0:T(8,128)(2,1)S(1)}, bf16[3,3,135,256]{3,2,1,0:T(8,128)(2,1)}, u32[]{:S(2)}) copy-start(bf16[3,3,135,256]{3,2,1,0:T(8,128)(2,1)} %param.12) | copy-start | bytes 1866244
  4.6 12.3 %collective-permute-start = (bf16[4,288,128]{2,1,0:T(8,128)(2,1)S(1)}, bf16[4,288,128]{2,1,0:T(8,128)(2,1)S(1)}, u32[]{:S(2)}, u32[]{:S(2)}) collective-permute-start(bf16[4,288,128]{2,1,0:T(8,128)(2,1)S(1)} %maximum_bitcast_fusion), channel_id=1, source_target_pairs={{0,4},{4,8},{8,12},{1,5},{5,9},{9,13},{2,6},{6,10},{10,14},{3,7},{... | collective-permute-start | bytes 884744 | tf_op jit(solution)/shard_map/ppermute | solution.py:393
  9.2 9.8 %collective-permute-start.1 = (bf16[4,288,128]{2,1,0:T(8,128)(2,1)S(1)}, bf16[4,288,128]{2,1,0:T(8,128)(2,1)S(1)}, u32[]{:S(2)}, u32[]{:S(2)}) collective-permute-start(bf16[4,288,128]{2,1,0:T(8,128)(2,1)S(1)} %maximum_bitcast_fusion.1), channel_id=1, source_target_pairs={{4,0},{8,4},{12,8},{5,1},{9,5},{13,9},{6,2},{10,6},{14,10},{7,3},{... | collective-permute-start | bytes 884744 | tf_op jit(solution)/shard_map/ppermute | solution.py:394
  16.9 2.1 %copy-start.3 = (bf16[4,288,128]{2,1,0:T(8,128)(2,1)}, bf16[4,288,128]{2,1,0:T(8,128)(2,1)S(1)}, u32[]{:S(2)}) copy-start(bf16[4,288,128]{2,1,0:T(8,128)(2,1)S(1)} %collective-permute-done.top_ref) | copy-start | bytes 884740
  19.0 0.7 copy-start.4
  21.9 10.1 %collective-permute-start.2 = (bf16[288,256]{1,0:T(8,128)(2,1)}, bf16[288,256]{1,0:T(8,128)(2,1)S(1)}, u32[]{:S(2)}, u32[]{:S(2)}) collective-permute-start(bf16[288,256]{1,0:T(8,128)(2,1)} %get-tuple-element.18), channel_id=1, source_target_pairs={{0,1},{1,2},{2,3},{4,5},{5,6},{6,7},{8,9},{9,10},{10,11},{12,13},{... | collective-permute-start | bytes 442376 | tf_op jit(solution)/shard_map/ppermute | solution.py:407
  25.0 7.0 %collective-permute-start.3 = (bf16[288,256]{1,0:T(8,128)(2,1)}, bf16[288,256]{1,0:T(8,128)(2,1)S(1)}, u32[]{:S(2)}, u32[]{:S(2)}) collective-permute-start(bf16[288,256]{1,0:T(8,128)(2,1)} %get-tuple-element.19), channel_id=1, source_target_pairs={{1,0},{2,1},{3,2},{5,4},{6,5},{7,6},{9,8},{10,9},{11,10},{13,12},{... | collective-permute-start | bytes 442376 | tf_op jit(solution)/shard_map/ppermute | solution.py:408
  26.8 1.4 %copy-start.5 = (bf16[3,3,64,64]{3,2,1,0:T(8,128)(2,1)S(1)}, bf16[3,3,64,64]{3,2,1,0:T(8,128)(2,1)}, u32[]{:S(2)}) copy-start(bf16[3,3,64,64]{3,2,1,0:T(8,128)(2,1)} %param.10) | copy-start | bytes 221188
  26.9 3.2 %copy-start.8 = (bf16[256,64]{0,1:T(8,128)(2,1)S(1)}, bf16[256,64]{0,1:T(8,128)(2,1)}, u32[]{:S(2)}) copy-start(bf16[256,64]{0,1:T(8,128)(2,1)} %param.11) | copy-start | bytes 98308
  32.1 0.7 copy-start.6
  32.1 0.7 copy-start.7
  61.8 29.2 %all-to-all-start = ((bf16[128,24,128]{2,1,0:T(8,128)(2,1)}), bf16[128,24,128]{2,1,0:T(8,128)(2,1)S(1)}, u32[]{:S(2)}, u32[]{:S(2)}) async-start(bf16[128,24,128]{2,1,0:T(8,128)(2,1)} %bitcast.41), calls=%async_computation | async-start | bytes 1572864 | tf_op jit(solution)/shard_map/all_to_all | solution.py:458
  91.1 0.9 copy-start.1

commit v4 on v3

--- a/solution.py
+++ b/solution.py
@@ -4,6 +4,7 @@
 from jax import lax
 from jax.experimental import pallas as pl
 from jax.experimental.pallas import tpu as pltpu
+from jax.sharding import Mesh
 from jax.sharding import PartitionSpec as P
 
 A = 9
@@ -37,9 +38,11 @@
 TAGS = CHANNELS - C
 TAIL = 8
 STACK = 9 * 128 + 9 * TAIL + 8
-ALL = ("dp", "row", "col")
+CHIPS = ("y", "row", "col")
 DEVICES = 128
+PAIRS = 64
 SHARE = 24
+HALF = PAIRS * SHARE
 RED0 = 2 * STACK
 SPAT0 = RED0 + 2 * MID
 EXP0 = SPAT0 + 9 * MID // 2
@@ -144,11 +147,11 @@
 
 
 def main_kernel(
-    x0_ref, top_ref, bottom_ref, left_ref, right_ref,
+    core_ref, x0_ref, top_ref, bottom_ref, left_ref, right_ref,
     wr_ref, w2_ref, w2t_ref, we_ref, wet_ref, w3_ref, w3t_ref, e_ref,
-    out_ref,
+    keep_ref, send_ref,
     x_ref, first_ref, second_ref, block_ref, d_ref, dt_ref, ds_ref, p_ref, facc_ref, cacc_ref,
-    gclass_ref, gred_ref, gspat_ref, gexp_ref, sem,
+    gclass_ref, gred_ref, gspat_ref, gexp_ref, out_ref, sem,
 ):
     copy = pltpu.make_async_copy(x0_ref, x_ref, sem)
     copy.start()
@@ -307,7 +310,11 @@
     out_ref[STAT0:] = jnp.zeros((DEVICES * SHARE - STAT0, 128), BF)
     focal = jnp.sum(facc_ref[...], keepdims=True)
     count = jnp.sum(cacc_ref[...], keepdims=True)
-    out_ref[STAT0 : STAT0 + 16] = stat_rows(focal, count, 16).astype(BF)
+    stats = stat_rows(focal, count, 16)
+    at = lax.broadcasted_iota(jnp.int32, (16, 128), 0)
+    out_ref[STAT0 : STAT0 + 16] = jnp.where(at == core_ref[0], stats, 0.0).astype(BF)
+    for ref, core in ((keep_ref, core_ref[0]), (send_ref, 1 - core_ref[0])):
+        ref[...] = out_ref[pl.ds(pl.multiple_of(core * HALF, HALF), HALF), :]
 
 
 def rounded(x):
@@ -335,19 +342,23 @@
 
 def sum_kernel(index_ref, came_ref, copies_ref):
     total = came_ref[0].astype(F32)
-    for k in range(1, DEVICES):
+    for k in range(1, PAIRS):
         total = total + came_ref[k].astype(F32)
     row = STAT0 % SHARE
     at = lax.broadcasted_iota(jnp.int32, (SHARE, 128), 0)
-    focal, count = stat_values(total[row : row + 1])
+    focal, count = stat_values(total[row : row + 1] + total[row + 1 : row + 2])
     stats = stat_rows(focal, count, SHARE)
     total = jnp.where((at == row) & (index_ref[0] == STAT0 // SHARE), stats, total)
     total = total.astype(BF)
-    for k in range(DEVICES):
+    for k in range(PAIRS):
         copies_ref[k] = total
 
 
-def final_kernel(flat_ref, loss_ref, gred_ref, gspat_ref, gexp_ref, gclass_ref):
+def final_kernel(
+    core_ref, own_ref, other_ref, loss_ref, gred_ref, gspat_ref, gexp_ref, gclass_ref, flat_ref
+):
+    for ref, core in ((own_ref, core_ref[0]), (other_ref, 1 - core_ref[0])):
+        flat_ref[pl.ds(pl.multiple_of(core * HALF, HALF), HALF), :] = ref[...]
     focal, count = stat_values(flat_ref[STAT0 : STAT0 + 16].astype(F32)[:1])
     scale = 1.0 / count
     loss_ref[...] = focal * scale
@@ -427,10 +438,11 @@
     spread = jnp.asarray(spread, BF)
 
     shape = jax.ShapeDtypeStruct
-    out = pl.pallas_call(
+    core = lax.axis_index("core").astype(jnp.int32).reshape(1)
+    keep, send = pl.pallas_call(
         main_kernel,
-        out_shape=shape((DEVICES * SHARE, 128), BF),
-        in_specs=[pl.BlockSpec(memory_space=pl.ANY)] + [pl.BlockSpec(memory_space=pltpu.VMEM)] * 12,
+        out_shape=(shape((HALF, 128), BF), shape((HALF, 128), BF)),
+        in_specs=[pl.BlockSpec(memory_space=pltpu.SMEM), pl.BlockSpec(memory_space=pl.ANY)] + [pl.BlockSpec(memory_space=pltpu.VMEM)] * 12,
         scratch_shapes=[
             pltpu.VMEM((CHANNELS, WIDTH), BF),
             pltpu.VMEM((MID, WIDTH), BF),
@@ -446,27 +458,30 @@
             pltpu.VMEM((MID, C), F32),
             pltpu.VMEM((3 * MID, 3 * MID), F32),
             pltpu.VMEM((MID, C), F32),
+            pltpu.VMEM((DEVICES * SHARE, 128), BF),
             pltpu.SemaphoreType.DMA(()),
         ],
         compiler_params=params,
     )(
-        start, top, bottom, left, right,
+        core, start, top, bottom, left, right,
         reduce_weight, w2, w2t, expand_weight, expand_weight.T, w3, w3t, spread,
     )
 
-    sent = out.reshape(DEVICES, SHARE, 128)
-    came = lax.all_to_all(sent, ALL, 0, 0, tiled=True)
-    index = lax.axis_index(ALL).astype(jnp.int32).reshape(1)
+    swap = [(0, 1), (1, 0)]
+    pair = lax.ppermute(send, "core", swap).astype(F32) + keep.astype(F32)
+    came = lax.all_to_all(pair.astype(BF).reshape(PAIRS, SHARE, 128), CHIPS, 0, 0, tiled=True)
+    index = core * PAIRS + lax.axis_index(CHIPS).astype(jnp.int32)
     copies = pl.pallas_call(
         sum_kernel,
-        out_shape=shape((DEVICES, SHARE, 128), BF),
+        out_shape=shape((PAIRS, SHARE, 128), BF),
         in_specs=[
             pl.BlockSpec(memory_space=pltpu.SMEM),
             pl.BlockSpec(memory_space=pltpu.VMEM),
         ],
         compiler_params=params,
     )(index, came)
-    flat = lax.all_to_all(copies, ALL, 0, 0, tiled=True).reshape(DEVICES * SHARE, 128)
+    own = lax.all_to_all(copies, CHIPS, 0, 0, tiled=True).reshape(PAIRS * SHARE, 128)
+    other = lax.ppermute(own, "core", swap)
     loss, gred, gspat, gexp, gclass = pl.pallas_call(
         final_kernel,
         out_shape=(
@@ -476,8 +491,11 @@
             shape((MID, C), F32),
             shape((9, OUT, C), F32),
         ),
+        in_specs=[pl.BlockSpec(memory_space=pltpu.SMEM)]
+        + [pl.BlockSpec(memory_space=pltpu.VMEM)] * 2,
+        scratch_shapes=[pltpu.VMEM((DEVICES * SHARE, 128), BF)],
         compiler_params=params,
-    )(flat)
+    )(core, own, other)
     return (
         loss.reshape(()),
         gred,
@@ -488,10 +506,14 @@
 
 
 def solution(mesh):
-    maps = P("dp", None, "row", "col")
+    finer = Mesh(
+        mesh.devices.reshape(4, 2, mesh.shape["row"], mesh.shape["col"]),
+        ("y", "core", "row", "col"),
+    )
+    maps = P(("y", "core"), None, "row", "col")
     return jax.shard_map(
         per_device,
-        mesh=mesh,
+        mesh=finer,
         in_specs=(maps, P(), P(), P(), P(), maps, maps),
         out_specs=(P(), P(), P(), P(), P()),
         check_vma=False,

time: 119 us -> 116 us (0.975)
  blocking collectives: 21.9 us -> 14.9 us
  starting transfers between devices: 22.7 us -> 27 us
  waiting for transfers between devices: 18.9 us -> 16.1 us
  other arithmetic: 2.18 us -> 4.02 us
    all_to_all x1, blocking collectives: 21.9 us -> 14.9 us  [per_device(): lax.all_to_all(copies, CHIPS, 0, 0, tiled=True).reshape(PAIRS * SHARE, 128)]
    all_to_all x1, waiting for transfers between devices: 16.8 us -> 11.1 us  [per_device(): lax.all_to_all(pair.astype(BF).reshape(PAIRS, SHARE, 128), CHIPS, 0, 0, t...]
    ppermute x0 -> x2, starting transfers between devices: none -> 5.27 us  [the longest x1 3.08 us: per_device(): other = lax.ppermute(own, 'core', swap)]
    ppermute x0 -> x2, waiting for transfers between devices: none -> 2.91 us  [the longest x1 1.56 us: per_device(): pair = lax.ppermute(send, 'core', swap).astype(F32) + keep.astype(F32)]
    convert_element_type x0 -> x1, other arithmetic: none -> 1.84 us  [per_device(): pair.astype(BF).reshape(PAIRS, SHARE, 128)]
    unnamed x21 -> x25, local copies, waits for them, and re-layouts: 6.44 us -> 7.05 us
  transfers between devices with their start and end apart: 5 -> 7, of which waited for: 2 -> 4; matrix products, arithmetic and copies ran while one was open for 5% -> 6% of each run, Pallas kernels for 5% -> 5%
where the time goes in v4:
time: 116 us; the launch traced here: 115 us
  Pallas kernels  41.3 us (36%)
  starting transfers between devices  27 us (23%)
  waiting for transfers between devices  16.1 us (14%)
  blocking collectives  14.9 us (13%)
  local copies, waits for them, and re-layouts  11.2 us (10%)
  other arithmetic  4.02 us (3%)
    pallas_call x1, Pallas kernels, per_device(): pl.pallas_call(main_kernel, out_shape=(shape((HALF, 128), BF), shape((HAL...  29.1 us
    all_to_all x1, blocking collectives, per_device(): lax.all_to_all(copies, CHIPS, 0, 0, tiled=True).reshape(PAIRS * SHARE, 128)  14.9 us
    all_to_all x1, starting transfers between devices, per_device(): lax.all_to_all(pair.astype(BF).reshape(PAIRS, SHARE, 128), CHIPS, 0, 0, t...  11.5 us
    all_to_all x1, waiting for transfers between devices, per_device(): lax.all_to_all(pair.astype(BF).reshape(PAIRS, SHARE, 128), CHIPS, 0, 0, t...  11.1 us
    unnamed x25, local copies, waits for them, and re-layouts  7.05 us
    pallas_call x1, Pallas kernels, per_device(): pl.pallas_call(edges_kernel, out_shape=(pack, pack, start), compiler_para...  5.58 us
    ppermute x1, starting transfers between devices, per_device(): top = lax.ppermute(edge_rows(ROWS - HALO), 'row', ahead)  4.52 us
    ppermute x1, starting transfers between devices, per_device(): left = lax.ppermute(right_edge, 'col', ahead)  3.11 us
  transfers between devices with their start and end apart: 7, of which 4 were waited for; matrix products, arithmetic and copies ran while one was open for 6% of the time, Pallas kernels for 5%

profile of v4, /device:TPU:1, one launch (start us, length us, event | category | flops | bytes accessed | tf_op | source)
XLA Modules:
  0.0 115.3 jit_solution(9354318607308340133)
XLA Ops:
  0.8 1.2 %fusion = (bf16[9,32,128]{2,0,1:T(8,128)(2,1)S(1)}, bf16[9,32,128]{2,0,1:T(8,128)(2,1)S(1)}) fusion(s32[1,9,32,128]{3,2,1,0:T(8,128)} %param.13, s32[1,9,32,128]{3,2,1,0:T(8,128)} %param.14), kind=kLoop, calls=%fused_computation.9 | loop fusion | flops 73728 | bytes 442368 | tf_op jit(solution)/shard_map/convert_element_type | solution.py:395
  2.1 2.4 %copy.44 = bf16[1,256,32,128]{3,1,2,0:T(8,128)(2,1)S(1)} copy(bf16[1,256,32,128]{3,2,1,0:T(8,128)(2,1)} %param.8) | data formatting | bytes 4194304 | tf_op args[0]
  4.6 4.5 %collective-permute-start = (bf16[4,288,128]{2,1,0:T(8,128)(2,1)S(1)}, bf16[4,288,128]{2,1,0:T(8,128)(2,1)S(1)}, u32[]{:S(2)}, u32[]{:S(2)}) collective-permute-start(bf16[4,288,128]{2,1,0:T(8,128)(2,1)S(1)} %maximum_bitcast_fusion), channel_id=1, source_target_pairs={{0,4},{4,8},{8,12},{1,5},{5,9},{9,13},{2,6},{6,10},{10,14},{3,7},{... | collective-permute-start | bytes 884744 | tf_op jit(solution)/shard_map/ppermute | solution.py:404
  9.2 1.3 %collective-permute-start.1 = (bf16[4,288,128]{2,1,0:T(8,128)(2,1)S(1)}, bf16[4,288,128]{2,1,0:T(8,128)(2,1)S(1)}, u32[]{:S(2)}, u32[]{:S(2)}) collective-permute-start(bf16[4,288,128]{2,1,0:T(8,128)(2,1)S(1)} %maximum_bitcast_fusion.1), channel_id=1, source_target_pairs={{4,0},{8,4},{12,8},{5,1},{9,5},{13,9},{6,2},{10,6},{14,10},{7,3},{... | collective-permute-start | bytes 884744 | tf_op jit(solution)/shard_map/ppermute | solution.py:405
  10.5 0.8 fusion.4.tags_ref
  11.3 5.6 %shard_map.119 = (bf16[288,128]{1,0:T(8,128)(2,1)}, bf16[288,128]{1,0:T(8,128)(2,1)}, bf16[288,6656]{1,0:T(8,128)(2,1)}) custom-call(bf16[32,256,128]{2,1,0:T(8,128)(2,1)} %bitcast.40, bf16[32,32,128]{2,1,0:T(8,128)(2,1)} %fusion.4.tags_ref), custom_call_target="tpu_custom_call" | custom-call | tf_op jit(solution)/shard_map/pallas_call | solution.py:411
  16.9 2.1 %collective-permute-done.1.bottom_ref = bf16[4,288,128]{2,1,0:T(8,128)(2,1)S(1)} collective-permute-done((bf16[4,288,128]{2,1,0:T(8,128)(2,1)S(1)}, bf16[4,288,128]{2,1,0:T(8,128)(2,1)S(1)}, u32[]{:S(2)}, u32[]{:S(2)}) %collective-permute-start.1) | collective-permute-done | bytes 294944 | tf_op jit(solution)/shard_map/ppermute | solution.py:405
  19.7 2.2 %shard_map.120 = (bf16[288,256]{1,0:T(8,128)(2,1)}, bf16[288,256]{1,0:T(8,128)(2,1)}) custom-call(bf16[288,128]{1,0:T(8,128)(2,1)} %get-tuple-element.18.left_ref, bf16[288,128]{1,0:T(8,128)(2,1)} %get-tuple-element.19.right_ref, bf16[4,288,128]{2,1,0:T(8,128)(2,1)} %copy-done.4, bf16[4,288,128]{2,1,0:T(8,128)(2,1)} %copy-done.5), custom_call_target="tpu_custom_call" | custom-call | tf_op jit(solution)/shard_map/pallas_call | solution.py:415
  21.9 3.1 %collective-permute-start.2 = (bf16[288,256]{1,0:T(8,128)(2,1)}, bf16[288,256]{1,0:T(8,128)(2,1)S(1)}, u32[]{:S(2)}, u32[]{:S(2)}) collective-permute-start(bf16[288,256]{1,0:T(8,128)(2,1)} %get-tuple-element.20), channel_id=1, source_target_pairs={{0,1},{1,2},{2,3},{4,5},{5,6},{6,7},{8,9},{9,10},{10,11},{12,13},{... | collective-permute-start | bytes 442376 | tf_op jit(solution)/shard_map/ppermute | solution.py:418
  25.1 1.3 %collective-permute-start.3 = (bf16[288,256]{1,0:T(8,128)(2,1)}, bf16[288,256]{1,0:T(8,128)(2,1)S(1)}, u32[]{:S(2)}, u32[]{:S(2)}) collective-permute-start(bf16[288,256]{1,0:T(8,128)(2,1)} %get-tuple-element.21), channel_id=1, source_target_pairs={{1,0},{2,1},{3,2},{5,4},{6,5},{7,6},{9,8},{10,9},{11,10},{13,12},{... | collective-permute-start | bytes 442376 | tf_op jit(solution)/shard_map/ppermute | solution.py:419
  27.3 1.0 copy.35
  29.3 0.8 reshape.50.w2t_ref
  30.9 1.2 %concatenate.15 = bf16[1232,256]{0,1:T(8,128)(2,1)} concatenate(bf16[1152,256]{0,1:T(8,128)(2,1)S(1)} %copy.32, bf16[72,256]{0,1:T(8,128)(2,1)S(1)} %copy.33, bf16[8,256]{0,1:T(8,128)(2,1)S(1)} %broadcast_in_dim.11), dimensions={0} | concatenate | bytes 1261568 | tf_op jit(solution)/shard_map/concatenate | solution.py:426
  32.8 29.1 %shard_map.121 = (bf16[1536,128]{1,0:T(8,128)(2,1)}, bf16[1536,128]{1,0:T(8,128)(2,1)}) custom-call(s32[1]{0:T(128)} %bitcast.core_ref, bf16[288,6656]{1,0:T(8,128)(2,1)} %get-tuple-element.17.x0_ref, bf16[4,288,128]{2,1,0:T(8,128)(2,1)} %copy-done.4, bf16[4,288,128]{2,1,0:T(8,128)(2,1)} %copy-done.5, bf16[288,256]{1,0:T(8,128)(2,1)} %copy-done.8, ...), custom_call_target="tpu_custom_call" | custom-call | tf_op jit(solution)/shard_map/pallas_call | solution.py:442
  61.9 2.2 %collective-permute-start.4 = (bf16[1536,128]{1,0:T(8,128)(2,1)}, bf16[1536,128]{1,0:T(8,128)(2,1)S(1)}, u32[]{:S(2)}, u32[]{:S(2)}) collective-permute-start(bf16[1536,128]{1,0:T(8,128)(2,1)} %get-tuple-element.22), channel_id=1, source_target_pairs={{0,16},{16,0},{1,17},{17,1},{2,18},{18,2},{3,19},{19,3},{4,20},{20... | collective-permute-start | bytes 1179656 | tf_op jit(solution)/shard_map/ppermute | solution.py:471
  64.1 1.6 %collective-permute-done.4 = bf16[1536,128]{1,0:T(8,128)(2,1)S(1)} collective-permute-done((bf16[1536,128]{1,0:T(8,128)(2,1)}, bf16[1536,128]{1,0:T(8,128)(2,1)S(1)}, u32[]{:S(2)}, u32[]{:S(2)}) %collective-permute-start.4) | collective-permute-done | bytes 393248 | tf_op jit(solution)/shard_map/ppermute | solution.py:471
  65.7 1.8 %add_convert_fusion = bf16[1536,128]{1,0:T(8,128)(2,1)} fusion(bf16[1536,128]{1,0:T(8,128)(2,1)} %get-tuple-element.23, bf16[1536,128]{1,0:T(8,128)(2,1)S(1)} %collective-permute-done.4), kind=kLoop, calls=%fused_computation | loop fusion | flops 786432 | bytes 1179648 | tf_op jit(solution)/shard_map/convert_element_type | solution.py:472
  67.5 11.5 %all-to-all-start = ((bf16[64,24,128]{2,1,0:T(8,128)(2,1)}), bf16[64,24,128]{2,1,0:T(8,128)(2,1)S(1)}, u32[]{:S(2)}, u32[]{:S(2)}) async-start(bf16[64,24,128]{2,1,0:T(8,128)(2,1)} %bitcast.19), calls=%async_computation | async-start | bytes 786432 | tf_op jit(solution)/shard_map/all_to_all | solution.py:472
  79.0 11.1 %all-to-all-done.came_ref = bf16[64,24,128]{2,1,0:T(8,128)(2,1)S(1)} async-done(((bf16[64,24,128]{2,1,0:T(8,128)(2,1)}), bf16[64,24,128]{2,1,0:T(8,128)(2,1)S(1)}, u32[]{:S(2)}, u32[]{:S(2)}) %all-to-all-start) | async-done | bytes 393248 | tf_op jit(solution)/shard_map/all_to_all | solution.py:472
  90.8 1.9 %shard_map.122 = bf16[64,24,128]{2,1,0:T(8,128)(2,1)} custom-call(s32[1]{0:T(128)S(6)} %add.22.index_ref, bf16[64,24,128]{2,1,0:T(8,128)(2,1)} %copy-done.2), custom_call_target="tpu_custom_call" | custom-call | tf_op jit(solution)/shard_map/pallas_call | solution.py:474
  92.8 14.9 %all_to_all.10 = bf16[64,24,128]{2,1,0:T(8,128)(2,1)S(1)} all-to-all(bf16[64,24,128]{2,1,0:T(8,128)(2,1)} %shard_map.122), channel_id=1, replica_groups=mesh['y'=4,'core'=2,'row'=4,'col'=4] {'y','row','col'}, dimensions={0} | all-to-all | bytes 786432 | tf_op jit(solution)/shard_map/all_to_all | solution.py:483
  107.6 3.1 %collective-permute-start.5 = (bf16[1536,128]{1,0:T(8,128)(2,1)S(1)}, bf16[1536,128]{1,0:T(8,128)(2,1)S(1)}, u32[]{:S(2)}, u32[]{:S(2)}) collective-permute-start(bf16[1536,128]{1,0:T(8,128)(2,1)S(1)} %bitcast.47), channel_id=1, source_target_pairs={{0,16},{16,0},{1,17},{17,1},{2,18},{18,2},{3,19},{19,3},{4,20},{20... | collective-permute-start | bytes 1179656 | tf_op jit(solution)/shard_map/ppermute | solution.py:484
  110.7 1.3 %collective-permute-done.5.other_ref = bf16[1536,128]{1,0:T(8,128)(2,1)S(1)} collective-permute-done((bf16[1536,128]{1,0:T(8,128)(2,1)S(1)}, bf16[1536,128]{1,0:T(8,128)(2,1)S(1)}, u32[]{:S(2)}, u32[]{:S(2)}) %collective-permute-start.5) | collective-permute-done | bytes 393248 | tf_op jit(solution)/shard_map/ppermute | solution.py:484
  112.8 2.5 %shard_map.123 = (f32[1,1]{1,0:T(1,128)}, f32[64,256]{1,0:T(8,128)}, f32[9,64,64]{2,1,0:T(8,128)}, f32[64,256]{1,0:T(8,128)}, f32[9,135,256]{2,1,0:T(8,128)}) custom-call(s32[1]{0:T(128)} %bitcast.core_ref, bf16[1536,128]{1,0:T(8,128)(2,1)} %bitcast.48, bf16[1536,128]{1,0:T(8,128)(2,1)} %copy-done.7), custom_call_target="tpu_custom_call" | custom-call | tf_op jit(solution)/shard_map/pallas_call | solution.py:485
  (45 shorter events, 6.0 us)
Async XLA Ops:
  4.5 6.8 %copy-start = (bf16[1,256,32,128]{3,1,2,0:T(8,128)(2,1)}, bf16[1,256,32,128]{3,1,2,0:T(8,128)(2,1)S(1)}, u32[]{:S(2)}) copy-start(bf16[1,256,32,128]{3,1,2,0:T(8,128)(2,1)S(1)} %copy.44) | copy-start | bytes 6291460
  4.5 5.9 %copy-start.1 = (bf16[3,3,135,256]{3,2,1,0:T(8,128)(2,1)S(1)}, bf16[3,3,135,256]{3,2,1,0:T(8,128)(2,1)}, u32[]{:S(2)}) copy-start(bf16[3,3,135,256]{3,2,1,0:T(8,128)(2,1)} %param.12) | copy-start | bytes 1866244
  4.6 12.3 %collective-permute-start = (bf16[4,288,128]{2,1,0:T(8,128)(2,1)S(1)}, bf16[4,288,128]{2,1,0:T(8,128)(2,1)S(1)}, u32[]{:S(2)}, u32[]{:S(2)}) collective-permute-start(bf16[4,288,128]{2,1,0:T(8,128)(2,1)S(1)} %maximum_bitcast_fusion), channel_id=1, source_target_pairs={{0,4},{4,8},{8,12},{1,5},{5,9},{9,13},{2,6},{6,10},{10,14},{3,7},{... | collective-permute-start | bytes 884744 | tf_op jit(solution)/shard_map/ppermute | solution.py:404
  9.2 9.8 %collective-permute-start.1 = (bf16[4,288,128]{2,1,0:T(8,128)(2,1)S(1)}, bf16[4,288,128]{2,1,0:T(8,128)(2,1)S(1)}, u32[]{:S(2)}, u32[]{:S(2)}) collective-permute-start(bf16[4,288,128]{2,1,0:T(8,128)(2,1)S(1)} %maximum_bitcast_fusion.1), channel_id=1, source_target_pairs={{4,0},{8,4},{12,8},{5,1},{9,5},{13,9},{6,2},{10,6},{14,10},{7,3},{... | collective-permute-start | bytes 884744 | tf_op jit(solution)/shard_map/ppermute | solution.py:405
  16.9 2.1 %copy-start.4 = (bf16[4,288,128]{2,1,0:T(8,128)(2,1)}, bf16[4,288,128]{2,1,0:T(8,128)(2,1)S(1)}, u32[]{:S(2)}) copy-start(bf16[4,288,128]{2,1,0:T(8,128)(2,1)S(1)} %collective-permute-done.top_ref) | copy-start | bytes 884740
  19.0 0.7 copy-start.5
  21.9 10.1 %collective-permute-start.2 = (bf16[288,256]{1,0:T(8,128)(2,1)}, bf16[288,256]{1,0:T(8,128)(2,1)S(1)}, u32[]{:S(2)}, u32[]{:S(2)}) collective-permute-start(bf16[288,256]{1,0:T(8,128)(2,1)} %get-tuple-element.20), channel_id=1, source_target_pairs={{0,1},{1,2},{2,3},{4,5},{5,6},{6,7},{8,9},{9,10},{10,11},{12,13},{... | collective-permute-start | bytes 442376 | tf_op jit(solution)/shard_map/ppermute | solution.py:418
  25.1 7.0 %collective-permute-start.3 = (bf16[288,256]{1,0:T(8,128)(2,1)}, bf16[288,256]{1,0:T(8,128)(2,1)S(1)}, u32[]{:S(2)}, u32[]{:S(2)}) collective-permute-start(bf16[288,256]{1,0:T(8,128)(2,1)} %get-tuple-element.21), channel_id=1, source_target_pairs={{1,0},{2,1},{3,2},{5,4},{6,5},{7,6},{9,8},{10,9},{11,10},{13,12},{... | collective-permute-start | bytes 442376 | tf_op jit(solution)/shard_map/ppermute | solution.py:419
  26.9 1.4 %copy-start.6 = (bf16[3,3,64,64]{3,2,1,0:T(8,128)(2,1)S(1)}, bf16[3,3,64,64]{3,2,1,0:T(8,128)(2,1)}, u32[]{:S(2)}) copy-start(bf16[3,3,64,64]{3,2,1,0:T(8,128)(2,1)} %param.10) | copy-start | bytes 221188
  26.9 3.2 %copy-start.10 = (bf16[256,64]{0,1:T(8,128)(2,1)S(1)}, bf16[256,64]{0,1:T(8,128)(2,1)}, u32[]{:S(2)}) copy-start(bf16[256,64]{0,1:T(8,128)(2,1)} %param.11) | copy-start | bytes 98308
  32.1 0.7 copy-start.8
  32.1 0.7 copy-start.9
  61.9 3.8 %collective-permute-start.4 = (bf16[1536,128]{1,0:T(8,128)(2,1)}, bf16[1536,128]{1,0:T(8,128)(2,1)S(1)}, u32[]{:S(2)}, u32[]{:S(2)}) collective-permute-start(bf16[1536,128]{1,0:T(8,128)(2,1)} %get-tuple-element.22), channel_id=1, source_target_pairs={{0,16},{16,0},{1,17},{17,1},{2,18},{18,2},{3,19},{19,3},{4,20},{20... | collective-permute-start | bytes 1179656 | tf_op jit(solution)/shard_map/ppermute | solution.py:471
  67.5 22.6 %all-to-all-start = ((bf16[64,24,128]{2,1,0:T(8,128)(2,1)}), bf16[64,24,128]{2,1,0:T(8,128)(2,1)S(1)}, u32[]{:S(2)}, u32[]{:S(2)}) async-start(bf16[64,24,128]{2,1,0:T(8,128)(2,1)} %bitcast.19), calls=%async_computation | async-start | bytes 786432 | tf_op jit(solution)/shard_map/all_to_all | solution.py:472
  90.1 0.7 copy-start.2
  107.6 4.4 %copy-start.3 = (bf16[64,24,128]{2,1,0:T(8,128)(2,1)}, bf16[64,24,128]{2,1,0:T(8,128)(2,1)S(1)}, u32[]{:S(2)}) copy-start(bf16[64,24,128]{2,1,0:T(8,128)(2,1)S(1)} %all_to_all.10) | copy-start | bytes 1179652
  107.6 4.4 %collective-permute-start.5 = (bf16[1536,128]{1,0:T(8,128)(2,1)S(1)}, bf16[1536,128]{1,0:T(8,128)(2,1)S(1)}, u32[]{:S(2)}, u32[]{:S(2)}) collective-permute-start(bf16[1536,128]{1,0:T(8,128)(2,1)S(1)} %bitcast.47), channel_id=1, source_target_pairs={{0,16},{16,0},{1,17},{17,1},{2,18},{18,2},{3,19},{19,3},{4,20},{20... | collective-permute-start | bytes 1179656 | tf_op jit(solution)/shard_map/ppermute | solution.py:484
  112.1 0.7 copy-start.7

commit v5 on v4

--- a/solution.py
+++ b/solution.py
@@ -71,6 +71,19 @@
     put(ref, rows, tile + 1, turned, 0, turn)
 
 
+def put_span(ref, value, at, width):
+    tile, low = divmod(at, 128)
+    put(ref, BOTH, tile, value, low, min(low + width, 128))
+    if low + width > 128:
+        put(ref, BOTH, tile + 1, value, 0, low + width - 128)
+
+
+def spot(r):
+    if HALO <= r < HALO + ROWS:
+        return HALO * (r - HALO)
+    return 128 + HALO * (r if r < HALO else r - ROWS)
+
+
 def edges_kernel(maps_ref, tags_ref, left_ref, right_ref, x_ref):
     x_ref[...] = jnp.zeros_like(x_ref)
     left_ref[...] = jnp.zeros_like(left_ref)
@@ -148,32 +161,40 @@
 
 def main_kernel(
     core_ref, x0_ref, top_ref, bottom_ref, left_ref, right_ref,
-    wr_ref, w2_ref, w2t_ref, we_ref, wet_ref, w3_ref, w3t_ref, e_ref,
+    wr_ref, w2_ref, w2t_ref, we_ref, wet_ref, w3_raw, w3t_raw, e_ref,
     keep_ref, send_ref,
     x_ref, first_ref, second_ref, block_ref, d_ref, dt_ref, ds_ref, p_ref, facc_ref, cacc_ref,
-    gclass_ref, gred_ref, gspat_ref, gexp_ref, out_ref, sem,
+    gclass_ref, gred_ref, gspat_ref, gexp_ref, out_ref, w3_ref, w3t_ref, sem,
 ):
-    copy = pltpu.make_async_copy(x0_ref, x_ref, sem)
-    copy.start()
-    for ref in (first_ref, second_ref, block_ref, d_ref, dt_ref, ds_ref, p_ref):
+    copy = pltpu.make_async_copy(x0_ref, x_ref, sem.at[0])
+    weights = pltpu.make_async_copy(w3_raw, w3_ref, sem.at[1])
+    weights_back = pltpu.make_async_copy(w3t_raw, w3t_ref, sem.at[2])
+    for each in (copy, weights, weights_back):
+        each.start()
+    p_ref[:, :MARGIN] = jnp.zeros((p_ref.shape[0], MARGIN), F32)
+    for ref in (first_ref, second_ref, block_ref, d_ref, dt_ref, ds_ref):
         ref[:, : 2 * MARGIN] = jnp.zeros((ref.shape[0], 2 * MARGIN), ref.dtype)
         ref[:, RIGHT:] = jnp.zeros((ref.shape[0], WIDTH - RIGHT), ref.dtype)
     for ref in (gclass_ref, gred_ref, gspat_ref, gexp_ref, facc_ref, cacc_ref):
         ref[...] = jnp.zeros_like(ref)
     copy.wait()
-    for r in range(FULL):
-        if r < HALO:
-            place(x_ref, BOTH, top_ref[r], r)
-        elif r >= HALO + ROWS:
-            place(x_ref, BOTH, bottom_ref[r - HALO - ROWS], r)
-        if HALO <= r < HALO + ROWS:
-            spot = HALO * (r - HALO)
-        else:
-            spot = 128 + HALO * (r if r < HALO else r - ROWS)
-        source = slice(spot // 128 * 128, spot // 128 * 128 + 128)
-        for edge_ref, at in ((left_ref, MARGIN + r * STRIDE), (right_ref, MARGIN + r * STRIDE + HALO + COLS)):
-            turned = pltpu.roll(edge_ref[:, source], (at - spot) % 128, 1)
-            put(x_ref, BOTH, at // 128, turned, at % 128, at % 128 + HALO)
+    for h in range(HALO):
+        place(x_ref, BOTH, top_ref[h], h)
+        place(x_ref, BOTH, bottom_ref[h], h + HALO + ROWS)
+    lane = lax.broadcasted_iota(jnp.int32, (CHANNELS, 128), 1)
+    for r in range(-1, FULL):
+        at = MARGIN + r * STRIDE + HALO + COLS
+        if 0 <= r < FULL - 1 and spot(r + 1) == spot(r) + HALO:
+            tile, low = divmod(spot(r), 128)
+            where = slice(tile * 128, tile * 128 + 128)
+            both = jnp.where(lane < low + HALO, right_ref[:, where], left_ref[:, where])
+            put_span(x_ref, pltpu.roll(both, (at - low) % 128, 1), at, 2 * HALO)
+            continue
+        for ref, row, to in ((right_ref, r, at), (left_ref, r + 1, at + HALO)):
+            if 0 <= row < FULL:
+                tile, low = divmod(spot(row), 128)
+                one = ref[:, tile * 128 : tile * 128 + 128]
+                put_span(x_ref, pltpu.roll(one, (to - low) % 128, 1), to, HALO)
 
     def first_step(lane, n):
         x = x_ref[:C, pl.ds(lane, n)]
@@ -232,6 +253,7 @@
         positives = jnp.where((labels > 0.5) & (tag < A) & inner, 1.0, 0.0)
         cacc_ref[...] += positives[:8] + positives[8:]
 
+    weights.wait()
     begin, n, count = SPLIT[3]
     for j in range(count + 2):
         if j >= 2 and j - 2 < SPLIT[4][2]:
@@ -268,6 +290,7 @@
         )
         gclass_ref[...] += dot_nt(own, block)
 
+    weights_back.wait()
     chunks(*SPLIT[5], class_back)
 
     def spatial_back(lane, n):
@@ -442,7 +465,10 @@
     keep, send = pl.pallas_call(
         main_kernel,
         out_shape=(shape((HALF, 128), BF), shape((HALF, 128), BF)),
-        in_specs=[pl.BlockSpec(memory_space=pltpu.SMEM), pl.BlockSpec(memory_space=pl.ANY)] + [pl.BlockSpec(memory_space=pltpu.VMEM)] * 12,
+        in_specs=[pl.BlockSpec(memory_space=pltpu.SMEM), pl.BlockSpec(memory_space=pl.ANY)]
+        + [pl.BlockSpec(memory_space=pltpu.VMEM)] * 9
+        + [pl.BlockSpec(memory_space=pl.ANY)] * 2
+        + [pl.BlockSpec(memory_space=pltpu.VMEM)],
         scratch_shapes=[
             pltpu.VMEM((CHANNELS, WIDTH), BF),
             pltpu.VMEM((MID, WIDTH), BF),
@@ -459,7 +485,9 @@
             pltpu.VMEM((3 * MID, 3 * MID), F32),
             pltpu.VMEM((MID, C), F32),
             pltpu.VMEM((DEVICES * SHARE, 128), BF),
-            pltpu.SemaphoreType.DMA(()),
+            pltpu.VMEM((3 * 136, 3 * C), BF),
+            pltpu.VMEM((C, STACK), BF),
+            pltpu.SemaphoreType.DMA((3,)),
         ],
         compiler_params=params,
     )(

time: 116 us -> 115 us (level)
  no operation moved by 1% of the time
where the time goes in v5:
time: 115 us; the launch traced here: 114 us
  Pallas kernels  40.2 us (35%)
  starting transfers between devices  27.2 us (24%)
  waiting for transfers between devices  16.1 us (14%)
  blocking collectives  14.9 us (13%)
  local copies, waits for them, and re-layouts  11 us (10%)
  other arithmetic  4.02 us (3%)
    pallas_call x1, Pallas kernels, per_device(): pl.pallas_call(main_kernel, out_shape=(shape((HALF, 128), BF), shape((HAL...  28 us
    all_to_all x1, blocking collectives, per_device(): lax.all_to_all(copies, CHIPS, 0, 0, tiled=True).reshape(PAIRS * SHARE, 128)  14.9 us
    all_to_all x1, starting transfers between devices, per_device(): lax.all_to_all(pair.astype(BF).reshape(PAIRS, SHARE, 128), CHIPS, 0, 0, t...  11.5 us
    all_to_all x1, waiting for transfers between devices, per_device(): lax.all_to_all(pair.astype(BF).reshape(PAIRS, SHARE, 128), CHIPS, 0, 0, t...  11.1 us
    unnamed x25, local copies, waits for them, and re-layouts  7.05 us
    pallas_call x1, Pallas kernels, per_device(): pl.pallas_call(edges_kernel, out_shape=(pack, pack, start), compiler_para...  5.58 us
    ppermute x1, starting transfers between devices, per_device(): top = lax.ppermute(edge_rows(ROWS - HALO), 'row', ahead)  4.52 us
    ppermute x1, starting transfers between devices, per_device(): left = lax.ppermute(right_edge, 'col', ahead)  3.11 us
  transfers between devices with their start and end apart: 7, of which 4 were waited for; matrix products, arithmetic and copies ran while one was open for 6% of the time, Pallas kernels for 5%

profile of v5, /device:TPU:1, one launch (start us, length us, event | category | flops | bytes accessed | tf_op | source)
XLA Modules:
  0.0 114.2 jit_solution(929780987552924184)
XLA Ops:
  0.8 1.2 %fusion = (bf16[9,32,128]{2,0,1:T(8,128)(2,1)S(1)}, bf16[9,32,128]{2,0,1:T(8,128)(2,1)S(1)}) fusion(s32[1,9,32,128]{3,2,1,0:T(8,128)} %param.13, s32[1,9,32,128]{3,2,1,0:T(8,128)} %param.14), kind=kLoop, calls=%fused_computation.9 | loop fusion | flops 73728 | bytes 442368 | tf_op jit(solution)/shard_map/convert_element_type | solution.py:418
  2.1 2.4 %copy.44 = bf16[1,256,32,128]{3,1,2,0:T(8,128)(2,1)S(1)} copy(bf16[1,256,32,128]{3,2,1,0:T(8,128)(2,1)} %param.8) | data formatting | bytes 4194304 | tf_op args[0]
  4.6 4.5 %collective-permute-start = (bf16[4,288,128]{2,1,0:T(8,128)(2,1)S(1)}, bf16[4,288,128]{2,1,0:T(8,128)(2,1)S(1)}, u32[]{:S(2)}, u32[]{:S(2)}) collective-permute-start(bf16[4,288,128]{2,1,0:T(8,128)(2,1)S(1)} %maximum_bitcast_fusion), channel_id=1, source_target_pairs={{0,4},{4,8},{8,12},{1,5},{5,9},{9,13},{2,6},{6,10},{10,14},{3,7},{... | collective-permute-start | bytes 884744 | tf_op jit(solution)/shard_map/ppermute | solution.py:427
  9.2 1.3 %collective-permute-start.1 = (bf16[4,288,128]{2,1,0:T(8,128)(2,1)S(1)}, bf16[4,288,128]{2,1,0:T(8,128)(2,1)S(1)}, u32[]{:S(2)}, u32[]{:S(2)}) collective-permute-start(bf16[4,288,128]{2,1,0:T(8,128)(2,1)S(1)} %maximum_bitcast_fusion.1), channel_id=1, source_target_pairs={{4,0},{8,4},{12,8},{5,1},{9,5},{13,9},{6,2},{10,6},{14,10},{7,3},{... | collective-permute-start | bytes 884744 | tf_op jit(solution)/shard_map/ppermute | solution.py:428
  10.5 0.8 fusion.4.tags_ref
  11.3 5.6 %shard_map.119 = (bf16[288,128]{1,0:T(8,128)(2,1)}, bf16[288,128]{1,0:T(8,128)(2,1)}, bf16[288,6656]{1,0:T(8,128)(2,1)}) custom-call(bf16[32,256,128]{2,1,0:T(8,128)(2,1)} %bitcast.40, bf16[32,32,128]{2,1,0:T(8,128)(2,1)} %fusion.4.tags_ref), custom_call_target="tpu_custom_call" | custom-call | tf_op jit(solution)/shard_map/pallas_call | solution.py:434
  16.9 2.1 %collective-permute-done.1.bottom_ref = bf16[4,288,128]{2,1,0:T(8,128)(2,1)S(1)} collective-permute-done((bf16[4,288,128]{2,1,0:T(8,128)(2,1)S(1)}, bf16[4,288,128]{2,1,0:T(8,128)(2,1)S(1)}, u32[]{:S(2)}, u32[]{:S(2)}) %collective-permute-start.1) | collective-permute-done | bytes 294944 | tf_op jit(solution)/shard_map/ppermute | solution.py:428
  19.7 2.2 %shard_map.120 = (bf16[288,256]{1,0:T(8,128)(2,1)}, bf16[288,256]{1,0:T(8,128)(2,1)}) custom-call(bf16[288,128]{1,0:T(8,128)(2,1)} %get-tuple-element.18.left_ref, bf16[288,128]{1,0:T(8,128)(2,1)} %get-tuple-element.19.right_ref, bf16[4,288,128]{2,1,0:T(8,128)(2,1)} %copy-done.4, bf16[4,288,128]{2,1,0:T(8,128)(2,1)} %copy-done.5), custom_call_target="tpu_custom_call" | custom-call | tf_op jit(solution)/shard_map/pallas_call | solution.py:438
  21.9 3.1 %collective-permute-start.2 = (bf16[288,256]{1,0:T(8,128)(2,1)}, bf16[288,256]{1,0:T(8,128)(2,1)S(1)}, u32[]{:S(2)}, u32[]{:S(2)}) collective-permute-start(bf16[288,256]{1,0:T(8,128)(2,1)} %get-tuple-element.20), channel_id=1, source_target_pairs={{0,1},{1,2},{2,3},{4,5},{5,6},{6,7},{8,9},{9,10},{10,11},{12,13},{... | collective-permute-start | bytes 442376 | tf_op jit(solution)/shard_map/ppermute | solution.py:441
  25.1 1.5 %collective-permute-start.3 = (bf16[288,256]{1,0:T(8,128)(2,1)}, bf16[288,256]{1,0:T(8,128)(2,1)S(1)}, u32[]{:S(2)}, u32[]{:S(2)}) collective-permute-start(bf16[288,256]{1,0:T(8,128)(2,1)} %get-tuple-element.21), channel_id=1, source_target_pairs={{1,0},{2,1},{3,2},{5,4},{6,5},{7,6},{9,8},{10,9},{11,10},{13,12},{... | collective-permute-start | bytes 442376 | tf_op jit(solution)/shard_map/ppermute | solution.py:442
  27.4 1.0 copy.35
  29.5 0.8 reshape.50.w2t_ref
  31.1 1.0 concatenate.15
  32.8 28.0 %shard_map.121 = (bf16[1536,128]{1,0:T(8,128)(2,1)}, bf16[1536,128]{1,0:T(8,128)(2,1)}) custom-call(s32[1]{0:T(128)} %bitcast.core_ref, bf16[288,6656]{1,0:T(8,128)(2,1)} %get-tuple-element.17.x0_ref, bf16[4,288,128]{2,1,0:T(8,128)(2,1)} %copy-done.4, bf16[4,288,128]{2,1,0:T(8,128)(2,1)} %copy-done.5, bf16[288,256]{1,0:T(8,128)(2,1)} %copy-done.8, ...), custom_call_target="tpu_custom_call" | custom-call | tf_op jit(solution)/shard_map/pallas_call | solution.py:465
  60.8 2.2 %collective-permute-start.4 = (bf16[1536,128]{1,0:T(8,128)(2,1)}, bf16[1536,128]{1,0:T(8,128)(2,1)S(1)}, u32[]{:S(2)}, u32[]{:S(2)}) collective-permute-start(bf16[1536,128]{1,0:T(8,128)(2,1)} %get-tuple-element.22), channel_id=1, source_target_pairs={{0,16},{16,0},{1,17},{17,1},{2,18},{18,2},{3,19},{19,3},{4,20},{20... | collective-permute-start | bytes 1179656 | tf_op jit(solution)/shard_map/ppermute | solution.py:499
  63.0 1.6 %collective-permute-done.4 = bf16[1536,128]{1,0:T(8,128)(2,1)S(1)} collective-permute-done((bf16[1536,128]{1,0:T(8,128)(2,1)}, bf16[1536,128]{1,0:T(8,128)(2,1)S(1)}, u32[]{:S(2)}, u32[]{:S(2)}) %collective-permute-start.4) | collective-permute-done | bytes 393248 | tf_op jit(solution)/shard_map/ppermute | solution.py:499
  64.6 1.8 %add_convert_fusion = bf16[1536,128]{1,0:T(8,128)(2,1)} fusion(bf16[1536,128]{1,0:T(8,128)(2,1)} %get-tuple-element.23, bf16[1536,128]{1,0:T(8,128)(2,1)S(1)} %collective-permute-done.4), kind=kLoop, calls=%fused_computation | loop fusion | flops 786432 | bytes 1179648 | tf_op jit(solution)/shard_map/convert_element_type | solution.py:500
  66.4 11.5 %all-to-all-start = ((bf16[64,24,128]{2,1,0:T(8,128)(2,1)}), bf16[64,24,128]{2,1,0:T(8,128)(2,1)S(1)}, u32[]{:S(2)}, u32[]{:S(2)}) async-start(bf16[64,24,128]{2,1,0:T(8,128)(2,1)} %bitcast.19), calls=%async_computation | async-start | bytes 786432 | tf_op jit(solution)/shard_map/all_to_all | solution.py:500
  77.9 11.1 %all-to-all-done.came_ref = bf16[64,24,128]{2,1,0:T(8,128)(2,1)S(1)} async-done(((bf16[64,24,128]{2,1,0:T(8,128)(2,1)}), bf16[64,24,128]{2,1,0:T(8,128)(2,1)S(1)}, u32[]{:S(2)}, u32[]{:S(2)}) %all-to-all-start) | async-done | bytes 393248 | tf_op jit(solution)/shard_map/all_to_all | solution.py:500
  89.8 1.9 %shard_map.122 = bf16[64,24,128]{2,1,0:T(8,128)(2,1)} custom-call(s32[1]{0:T(128)S(6)} %add.22.index_ref, bf16[64,24,128]{2,1,0:T(8,128)(2,1)} %copy-done.2), custom_call_target="tpu_custom_call" | custom-call | tf_op jit(solution)/shard_map/pallas_call | solution.py:502
  91.7 14.9 %all_to_all.10 = bf16[64,24,128]{2,1,0:T(8,128)(2,1)S(1)} all-to-all(bf16[64,24,128]{2,1,0:T(8,128)(2,1)} %shard_map.122), channel_id=1, replica_groups=mesh['y'=4,'core'=2,'row'=4,'col'=4] {'y','row','col'}, dimensions={0} | all-to-all | bytes 786432 | tf_op jit(solution)/shard_map/all_to_all | solution.py:511
  106.6 3.1 %collective-permute-start.5 = (bf16[1536,128]{1,0:T(8,128)(2,1)S(1)}, bf16[1536,128]{1,0:T(8,128)(2,1)S(1)}, u32[]{:S(2)}, u32[]{:S(2)}) collective-permute-start(bf16[1536,128]{1,0:T(8,128)(2,1)S(1)} %bitcast.47), channel_id=1, source_target_pairs={{0,16},{16,0},{1,17},{17,1},{2,18},{18,2},{3,19},{19,3},{4,20},{20... | collective-permute-start | bytes 1179656 | tf_op jit(solution)/shard_map/ppermute | solution.py:512
  109.6 1.3 %collective-permute-done.5.other_ref = bf16[1536,128]{1,0:T(8,128)(2,1)S(1)} collective-permute-done((bf16[1536,128]{1,0:T(8,128)(2,1)S(1)}, bf16[1536,128]{1,0:T(8,128)(2,1)S(1)}, u32[]{:S(2)}, u32[]{:S(2)}) %collective-permute-start.5) | collective-permute-done | bytes 393248 | tf_op jit(solution)/shard_map/ppermute | solution.py:512
  111.7 2.5 %shard_map.123 = (f32[1,1]{1,0:T(1,128)}, f32[64,256]{1,0:T(8,128)}, f32[9,64,64]{2,1,0:T(8,128)}, f32[64,256]{1,0:T(8,128)}, f32[9,135,256]{2,1,0:T(8,128)}) custom-call(s32[1]{0:T(128)} %bitcast.core_ref, bf16[1536,128]{1,0:T(8,128)(2,1)} %bitcast.48, bf16[1536,128]{1,0:T(8,128)(2,1)} %copy-done.7), custom_call_target="tpu_custom_call" | custom-call | tf_op jit(solution)/shard_map/pallas_call | solution.py:513
  (45 shorter events, 6.0 us)
Async XLA Ops:
  4.5 6.8 %copy-start = (bf16[1,256,32,128]{3,1,2,0:T(8,128)(2,1)}, bf16[1,256,32,128]{3,1,2,0:T(8,128)(2,1)S(1)}, u32[]{:S(2)}) copy-start(bf16[1,256,32,128]{3,1,2,0:T(8,128)(2,1)S(1)} %copy.44) | copy-start | bytes 6291460
  4.5 5.9 %copy-start.1 = (bf16[3,3,135,256]{3,2,1,0:T(8,128)(2,1)S(1)}, bf16[3,3,135,256]{3,2,1,0:T(8,128)(2,1)}, u32[]{:S(2)}) copy-start(bf16[3,3,135,256]{3,2,1,0:T(8,128)(2,1)} %param.12) | copy-start | bytes 1866244
  4.6 12.3 %collective-permute-start = (bf16[4,288,128]{2,1,0:T(8,128)(2,1)S(1)}, bf16[4,288,128]{2,1,0:T(8,128)(2,1)S(1)}, u32[]{:S(2)}, u32[]{:S(2)}) collective-permute-start(bf16[4,288,128]{2,1,0:T(8,128)(2,1)S(1)} %maximum_bitcast_fusion), channel_id=1, source_target_pairs={{0,4},{4,8},{8,12},{1,5},{5,9},{9,13},{2,6},{6,10},{10,14},{3,7},{... | collective-permute-start | bytes 884744 | tf_op jit(solution)/shard_map/ppermute | solution.py:427
  9.2 9.8 %collective-permute-start.1 = (bf16[4,288,128]{2,1,0:T(8,128)(2,1)S(1)}, bf16[4,288,128]{2,1,0:T(8,128)(2,1)S(1)}, u32[]{:S(2)}, u32[]{:S(2)}) collective-permute-start(bf16[4,288,128]{2,1,0:T(8,128)(2,1)S(1)} %maximum_bitcast_fusion.1), channel_id=1, source_target_pairs={{4,0},{8,4},{12,8},{5,1},{9,5},{13,9},{6,2},{10,6},{14,10},{7,3},{... | collective-permute-start | bytes 884744 | tf_op jit(solution)/shard_map/ppermute | solution.py:428
  16.9 2.1 %copy-start.4 = (bf16[4,288,128]{2,1,0:T(8,128)(2,1)}, bf16[4,288,128]{2,1,0:T(8,128)(2,1)S(1)}, u32[]{:S(2)}) copy-start(bf16[4,288,128]{2,1,0:T(8,128)(2,1)S(1)} %collective-permute-done.top_ref) | copy-start | bytes 884740
  19.0 0.7 copy-start.5
  21.9 10.1 %collective-permute-start.2 = (bf16[288,256]{1,0:T(8,128)(2,1)}, bf16[288,256]{1,0:T(8,128)(2,1)S(1)}, u32[]{:S(2)}, u32[]{:S(2)}) collective-permute-start(bf16[288,256]{1,0:T(8,128)(2,1)} %get-tuple-element.20), channel_id=1, source_target_pairs={{0,1},{1,2},{2,3},{4,5},{5,6},{6,7},{8,9},{9,10},{10,11},{12,13},{... | collective-permute-start | bytes 442376 | tf_op jit(solution)/shard_map/ppermute | solution.py:441
  25.1 7.0 %collective-permute-start.3 = (bf16[288,256]{1,0:T(8,128)(2,1)}, bf16[288,256]{1,0:T(8,128)(2,1)S(1)}, u32[]{:S(2)}, u32[]{:S(2)}) collective-permute-start(bf16[288,256]{1,0:T(8,128)(2,1)} %get-tuple-element.21), channel_id=1, source_target_pairs={{1,0},{2,1},{3,2},{5,4},{6,5},{7,6},{9,8},{10,9},{11,10},{13,12},{... | collective-permute-start | bytes 442376 | tf_op jit(solution)/shard_map/ppermute | solution.py:442
  27.0 1.4 %copy-start.6 = (bf16[3,3,64,64]{3,2,1,0:T(8,128)(2,1)S(1)}, bf16[3,3,64,64]{3,2,1,0:T(8,128)(2,1)}, u32[]{:S(2)}) copy-start(bf16[3,3,64,64]{3,2,1,0:T(8,128)(2,1)} %param.10) | copy-start | bytes 221188
  27.1 3.2 %copy-start.10 = (bf16[256,64]{0,1:T(8,128)(2,1)S(1)}, bf16[256,64]{0,1:T(8,128)(2,1)}, u32[]{:S(2)}) copy-start(bf16[256,64]{0,1:T(8,128)(2,1)} %param.11) | copy-start | bytes 98308
  32.1 0.7 copy-start.8
  32.1 0.7 copy-start.9
  60.8 3.8 %collective-permute-start.4 = (bf16[1536,128]{1,0:T(8,128)(2,1)}, bf16[1536,128]{1,0:T(8,128)(2,1)S(1)}, u32[]{:S(2)}, u32[]{:S(2)}) collective-permute-start(bf16[1536,128]{1,0:T(8,128)(2,1)} %get-tuple-element.22), channel_id=1, source_target_pairs={{0,16},{16,0},{1,17},{17,1},{2,18},{18,2},{3,19},{19,3},{4,20},{20... | collective-permute-start | bytes 1179656 | tf_op jit(solution)/shard_map/ppermute | solution.py:499
  66.4 22.6 %all-to-all-start = ((bf16[64,24,128]{2,1,0:T(8,128)(2,1)}), bf16[64,24,128]{2,1,0:T(8,128)(2,1)S(1)}, u32[]{:S(2)}, u32[]{:S(2)}) async-start(bf16[64,24,128]{2,1,0:T(8,128)(2,1)} %bitcast.19), calls=%async_computation | async-start | bytes 786432 | tf_op jit(solution)/shard_map/all_to_all | solution.py:500
  89.0 0.7 copy-start.2
  106.6 4.4 %copy-start.3 = (bf16[64,24,128]{2,1,0:T(8,128)(2,1)}, bf16[64,24,128]{2,1,0:T(8,128)(2,1)S(1)}, u32[]{:S(2)}) copy-start(bf16[64,24,128]{2,1,0:T(8,128)(2,1)S(1)} %all_to_all.10) | copy-start | bytes 1179652
  106.6 4.4 %collective-permute-start.5 = (bf16[1536,128]{1,0:T(8,128)(2,1)S(1)}, bf16[1536,128]{1,0:T(8,128)(2,1)S(1)}, u32[]{:S(2)}, u32[]{:S(2)}) collective-permute-start(bf16[1536,128]{1,0:T(8,128)(2,1)S(1)} %bitcast.47), channel_id=1, source_target_pairs={{0,16},{16,0},{1,17},{17,1},{2,18},{18,2},{3,19},{19,3},{4,20},{20... | collective-permute-start | bytes 1179656 | tf_op jit(solution)/shard_map/ppermute | solution.py:512
  111.0 0.7 copy-start.7

commit v6 on v5

--- a/solution.py
+++ b/solution.py
@@ -23,14 +23,14 @@
 RIGHT = MARGIN + 5120
 PIPE = 640
 SPLIT = (
-    (0, 2816, 2),
-    (0, 2816, 2),
-    (128, 2688, 2),
+    (0, 5632, 1),
+    (0, 5632, 1),
+    (128, 5376, 1),
     (0, PIPE, 9),
     (256, PIPE, 8),
     (384, 2432, 2),
-    (384, 2432, 2),
-    (512, 2304, 2),
+    (384, 4864, 1),
+    (512, 4608, 1),
 )
 LABEL0 = C
 MASK0 = C + A

time: 115 us -> 113 us (0.983)
  Pallas kernels: 40.2 us -> 38.4 us
    pallas_call x1, Pallas kernels: 28 us -> 26.2 us  [per_device(): pl.pallas_call(main_kernel, out_shape=(shape((HALF, 128), BF), shape((HAL...]
where the time goes in v6:
time: 113 us; the launch traced here: 112 us
  Pallas kernels  38.4 us (34%)
  starting transfers between devices  27 us (24%)
  waiting for transfers between devices  16.1 us (14%)
  blocking collectives  14.9 us (13%)
  local copies, waits for them, and re-layouts  11.2 us (10%)
  other arithmetic  4.02 us (4%)
    pallas_call x1, Pallas kernels, per_device(): pl.pallas_call(main_kernel, out_shape=(shape((HALF, 128), BF), shape((HAL...  26.2 us
    all_to_all x1, blocking collectives, per_device(): lax.all_to_all(copies, CHIPS, 0, 0, tiled=True).reshape(PAIRS * SHARE, 128)  14.9 us
    all_to_all x1, starting transfers between devices, per_device(): lax.all_to_all(pair.astype(BF).reshape(PAIRS, SHARE, 128), CHIPS, 0, 0, t...  11.5 us
    all_to_all x1, waiting for transfers between devices, per_device(): lax.all_to_all(pair.astype(BF).reshape(PAIRS, SHARE, 128), CHIPS, 0, 0, t...  11.1 us
    unnamed x25, local copies, waits for them, and re-layouts  7.05 us
    pallas_call x1, Pallas kernels, per_device(): pl.pallas_call(edges_kernel, out_shape=(pack, pack, start), compiler_para...  5.58 us
    ppermute x1, starting transfers between devices, per_device(): top = lax.ppermute(edge_rows(ROWS - HALO), 'row', ahead)  4.52 us
    ppermute x1, starting transfers between devices, per_device(): left = lax.ppermute(right_edge, 'col', ahead)  3.11 us
  transfers between devices with their start and end apart: 7, of which 4 were waited for; matrix products, arithmetic and copies ran while one was open for 6% of the time, Pallas kernels for 5%

profile of v6, /device:TPU:1, one launch (start us, length us, event | category | flops | bytes accessed | tf_op | source)
XLA Modules:
  0.0 112.4 jit_solution(10449820653043586966)
XLA Ops:
  0.8 1.2 %fusion = (bf16[9,32,128]{2,0,1:T(8,128)(2,1)S(1)}, bf16[9,32,128]{2,0,1:T(8,128)(2,1)S(1)}) fusion(s32[1,9,32,128]{3,2,1,0:T(8,128)} %param.13, s32[1,9,32,128]{3,2,1,0:T(8,128)} %param.14), kind=kLoop, calls=%fused_computation.9 | loop fusion | flops 73728 | bytes 442368 | tf_op jit(solution)/shard_map/convert_element_type | solution.py:418
  2.1 2.4 %copy.44 = bf16[1,256,32,128]{3,1,2,0:T(8,128)(2,1)S(1)} copy(bf16[1,256,32,128]{3,2,1,0:T(8,128)(2,1)} %param.8) | data formatting | bytes 4194304 | tf_op args[0]
  4.6 4.5 %collective-permute-start = (bf16[4,288,128]{2,1,0:T(8,128)(2,1)S(1)}, bf16[4,288,128]{2,1,0:T(8,128)(2,1)S(1)}, u32[]{:S(2)}, u32[]{:S(2)}) collective-permute-start(bf16[4,288,128]{2,1,0:T(8,128)(2,1)S(1)} %maximum_bitcast_fusion), channel_id=1, source_target_pairs={{0,4},{4,8},{8,12},{1,5},{5,9},{9,13},{2,6},{6,10},{10,14},{3,7},{... | collective-permute-start | bytes 884744 | tf_op jit(solution)/shard_map/ppermute | solution.py:427
  9.2 1.3 %collective-permute-start.1 = (bf16[4,288,128]{2,1,0:T(8,128)(2,1)S(1)}, bf16[4,288,128]{2,1,0:T(8,128)(2,1)S(1)}, u32[]{:S(2)}, u32[]{:S(2)}) collective-permute-start(bf16[4,288,128]{2,1,0:T(8,128)(2,1)S(1)} %maximum_bitcast_fusion.1), channel_id=1, source_target_pairs={{4,0},{8,4},{12,8},{5,1},{9,5},{13,9},{6,2},{10,6},{14,10},{7,3},{... | collective-permute-start | bytes 884744 | tf_op jit(solution)/shard_map/ppermute | solution.py:428
  10.5 0.8 fusion.4.tags_ref
  11.3 5.6 %shard_map.119 = (bf16[288,128]{1,0:T(8,128)(2,1)}, bf16[288,128]{1,0:T(8,128)(2,1)}, bf16[288,6656]{1,0:T(8,128)(2,1)}) custom-call(bf16[32,256,128]{2,1,0:T(8,128)(2,1)} %bitcast.40, bf16[32,32,128]{2,1,0:T(8,128)(2,1)} %fusion.4.tags_ref), custom_call_target="tpu_custom_call" | custom-call | tf_op jit(solution)/shard_map/pallas_call | solution.py:434
  16.9 2.1 %collective-permute-done.1.bottom_ref = bf16[4,288,128]{2,1,0:T(8,128)(2,1)S(1)} collective-permute-done((bf16[4,288,128]{2,1,0:T(8,128)(2,1)S(1)}, bf16[4,288,128]{2,1,0:T(8,128)(2,1)S(1)}, u32[]{:S(2)}, u32[]{:S(2)}) %collective-permute-start.1) | collective-permute-done | bytes 294944 | tf_op jit(solution)/shard_map/ppermute | solution.py:428
  19.7 2.2 %shard_map.120 = (bf16[288,256]{1,0:T(8,128)(2,1)}, bf16[288,256]{1,0:T(8,128)(2,1)}) custom-call(bf16[288,128]{1,0:T(8,128)(2,1)} %get-tuple-element.18.left_ref, bf16[288,128]{1,0:T(8,128)(2,1)} %get-tuple-element.19.right_ref, bf16[4,288,128]{2,1,0:T(8,128)(2,1)} %copy-done.4, bf16[4,288,128]{2,1,0:T(8,128)(2,1)} %copy-done.5), custom_call_target="tpu_custom_call" | custom-call | tf_op jit(solution)/shard_map/pallas_call | solution.py:438
  21.9 3.1 %collective-permute-start.2 = (bf16[288,256]{1,0:T(8,128)(2,1)}, bf16[288,256]{1,0:T(8,128)(2,1)S(1)}, u32[]{:S(2)}, u32[]{:S(2)}) collective-permute-start(bf16[288,256]{1,0:T(8,128)(2,1)} %get-tuple-element.20), channel_id=1, source_target_pairs={{0,1},{1,2},{2,3},{4,5},{5,6},{6,7},{8,9},{9,10},{10,11},{12,13},{... | collective-permute-start | bytes 442376 | tf_op jit(solution)/shard_map/ppermute | solution.py:441
  25.1 1.3 %collective-permute-start.3 = (bf16[288,256]{1,0:T(8,128)(2,1)}, bf16[288,256]{1,0:T(8,128)(2,1)S(1)}, u32[]{:S(2)}, u32[]{:S(2)}) collective-permute-start(bf16[288,256]{1,0:T(8,128)(2,1)} %get-tuple-element.21), channel_id=1, source_target_pairs={{1,0},{2,1},{3,2},{5,4},{6,5},{7,6},{9,8},{10,9},{11,10},{13,12},{... | collective-permute-start | bytes 442376 | tf_op jit(solution)/shard_map/ppermute | solution.py:442
  27.3 1.0 copy.35
  29.3 0.8 reshape.50.w2t_ref
  30.9 1.2 %concatenate.15 = bf16[1232,256]{0,1:T(8,128)(2,1)} concatenate(bf16[1152,256]{0,1:T(8,128)(2,1)S(1)} %copy.32, bf16[72,256]{0,1:T(8,128)(2,1)S(1)} %copy.33, bf16[8,256]{0,1:T(8,128)(2,1)S(1)} %broadcast_in_dim.11), dimensions={0} | concatenate | bytes 1261568 | tf_op jit(solution)/shard_map/concatenate | solution.py:449
  32.8 26.2 %shard_map.121 = (bf16[1536,128]{1,0:T(8,128)(2,1)}, bf16[1536,128]{1,0:T(8,128)(2,1)}) custom-call(s32[1]{0:T(128)} %bitcast.core_ref, bf16[288,6656]{1,0:T(8,128)(2,1)} %get-tuple-element.17.x0_ref, bf16[4,288,128]{2,1,0:T(8,128)(2,1)} %copy-done.4, bf16[4,288,128]{2,1,0:T(8,128)(2,1)} %copy-done.5, bf16[288,256]{1,0:T(8,128)(2,1)} %copy-done.8, ...), custom_call_target="tpu_custom_call" | custom-call | tf_op jit(solution)/shard_map/pallas_call | solution.py:465
  59.0 2.2 %collective-permute-start.4 = (bf16[1536,128]{1,0:T(8,128)(2,1)}, bf16[1536,128]{1,0:T(8,128)(2,1)S(1)}, u32[]{:S(2)}, u32[]{:S(2)}) collective-permute-start(bf16[1536,128]{1,0:T(8,128)(2,1)} %get-tuple-element.22), channel_id=1, source_target_pairs={{0,16},{16,0},{1,17},{17,1},{2,18},{18,2},{3,19},{19,3},{4,20},{20... | collective-permute-start | bytes 1179656 | tf_op jit(solution)/shard_map/ppermute | solution.py:499
  61.2 1.6 %collective-permute-done.4 = bf16[1536,128]{1,0:T(8,128)(2,1)S(1)} collective-permute-done((bf16[1536,128]{1,0:T(8,128)(2,1)}, bf16[1536,128]{1,0:T(8,128)(2,1)S(1)}, u32[]{:S(2)}, u32[]{:S(2)}) %collective-permute-start.4) | collective-permute-done | bytes 393248 | tf_op jit(solution)/shard_map/ppermute | solution.py:499
  62.7 1.8 %add_convert_fusion = bf16[1536,128]{1,0:T(8,128)(2,1)} fusion(bf16[1536,128]{1,0:T(8,128)(2,1)} %get-tuple-element.23, bf16[1536,128]{1,0:T(8,128)(2,1)S(1)} %collective-permute-done.4), kind=kLoop, calls=%fused_computation | loop fusion | flops 786432 | bytes 1179648 | tf_op jit(solution)/shard_map/convert_element_type | solution.py:500
  64.6 11.5 %all-to-all-start = ((bf16[64,24,128]{2,1,0:T(8,128)(2,1)}), bf16[64,24,128]{2,1,0:T(8,128)(2,1)S(1)}, u32[]{:S(2)}, u32[]{:S(2)}) async-start(bf16[64,24,128]{2,1,0:T(8,128)(2,1)} %bitcast.19), calls=%async_computation | async-start | bytes 786432 | tf_op jit(solution)/shard_map/all_to_all | solution.py:500
  76.1 11.1 %all-to-all-done.came_ref = bf16[64,24,128]{2,1,0:T(8,128)(2,1)S(1)} async-done(((bf16[64,24,128]{2,1,0:T(8,128)(2,1)}), bf16[64,24,128]{2,1,0:T(8,128)(2,1)S(1)}, u32[]{:S(2)}, u32[]{:S(2)}) %all-to-all-start) | async-done | bytes 393248 | tf_op jit(solution)/shard_map/all_to_all | solution.py:500
  87.9 1.9 %shard_map.122 = bf16[64,24,128]{2,1,0:T(8,128)(2,1)} custom-call(s32[1]{0:T(128)S(6)} %add.22.index_ref, bf16[64,24,128]{2,1,0:T(8,128)(2,1)} %copy-done.2), custom_call_target="tpu_custom_call" | custom-call | tf_op jit(solution)/shard_map/pallas_call | solution.py:502
  89.8 14.9 %all_to_all.10 = bf16[64,24,128]{2,1,0:T(8,128)(2,1)S(1)} all-to-all(bf16[64,24,128]{2,1,0:T(8,128)(2,1)} %shard_map.122), channel_id=1, replica_groups=mesh['y'=4,'core'=2,'row'=4,'col'=4] {'y','row','col'}, dimensions={0} | all-to-all | bytes 786432 | tf_op jit(solution)/shard_map/all_to_all | solution.py:511
  104.7 3.1 %collective-permute-start.5 = (bf16[1536,128]{1,0:T(8,128)(2,1)S(1)}, bf16[1536,128]{1,0:T(8,128)(2,1)S(1)}, u32[]{:S(2)}, u32[]{:S(2)}) collective-permute-start(bf16[1536,128]{1,0:T(8,128)(2,1)S(1)} %bitcast.47), channel_id=1, source_target_pairs={{0,16},{16,0},{1,17},{17,1},{2,18},{18,2},{3,19},{19,3},{4,20},{20... | collective-permute-start | bytes 1179656 | tf_op jit(solution)/shard_map/ppermute | solution.py:512
  107.8 1.3 %collective-permute-done.5.other_ref = bf16[1536,128]{1,0:T(8,128)(2,1)S(1)} collective-permute-done((bf16[1536,128]{1,0:T(8,128)(2,1)S(1)}, bf16[1536,128]{1,0:T(8,128)(2,1)S(1)}, u32[]{:S(2)}, u32[]{:S(2)}) %collective-permute-start.5) | collective-permute-done | bytes 393248 | tf_op jit(solution)/shard_map/ppermute | solution.py:512
  109.9 2.5 %shard_map.123 = (f32[1,1]{1,0:T(1,128)}, f32[64,256]{1,0:T(8,128)}, f32[9,64,64]{2,1,0:T(8,128)}, f32[64,256]{1,0:T(8,128)}, f32[9,135,256]{2,1,0:T(8,128)}) custom-call(s32[1]{0:T(128)} %bitcast.core_ref, bf16[1536,128]{1,0:T(8,128)(2,1)} %bitcast.48, bf16[1536,128]{1,0:T(8,128)(2,1)} %copy-done.7), custom_call_target="tpu_custom_call" | custom-call | tf_op jit(solution)/shard_map/pallas_call | solution.py:513
  (45 shorter events, 6.0 us)
Async XLA Ops:
  4.5 6.8 %copy-start = (bf16[1,256,32,128]{3,1,2,0:T(8,128)(2,1)}, bf16[1,256,32,128]{3,1,2,0:T(8,128)(2,1)S(1)}, u32[]{:S(2)}) copy-start(bf16[1,256,32,128]{3,1,2,0:T(8,128)(2,1)S(1)} %copy.44) | copy-start | bytes 6291460
  4.5 5.9 %copy-start.1 = (bf16[3,3,135,256]{3,2,1,0:T(8,128)(2,1)S(1)}, bf16[3,3,135,256]{3,2,1,0:T(8,128)(2,1)}, u32[]{:S(2)}) copy-start(bf16[3,3,135,256]{3,2,1,0:T(8,128)(2,1)} %param.12) | copy-start | bytes 1866244
  4.6 12.3 %collective-permute-start = (bf16[4,288,128]{2,1,0:T(8,128)(2,1)S(1)}, bf16[4,288,128]{2,1,0:T(8,128)(2,1)S(1)}, u32[]{:S(2)}, u32[]{:S(2)}) collective-permute-start(bf16[4,288,128]{2,1,0:T(8,128)(2,1)S(1)} %maximum_bitcast_fusion), channel_id=1, source_target_pairs={{0,4},{4,8},{8,12},{1,5},{5,9},{9,13},{2,6},{6,10},{10,14},{3,7},{... | collective-permute-start | bytes 884744 | tf_op jit(solution)/shard_map/ppermute | solution.py:427
  9.2 9.8 %collective-permute-start.1 = (bf16[4,288,128]{2,1,0:T(8,128)(2,1)S(1)}, bf16[4,288,128]{2,1,0:T(8,128)(2,1)S(1)}, u32[]{:S(2)}, u32[]{:S(2)}) collective-permute-start(bf16[4,288,128]{2,1,0:T(8,128)(2,1)S(1)} %maximum_bitcast_fusion.1), channel_id=1, source_target_pairs={{4,0},{8,4},{12,8},{5,1},{9,5},{13,9},{6,2},{10,6},{14,10},{7,3},{... | collective-permute-start | bytes 884744 | tf_op jit(solution)/shard_map/ppermute | solution.py:428
  16.9 2.1 %copy-start.4 = (bf16[4,288,128]{2,1,0:T(8,128)(2,1)}, bf16[4,288,128]{2,1,0:T(8,128)(2,1)S(1)}, u32[]{:S(2)}) copy-start(bf16[4,288,128]{2,1,0:T(8,128)(2,1)S(1)} %collective-permute-done.top_ref) | copy-start | bytes 884740
  19.0 0.7 copy-start.5
  21.9 10.1 %collective-permute-start.2 = (bf16[288,256]{1,0:T(8,128)(2,1)}, bf16[288,256]{1,0:T(8,128)(2,1)S(1)}, u32[]{:S(2)}, u32[]{:S(2)}) collective-permute-start(bf16[288,256]{1,0:T(8,128)(2,1)} %get-tuple-element.20), channel_id=1, source_target_pairs={{0,1},{1,2},{2,3},{4,5},{5,6},{6,7},{8,9},{9,10},{10,11},{12,13},{... | collective-permute-start | bytes 442376 | tf_op jit(solution)/shard_map/ppermute | solution.py:441
  25.1 7.0 %collective-permute-start.3 = (bf16[288,256]{1,0:T(8,128)(2,1)}, bf16[288,256]{1,0:T(8,128)(2,1)S(1)}, u32[]{:S(2)}, u32[]{:S(2)}) collective-permute-start(bf16[288,256]{1,0:T(8,128)(2,1)} %get-tuple-element.21), channel_id=1, source_target_pairs={{1,0},{2,1},{3,2},{5,4},{6,5},{7,6},{9,8},{10,9},{11,10},{13,12},{... | collective-permute-start | bytes 442376 | tf_op jit(solution)/shard_map/ppermute | solution.py:442
  26.9 1.4 %copy-start.6 = (bf16[3,3,64,64]{3,2,1,0:T(8,128)(2,1)S(1)}, bf16[3,3,64,64]{3,2,1,0:T(8,128)(2,1)}, u32[]{:S(2)}) copy-start(bf16[3,3,64,64]{3,2,1,0:T(8,128)(2,1)} %param.10) | copy-start | bytes 221188
  26.9 3.2 %copy-start.10 = (bf16[256,64]{0,1:T(8,128)(2,1)S(1)}, bf16[256,64]{0,1:T(8,128)(2,1)}, u32[]{:S(2)}) copy-start(bf16[256,64]{0,1:T(8,128)(2,1)} %param.11) | copy-start | bytes 98308
  32.1 0.7 copy-start.8
  32.1 0.7 copy-start.9
  59.0 3.8 %collective-permute-start.4 = (bf16[1536,128]{1,0:T(8,128)(2,1)}, bf16[1536,128]{1,0:T(8,128)(2,1)S(1)}, u32[]{:S(2)}, u32[]{:S(2)}) collective-permute-start(bf16[1536,128]{1,0:T(8,128)(2,1)} %get-tuple-element.22), channel_id=1, source_target_pairs={{0,16},{16,0},{1,17},{17,1},{2,18},{18,2},{3,19},{19,3},{4,20},{20... | collective-permute-start | bytes 1179656 | tf_op jit(solution)/shard_map/ppermute | solution.py:499
  64.6 22.6 %all-to-all-start = ((bf16[64,24,128]{2,1,0:T(8,128)(2,1)}), bf16[64,24,128]{2,1,0:T(8,128)(2,1)S(1)}, u32[]{:S(2)}, u32[]{:S(2)}) async-start(bf16[64,24,128]{2,1,0:T(8,128)(2,1)} %bitcast.19), calls=%async_computation | async-start | bytes 786432 | tf_op jit(solution)/shard_map/all_to_all | solution.py:500
  87.2 0.7 copy-start.2
  104.7 4.4 %copy-start.3 = (bf16[64,24,128]{2,1,0:T(8,128)(2,1)}, bf16[64,24,128]{2,1,0:T(8,128)(2,1)S(1)}, u32[]{:S(2)}) copy-start(bf16[64,24,128]{2,1,0:T(8,128)(2,1)S(1)} %all_to_all.10) | copy-start | bytes 1179652
  104.7 4.4 %collective-permute-start.5 = (bf16[1536,128]{1,0:T(8,128)(2,1)S(1)}, bf16[1536,128]{1,0:T(8,128)(2,1)S(1)}, u32[]{:S(2)}, u32[]{:S(2)}) collective-permute-start(bf16[1536,128]{1,0:T(8,128)(2,1)S(1)} %bitcast.47), channel_id=1, source_target_pairs={{0,16},{16,0},{1,17},{17,1},{2,18},{18,2},{3,19},{19,3},{4,20},{20... | collective-permute-start | bytes 1179656 | tf_op jit(solution)/shard_map/ppermute | solution.py:512
  109.2 0.7 copy-start.7
